TPU v7x, 512 devices: a whole 4x4x16 slice. The times are simulated.
512 devices in a mesh: grp: 8 (over y, z_hi), blk: 64 (over x, z_lo, core).
Axes of the slice: x: 4, y: 4, z: 16 (z_hi: 2, z_lo: 8; z = z_hi * 8 + z_lo), core: 2. Of those that a mesh axis runs over, the one named last changes fastest.
Arguments:
- images: bfloat16 [16384, 1152], P(('blk', 'grp')), may hold values from -6 to 6
- texts: bfloat16 [16384, 1152], P(('blk', 'grp')), may hold values from -6 to 6
- tile_mask: int32 [128, 128], replicated, may hold values from 0 to 1, as said below
Outputs:
- image_grads: float32 [16384, 1152], P(('blk', 'grp'))
- text_grads: float32 [16384, 1152], P(('blk', 'grp'))
- loss_mean: float32 [], replicated
Inputs may be any that keep to these rules, and one draw needn't show every extreme that they name: tile_mask is symmetric and 1 on its diagonal.
All inputs are finite; a program needn't handle non-finite values.
Results may differ from a plain program's by a relative error of at most 0.00045.
The roundings to bfloat16 on the way count: a program that leaves them out, or rounds other values in their place, can miss the bound.
Values may be sent and summed in bfloat16 or wider, within the bound.
No kernel may reach another device: no remote copies, remote signals or barrier semaphores. Data moves between devices by JAX's collectives and lax.ppermute only.
A program may use at most 64 MiB of HBM per device.

v0:
```python
import jax
import jax.numpy as jnp
from jax import lax
from jax.experimental import pallas as pl
from jax.experimental.pallas import tpu as pltpu
from jax.sharding import Mesh
from jax.sharding import PartitionSpec as P


TILE = 128
TEMP = 10.0
BIAS = -2.0
EPS = 1e-06
ROWS_AXES = ("x", "zb", "za", "c", "y", "zh")
ZB = ("zh", "zb")
SIDE = 4
DIGITS = 7
BASE = 512.0
TOP = 2.0**32
SPARE = 128
CHUNK = 256

VMEM = pl.BlockSpec(memory_space=pltpu.VMEM)


def inverse_norm(values):
    return lax.rsqrt(jnp.sum(values * values, axis=-1, keepdims=True) + EPS)


def slots_kernel(values_ref, slots_ref):
    values = values_ref[...].astype(jnp.float32)
    unit = (values * inverse_norm(values)).astype(jnp.bfloat16)
    for k in range(SIDE):
        slots_ref[k] = unit


def normalized_slots(values):
    return pl.pallas_call(
        slots_kernel,
        out_shape=pltpu.VMEM((SIDE, *values.shape), jnp.bfloat16),
        in_specs=[VMEM],
        out_specs=VMEM,
        compiler_params=pltpu.CompilerParams(vmem_limit_bytes=4 * 2**20),
    )(values)


def pair_kernel(codes_ref, *refs):
    part_refs, (own_ref, other_ref) = refs[:SIDE], refs[SIDE : SIDE + 2]
    coef_ref, own_sums_ref, other_sums_ref, loss_ref, group_ref = refs[SIDE + 2 :]
    near = part_refs[0].shape[0]
    for k in range(SIDE):
        group_ref[k * near : (k + 1) * near] = part_refs[k][...]
    group = group_ref[...]
    width = group.shape[1]
    half = own_ref.shape[0]
    loss = jnp.zeros((8, group.shape[0]), jnp.float32)
    for texts_ref, sums_ref, base in ((other_ref, other_sums_ref, half), (own_ref, own_sums_ref, 0)):
        for at in range(0, half, CHUNK):
            logits = TEMP * lax.dot_general(
                texts_ref[at : at + CHUNK],
                group,
                (((1,), (1,)), ((), ())),
                preferred_element_type=jnp.float32,
            )
            logits = logits + BIAS
            codes = codes_ref[base + at : base + at + CHUNK].astype(jnp.float32)
            small = jnp.exp(-jnp.abs(logits))
            soft = jnp.maximum(logits, 0.0) + jnp.log1p(small)
            sigmoid = jnp.where(logits >= 0.0, 1.0, small) / (1.0 + small)
            matched = codes > 1.5
            terms = jnp.where(codes > 0.5, soft - jnp.where(matched, logits, 0.0), 0.0)
            loss = loss + jnp.sum(terms.reshape(CHUNK // 8, 8, terms.shape[1]), axis=0)
            coef = jnp.where(codes > 0.5, sigmoid - jnp.where(matched, 1.0, 0.0), 0.0)
            coef = coef.astype(jnp.bfloat16)
            coef_ref[base + at : base + at + CHUNK] = coef
            sums_ref[at : at + CHUNK, :width] = jnp.dot(
                coef, group, preferred_element_type=jnp.float32
            )
    own_sums_ref[:, width:] = jnp.zeros((half, own_sums_ref.shape[1] - width), jnp.float32)
    loss_ref[...] = loss


def placed(value):
    return pltpu.with_memory_space_constraint(value, pltpu.VMEM)


def pair_terms(codes, parts, own_texts, other_texts):
    near, width = parts[0].shape
    half = own_texts.shape[0]
    images = SIDE * near
    return pl.pallas_call(
        pair_kernel,
        out_shape=(
            pltpu.VMEM((2 * half, images), jnp.bfloat16),
            pltpu.VMEM((half, width + SPARE), jnp.float32),
            pltpu.VMEM((half, width), jnp.float32),
            pltpu.VMEM((8, images), jnp.float32),
        ),
        in_specs=[VMEM] * (SIDE + 3),
        out_specs=(VMEM,) * 4,
        scratch_shapes=[pltpu.VMEM((images, width), jnp.bfloat16)],
        compiler_params=pltpu.CompilerParams(vmem_limit_bytes=20 * 2**20),
    )(*(placed(a) for a in (codes, *parts, own_texts, other_texts)))


def swapped(value):
    return lax.ppermute(value, "c", [(0, 1), (1, 0)])


def turned(value, axis, steps):
    return lax.ppermute(value, axis, [(k, (k + steps) % SIDE) for k in range(SIDE)])


def all_turned(block, axis):
    return [block] + [turned(block, axis, k) for k in range(1, SIDE)]


def turned_and_summed(parts, axis):
    sums = parts[0]
    got = [turned(parts[k].astype(jnp.float16), axis, -k) for k in range(1, SIDE)]
    for part in got:
        sums = sums + part.astype(jnp.float32)
    return sums


def over_image_group(total):
    axes = ("x", "za", "c")
    count = lax.axis_size(axes)
    sent = jnp.broadcast_to(total, (count, 8, 128))
    return jnp.sum(lax.all_to_all(sent, axes, 0, 0, tiled=True)[:, 0, 0])


def to_row(total, lanes, first):
    row = jnp.zeros(lanes.shape, jnp.float32)
    rest = total * (1.0 / TOP)
    for k in range(DIGITS):
        rest = rest * BASE
        digit = jnp.floor(rest)
        rest = rest - digit
        row = jnp.where(lanes == first + k, digit, row)
    return row


def from_row(row):
    worth = jnp.zeros(row.shape, jnp.float32)
    lanes = jnp.arange(row.shape[0], dtype=jnp.int32)
    for k in range(DIGITS):
        worth = jnp.where(lanes == k, TOP / BASE ** (k + 1), worth)
    return jnp.sum(row * worth)


def sent_and_summed(parts, axis):
    got = lax.all_to_all(parts, axis, 0, 0, tiled=True)
    return jnp.sum(got.astype(jnp.float32), axis=0)


def block_mask(tile_mask):
    x, zb, za, c, y = (lax.axis_index(n) for n in ("x", "zb", "za", "c", "y"))
    tiles = tile_mask.shape[0]

    def tile_of(xs, zbs, zas, cs, ys):
        return (((xs * 2 + zbs) * 4 + zas) * 2 + cs) * 2 + ys // 2

    k = jnp.arange(16, dtype=jnp.int32)
    image_tiles = tile_of((x - k // 4) % 4, zb, (za - k % 4) % 4, c, y)
    k = jnp.arange(32, dtype=jnp.int32)
    text_cores = jnp.where(k < 16, c, 1 - c)
    text_tiles = tile_of(x, k % 2, za, text_cores, (k // 4) % 4)
    every = jnp.arange(tiles, dtype=jnp.int32)
    left = (text_tiles[:, None] == every[None]).astype(jnp.float32)
    right = (image_tiles[:, None] == every[None]).astype(jnp.float32)
    chosen = lax.dot_general(right, tile_mask.astype(jnp.float32), (((1,), (0,)), ((), ())))
    return lax.dot_general(left, chosen, (((1,), (1,)), ((), ())))


def pair_codes(tile_mask, rows):
    own_text = lax.axis_index("y") * 4 + lax.axis_index(ZB)
    masked = block_mask(tile_mask)
    i = jnp.arange(16 * rows, dtype=jnp.int32)
    j = jnp.arange(32 * rows, dtype=jnp.int32)
    left = (j[:, None] // rows == jnp.arange(32)[None]).astype(jnp.float32)
    right = (jnp.arange(16)[:, None] == i[None] // rows).astype(jnp.float32)
    masked = jnp.dot(jnp.dot(left, masked), right)
    matched = i[None] == (j - own_text * rows)[:, None]
    matched = matched & (i < rows)[None]
    return jnp.where(matched, 2.0, jnp.where(masked < 0.5, 1.0, 0.0)).astype(jnp.bfloat16)


def back(values, inverse, grads):
    unit = values * inverse
    return inverse * (grads - unit * jnp.sum(unit * grads, axis=-1, keepdims=True))


def step(images, texts, tile_mask):
    rows, width = images.shape
    got = lax.all_to_all(normalized_slots(texts), ZB, 0, 0, tiled=True)
    images = images.astype(jnp.float32)
    texts = texts.astype(jnp.float32)
    image_inverse = inverse_norm(images)
    text_inverse = inverse_norm(texts)
    image_bf = (images * image_inverse).astype(jnp.bfloat16)
    near = all_turned(image_bf, "za")
    near = jnp.concatenate(near, axis=0)
    parts = all_turned(near, "x")
    sent = jnp.broadcast_to(got.reshape(1, SIDE * rows, width), (SIDE, SIDE * rows, width))
    own_texts = lax.all_to_all(sent, "y", 0, 0, tiled=True).reshape(16 * rows, width)
    other_texts = swapped(own_texts)
    codes = pair_codes(tile_mask, rows)

    coef, own_sums, other_sums, loss = pair_terms(codes, parts, own_texts, other_texts)
    other_sums = swapped(other_sums)
    loss = over_image_group(jnp.sum(loss))
    image_parts = lax.dot_general(
        coef[: 16 * rows], own_texts, (((0,), (0,)), ((), ())), preferred_element_type=jnp.float32
    ) + lax.dot_general(
        coef[16 * rows :], other_texts, (((0,), (0,)), ((), ())), preferred_element_type=jnp.float32
    )

    lanes = lax.broadcasted_iota(jnp.int32, (1, width + SPARE), 1)
    row = to_row(loss, lanes, width)
    text_parts = own_sums + jnp.pad(other_sums, ((0, 0), (0, SPARE)))
    text_parts = jnp.where(lanes >= width, row, text_parts).astype(jnp.float16)
    text_parts = sent_and_summed(text_parts.reshape(SIDE, SIDE * rows, -1), "y")
    image_parts = turned_and_summed(image_parts.reshape(SIDE, SIDE * rows, width), "x")
    text_parts = text_parts.astype(jnp.float16).reshape(SIDE, rows, -1)
    text_sums = sent_and_summed(text_parts, ZB)
    image_sums = turned_and_summed(image_parts.reshape(SIDE, rows, width), "za")
    loss = from_row(text_sums[0, width:])

    zero = tile_mask == 0
    size = tile_mask.shape[0]
    diagonal = jnp.eye(size, dtype=jnp.bool_)
    pairs = jnp.sum(jnp.where(zero, TILE * TILE, jnp.where(diagonal, TILE, 0)))
    return (
        back(images, image_inverse, TEMP * image_sums),
        back(texts, text_inverse, TEMP * text_sums[:, :width]),
        loss / pairs.astype(jnp.float32),
    )


def solution(mesh):
    finer = Mesh(mesh.devices.reshape(4, 2, 4, 2, 4, 2), ("y", "zh", "x", "zb", "za", "c"))
    placed = P(ROWS_AXES, None)
    return jax.shard_map(
        step,
        mesh=finer,
        in_specs=(placed, placed, P()),
        out_specs=(placed, placed, P()),
        check_vma=False,
    )
```

profile of v0, /device:TPU:8, one launch (start us, length us, event | category | flops | bytes accessed | tf_op | source)
XLA Modules:
  0.0 174.5 jit_solution(10984679670989096341)
XLA Ops:
  1.6 34.4 %all_to_all.25 = bf16[4,32,1152]{2,1,0:T(8,128)(2,1)S(1)} all-to-all(bf16[4,32,1152]{2,1,0:T(8,128)(2,1)S(1)} %shard_map.58), channel_id=1, replica_groups=mesh['y'=4,'zh'=2,'x'=4,'zb'=2,'za'=4,'c'=2] {'zh','zb'}, dimensions={0} | all-to-all | bytes 589824 | tf_op jit(solution)/shard_map/all_to_all | solution.py:196
  37.1 4.9 %all-to-all-start.1 = ((bf16[4,128,1152]{2,1,0:T(8,128)(2,1)}), bf16[4,128,1152]{2,1,0:T(8,128)(2,1)S(1)}, u32[]{:S(2)}, u32[]{:S(2)}) async-start(bf16[4,128,1152]{2,1,0:T(8,128)(2,1)} %broadcast_in_dim.127), calls=%async_computation.1 | async-start | bytes 2359296 | tf_op jit(solution)/shard_map/all_to_all | solution.py:206
  42.2 3.8 %collective-permute-start.2 = (bf16[32,1152]{1,0:T(8,128)(2,1)S(1)}, bf16[32,1152]{1,0:T(8,128)(2,1)S(1)}, u32[]{:S(2)}, u32[]{:S(2)}) collective-permute-start(bf16[32,1152]{1,0:T(8,128)(2,1)S(1)} %fusion.15), channel_id=1, source_target_pairs={{0,6},{2,0},{4,2},{6,4},{1,7},{3,1},{5,3},{7,5},{8,14},{10,8},{12,... | collective-permute-start | bytes 221192 | tf_op jit(solution)/shard_map/ppermute | solution.py:111
  46.1 6.2 %collective-permute-start.1 = (bf16[32,1152]{1,0:T(8,128)(2,1)S(1)}, bf16[32,1152]{1,0:T(8,128)(2,1)S(1)}, u32[]{:S(2)}, u32[]{:S(2)}) collective-permute-start(bf16[32,1152]{1,0:T(8,128)(2,1)S(1)} %fusion.15), channel_id=1, source_target_pairs={{0,4},{2,6},{4,0},{6,2},{1,5},{3,7},{5,1},{7,3},{8,12},{10,14},{12... | collective-permute-start | bytes 221192 | tf_op jit(solution)/shard_map/ppermute | solution.py:111
  52.3 2.9 %collective-permute-start = (bf16[32,1152]{1,0:T(8,128)(2,1)S(1)}, bf16[32,1152]{1,0:T(8,128)(2,1)S(1)}, u32[]{:S(2)}, u32[]{:S(2)}) collective-permute-start(bf16[32,1152]{1,0:T(8,128)(2,1)S(1)} %fusion.15), channel_id=1, source_target_pairs={{0,2},{2,4},{4,6},{6,0},{1,3},{3,5},{5,7},{7,1},{8,10},{10,12},{12... | collective-permute-start | bytes 221192 | tf_op jit(solution)/shard_map/ppermute | solution.py:111
  60.4 4.7 %collective-permute-start.5 = (bf16[128,1152]{1,0:T(8,128)(2,1)S(1)}, bf16[128,1152]{1,0:T(8,128)(2,1)S(1)}, u32[]{:S(2)}, u32[]{:S(2)}) collective-permute-start(bf16[128,1152]{1,0:T(8,128)(2,1)S(1)} %pad_maximum_fusion.refs_0_), channel_id=1, source_target_pairs={{0,48},{16,0},{32,16},{48,32},{1,49},{17,1},{33,17},{49,33},{2,50}... | collective-permute-start | bytes 884744 | tf_op jit(solution)/shard_map/ppermute | solution.py:111
  65.1 2.7 %collective-permute-start.4 = (bf16[128,1152]{1,0:T(8,128)(2,1)S(1)}, bf16[128,1152]{1,0:T(8,128)(2,1)S(1)}, u32[]{:S(2)}, u32[]{:S(2)}) collective-permute-start(bf16[128,1152]{1,0:T(8,128)(2,1)S(1)} %pad_maximum_fusion.refs_0_), channel_id=1, source_target_pairs={{0,32},{16,48},{32,0},{48,16},{1,33},{17,49},{33,1},{49,17},{2,34}... | collective-permute-start | bytes 884744 | tf_op jit(solution)/shard_map/ppermute | solution.py:111
  67.8 2.8 %collective-permute-start.3 = (bf16[128,1152]{1,0:T(8,128)(2,1)S(1)}, bf16[128,1152]{1,0:T(8,128)(2,1)S(1)}, u32[]{:S(2)}, u32[]{:S(2)}) collective-permute-start(bf16[128,1152]{1,0:T(8,128)(2,1)S(1)} %pad_maximum_fusion.refs_0_), channel_id=1, source_target_pairs={{0,16},{16,32},{32,48},{48,0},{1,17},{17,33},{33,49},{49,1},{2,18}... | collective-permute-start | bytes 884744 | tf_op jit(solution)/shard_map/ppermute | solution.py:111
  70.6 2.6 %select_convert_fusion.1.codes_ref = bf16[1024,512]{1,0:T(8,128)(2,1)} fusion(bf16[32,16]{0,1:T(8,128)(2,1)} %fusion.3, s32[1024]{0:T(1024)S(1)} %get-tuple-element.22, pred[512]{0:T(512)(128)(4,1)S(1)} %iota_compare_fusion.27, s32[1024]{0:T(1024)S(1)} %get-tuple-element.21, s32[512]{0:T(512)S(1)} %add_select_fusion.1), kind=kOutput, calls=%fused_computation.3 | convolution fusion | flops 21012480 | bytes 1060352 | tf_op jit(solution)/shard_map/dot_general | solution.py:183
  73.3 3.0 %collective-permute-done.5.refs_3_ = bf16[128,1152]{1,0:T(8,128)(2,1)S(1)} collective-permute-done((bf16[128,1152]{1,0:T(8,128)(2,1)S(1)}, bf16[128,1152]{1,0:T(8,128)(2,1)S(1)}, u32[]{:S(2)}, u32[]{:S(2)}) %collective-permute-start.5) | collective-permute-done | bytes 294944 | tf_op jit(solution)/shard_map/ppermute | solution.py:111
  78.4 3.4 %collective-permute-done.3.refs_1_ = bf16[128,1152]{1,0:T(8,128)(2,1)S(1)} collective-permute-done((bf16[128,1152]{1,0:T(8,128)(2,1)S(1)}, bf16[128,1152]{1,0:T(8,128)(2,1)S(1)}, u32[]{:S(2)}, u32[]{:S(2)}) %collective-permute-start.3) | collective-permute-done | bytes 294944 | tf_op jit(solution)/shard_map/ppermute | solution.py:111
  83.0 5.0 %shard_map.59 = (bf16[1024,512]{1,0:T(8,128)(2,1)S(1)}, f32[512,1280]{1,0:T(8,128)S(1)}, f32[512,1152]{1,0:T(8,128)}, f32[8,512]{1,0:T(8,128)S(1)}) custom-call(bf16[1024,512]{1,0:T(8,128)(2,1)S(1)} %copy-done.3, bf16[128,1152]{1,0:T(8,128)(2,1)S(1)} %pad_maximum_fusion.refs_0_, bf16[128,1152]{1,0:T(8,128)(2,1)S(1)} %collective-permute-done.3.refs_1_, ...), custom_call_target="tpu_custom_call" | custom-call | tf_op jit(solution)/shard_map/pallas_call | solution.py:91
  94.5 7.9 %all-to-all-start.2 = ((f32[32,8,128]{2,1,0:T(8,128)}), f32[32,8,128]{2,1,0:T(8,128)S(1)}, u32[]{:S(2)}, u32[]{:S(2)}) async-start(f32[32,8,128]{2,1,0:T(8,128)} %broadcast_in_dim.129), calls=%async_computation.2 | async-start | bytes 262144 | tf_op jit(solution)/shard_map/all_to_all | solution.py:130
  106.8 4.4 %all-to-all-done.2 = f32[32,8,128]{2,1,0:T(8,128)S(1)} async-done(((f32[32,8,128]{2,1,0:T(8,128)}), f32[32,8,128]{2,1,0:T(8,128)S(1)}, u32[]{:S(2)}, u32[]{:S(2)}) %all-to-all-start.2) | async-done | bytes 131104 | tf_op jit(solution)/shard_map/all_to_all | solution.py:130
  112.6 3.8 %select_convert_fusion = f16[512,1280]{1,0:T(8,128)(2,1)} fusion(f32[512,1280]{1,0:T(8,128)} %copy-done, f32[512,1152]{1,0:T(8,128)} %collective-permute-done.13, f32[1280]{0:T(1024)S(1)} %select_select_fusion, pred[1280]{0:T(1024)(128)(4,1)S(1)} %iota_compare_fusion.16), kind=kLoop, calls=%fused_computation.2 | loop fusion | flops 1966080 | bytes 6297856 | tf_op jit(solution)/shard_map/convert_element_type | solution.py:222
  116.4 5.1 %all-to-all-start.3 = ((f16[4,128,1280]{2,1,0:T(8,128)(2,1)}), f16[4,128,1280]{2,1,0:T(8,128)(2,1)S(1)}, u32[]{:S(2)}, u32[]{:S(2)}) async-start(f16[4,128,1280]{2,1,0:T(8,128)(2,1)} %bitcast.2), calls=%async_computation.3 | async-start | bytes 2621440 | tf_op jit(solution)/shard_map/all_to_all | solution.py:153
  121.7 3.0 %collective-permute-start.7 = (f16[128,1152]{1,0:T(8,128)(2,1)S(1)}, f16[128,1152]{1,0:T(8,128)(2,1)S(1)}, u32[]{:S(2)}, u32[]{:S(2)}) collective-permute-start(f16[128,1152]{1,0:T(8,128)(2,1)S(1)} %get-tuple-element.13), channel_id=1, source_target_pairs={{0,48},{16,0},{32,16},{48,32},{1,49},{17,1},{33,17},{49,33},{2,50}... | collective-permute-start | bytes 884744 | tf_op jit(solution)/shard_map/ppermute | solution.py:111
  124.7 2.8 %collective-permute-start.9 = (f16[128,1152]{1,0:T(8,128)(2,1)S(1)}, f16[128,1152]{1,0:T(8,128)(2,1)S(1)}, u32[]{:S(2)}, u32[]{:S(2)}) collective-permute-start(f16[128,1152]{1,0:T(8,128)(2,1)S(1)} %get-tuple-element.14), channel_id=1, source_target_pairs={{0,16},{16,32},{32,48},{48,0},{1,17},{17,33},{33,49},{49,1},{2,18}... | collective-permute-start | bytes 884744 | tf_op jit(solution)/shard_map/ppermute | solution.py:111
  127.5 3.3 %collective-permute-start.8 = (f16[128,1152]{1,0:T(8,128)(2,1)S(1)}, f16[128,1152]{1,0:T(8,128)(2,1)S(1)}, u32[]{:S(2)}, u32[]{:S(2)}) collective-permute-start(f16[128,1152]{1,0:T(8,128)(2,1)S(1)} %get-tuple-element.15), channel_id=1, source_target_pairs={{0,32},{16,48},{32,0},{48,16},{1,33},{17,49},{33,1},{49,17},{2,34}... | collective-permute-start | bytes 884744 | tf_op jit(solution)/shard_map/ppermute | solution.py:111
  132.4 10.0 %collective-permute-done.9 = f16[128,1152]{1,0:T(8,128)(2,1)S(1)} collective-permute-done((f16[128,1152]{1,0:T(8,128)(2,1)S(1)}, f16[128,1152]{1,0:T(8,128)(2,1)S(1)}, u32[]{:S(2)}, u32[]{:S(2)}) %collective-permute-start.9) | collective-permute-done | bytes 294944 | tf_op jit(solution)/shard_map/ppermute | solution.py:111
  144.6 3.5 %all-to-all-start.4 = ((f16[4,32,1280]{2,1,0:T(8,128)(2,1)}), f16[4,32,1280]{2,1,0:T(8,128)(2,1)S(1)}, u32[]{:S(2)}, u32[]{:S(2)}) async-start(f16[4,32,1280]{2,1,0:T(8,128)(2,1)} %bitcast.3), calls=%async_computation.4 | async-start | bytes 655360 | tf_op jit(solution)/shard_map/all_to_all | solution.py:153
  148.1 3.4 %collective-permute-start.10 = (f16[32,1152]{1,0:T(8,128)(2,1)S(1)}, f16[32,1152]{1,0:T(8,128)(2,1)S(1)}, u32[]{:S(2)}, u32[]{:S(2)}) collective-permute-start(f16[32,1152]{1,0:T(8,128)(2,1)S(1)} %get-tuple-element.16), channel_id=1, source_target_pairs={{0,6},{2,0},{4,2},{6,4},{1,7},{3,1},{5,3},{7,5},{8,14},{10,8},{12,... | collective-permute-start | bytes 221192 | tf_op jit(solution)/shard_map/ppermute | solution.py:111
  157.9 4.8 %collective-permute-done.10 = f16[32,1152]{1,0:T(8,128)(2,1)S(1)} collective-permute-done((f16[32,1152]{1,0:T(8,128)(2,1)S(1)}, f16[32,1152]{1,0:T(8,128)(2,1)S(1)}, u32[]{:S(2)}, u32[]{:S(2)}) %collective-permute-start.10) | collective-permute-done | bytes 73760 | tf_op jit(solution)/shard_map/ppermute | solution.py:111
  162.7 3.5 %collective-permute-done.12 = f16[32,1152]{1,0:T(8,128)(2,1)S(1)} collective-permute-done((f16[32,1152]{1,0:T(8,128)(2,1)S(1)}, f16[32,1152]{1,0:T(8,128)(2,1)S(1)}, u32[]{:S(2)}, u32[]{:S(2)}) %collective-permute-start.12) | collective-permute-done | bytes 73760 | tf_op jit(solution)/shard_map/ppermute | solution.py:111
  (73 shorter events, 38.3 us)
Async XLA Ops:
  1.6 40.4 %copy-start.6 = (bf16[32,1152]{1,0:T(8,128)(2,1)S(1)}, bf16[32,1152]{1,0:T(8,128)(2,1)}, u32[]{:S(2)}) copy-start(bf16[32,1152]{1,0:T(8,128)(2,1)} %param.3) | copy-start | bytes 221188
  36.0 21.3 %copy-start.8 = (s32[128,128]{1,0:T(8,128)S(1)}, s32[128,128]{1,0:T(8,128)}, u32[]{:S(2)}) copy-start(s32[128,128]{1,0:T(8,128)} %param.5) | copy-start | bytes 196612
  37.1 18.2 %all-to-all-start.1 = ((bf16[4,128,1152]{2,1,0:T(8,128)(2,1)}), bf16[4,128,1152]{2,1,0:T(8,128)(2,1)S(1)}, u32[]{:S(2)}, u32[]{:S(2)}) async-start(bf16[4,128,1152]{2,1,0:T(8,128)(2,1)} %broadcast_in_dim.127), calls=%async_computation.1 | async-start | bytes 2359296 | tf_op jit(solution)/shard_map/all_to_all | solution.py:206
  42.2 16.1 %copy-start.10 = (f32[32]{0:T(128)}, f32[32]{0:T(128)S(1)}, u32[]{:S(2)}) copy-start(f32[32]{0:T(128)S(1)} %add_rsqrt_fusion.1) | copy-start | bytes 388
  42.2 16.0 %collective-permute-start.2 = (bf16[32,1152]{1,0:T(8,128)(2,1)S(1)}, bf16[32,1152]{1,0:T(8,128)(2,1)S(1)}, u32[]{:S(2)}, u32[]{:S(2)}) collective-permute-start(bf16[32,1152]{1,0:T(8,128)(2,1)S(1)} %fusion.15), channel_id=1, source_target_pairs={{0,6},{2,0},{4,2},{6,4},{1,7},{3,1},{5,3},{7,5},{8,14},{10,8},{12,... | collective-permute-start | bytes 221192 | tf_op jit(solution)/shard_map/ppermute | solution.py:111
  46.1 12.1 %collective-permute-start.1 = (bf16[32,1152]{1,0:T(8,128)(2,1)S(1)}, bf16[32,1152]{1,0:T(8,128)(2,1)S(1)}, u32[]{:S(2)}, u32[]{:S(2)}) collective-permute-start(bf16[32,1152]{1,0:T(8,128)(2,1)S(1)} %fusion.15), channel_id=1, source_target_pairs={{0,4},{2,6},{4,0},{6,2},{1,5},{3,7},{5,1},{7,3},{8,12},{10,14},{12... | collective-permute-start | bytes 221192 | tf_op jit(solution)/shard_map/ppermute | solution.py:111
  52.3 8.0 %collective-permute-start = (bf16[32,1152]{1,0:T(8,128)(2,1)S(1)}, bf16[32,1152]{1,0:T(8,128)(2,1)S(1)}, u32[]{:S(2)}, u32[]{:S(2)}) collective-permute-start(bf16[32,1152]{1,0:T(8,128)(2,1)S(1)} %fusion.15), channel_id=1, source_target_pairs={{0,2},{2,4},{4,6},{6,0},{1,3},{3,5},{5,7},{7,1},{8,10},{10,12},{12... | collective-permute-start | bytes 221192 | tf_op jit(solution)/shard_map/ppermute | solution.py:111
  55.3 26.5 %collective-permute-start.6 = (bf16[512,1152]{1,0:T(8,128)(2,1)S(1)}, bf16[512,1152]{1,0:T(8,128)(2,1)S(1)}, u32[]{:S(2)}, u32[]{:S(2)}) collective-permute-start(bf16[512,1152]{1,0:T(8,128)(2,1)S(1)} %bitcast.11), channel_id=1, source_target_pairs={{0,1},{1,0},{2,3},{3,2},{4,5},{5,4},{6,7},{7,6},{8,9},{9,8},{10,11... | collective-permute-start | bytes 3538952 | tf_op jit(solution)/shard_map/ppermute | solution.py:107
  60.4 15.8 %collective-permute-start.5 = (bf16[128,1152]{1,0:T(8,128)(2,1)S(1)}, bf16[128,1152]{1,0:T(8,128)(2,1)S(1)}, u32[]{:S(2)}, u32[]{:S(2)}) collective-permute-start(bf16[128,1152]{1,0:T(8,128)(2,1)S(1)} %pad_maximum_fusion.refs_0_), channel_id=1, source_target_pairs={{0,48},{16,0},{32,16},{48,32},{1,49},{17,1},{33,17},{49,33},{2,50}... | collective-permute-start | bytes 884744 | tf_op jit(solution)/shard_map/ppermute | solution.py:111
  65.1 13.3 %collective-permute-start.4 = (bf16[128,1152]{1,0:T(8,128)(2,1)S(1)}, bf16[128,1152]{1,0:T(8,128)(2,1)S(1)}, u32[]{:S(2)}, u32[]{:S(2)}) collective-permute-start(bf16[128,1152]{1,0:T(8,128)(2,1)S(1)} %pad_maximum_fusion.refs_0_), channel_id=1, source_target_pairs={{0,32},{16,48},{32,0},{48,16},{1,33},{17,49},{33,1},{49,17},{2,34}... | collective-permute-start | bytes 884744 | tf_op jit(solution)/shard_map/ppermute | solution.py:111
  67.8 14.0 %collective-permute-start.3 = (bf16[128,1152]{1,0:T(8,128)(2,1)S(1)}, bf16[128,1152]{1,0:T(8,128)(2,1)S(1)}, u32[]{:S(2)}, u32[]{:S(2)}) collective-permute-start(bf16[128,1152]{1,0:T(8,128)(2,1)S(1)} %pad_maximum_fusion.refs_0_), channel_id=1, source_target_pairs={{0,16},{16,32},{32,48},{48,0},{1,17},{17,33},{33,49},{49,1},{2,18}... | collective-permute-start | bytes 884744 | tf_op jit(solution)/shard_map/ppermute | solution.py:111
  90.6 21.9 %collective-permute-start.13 = (f32[512,1152]{1,0:T(8,128)}, f32[512,1152]{1,0:T(8,128)}, u32[]{:S(2)}, u32[]{:S(2)}) collective-permute-start(f32[512,1152]{1,0:T(8,128)} %get-tuple-element.10), channel_id=1, source_target_pairs={{0,1},{1,0},{2,3},{3,2},{4,5},{5,4},{6,7},{7,6},{8,9},{9,8},{10,11... | collective-permute-start | bytes 7077896 | tf_op jit(solution)/shard_map/ppermute | solution.py:107
  94.5 16.8 %all-to-all-start.2 = ((f32[32,8,128]{2,1,0:T(8,128)}), f32[32,8,128]{2,1,0:T(8,128)S(1)}, u32[]{:S(2)}, u32[]{:S(2)}) async-start(f32[32,8,128]{2,1,0:T(8,128)} %broadcast_in_dim.129), calls=%async_computation.2 | async-start | bytes 262144 | tf_op jit(solution)/shard_map/all_to_all | solution.py:130
  116.4 14.4 %copy-start.2 = (bf16[32,1152]{1,0:T(8,128)(2,1)S(1)}, bf16[32,1152]{1,0:T(8,128)(2,1)}, u32[]{:S(2)}) copy-start(bf16[32,1152]{1,0:T(8,128)(2,1)} %values_ref.1) | copy-start | bytes 221188
  116.4 27.2 %all-to-all-start.3 = ((f16[4,128,1280]{2,1,0:T(8,128)(2,1)}), f16[4,128,1280]{2,1,0:T(8,128)(2,1)S(1)}, u32[]{:S(2)}, u32[]{:S(2)}) async-start(f16[4,128,1280]{2,1,0:T(8,128)(2,1)} %bitcast.2), calls=%async_computation.3 | async-start | bytes 2621440 | tf_op jit(solution)/shard_map/all_to_all | solution.py:153
  121.7 10.7 %collective-permute-start.7 = (f16[128,1152]{1,0:T(8,128)(2,1)S(1)}, f16[128,1152]{1,0:T(8,128)(2,1)S(1)}, u32[]{:S(2)}, u32[]{:S(2)}) collective-permute-start(f16[128,1152]{1,0:T(8,128)(2,1)S(1)} %get-tuple-element.13), channel_id=1, source_target_pairs={{0,48},{16,0},{32,16},{48,32},{1,49},{17,1},{33,17},{49,33},{2,50}... | collective-permute-start | bytes 884744 | tf_op jit(solution)/shard_map/ppermute | solution.py:111
  124.7 17.7 %collective-permute-start.9 = (f16[128,1152]{1,0:T(8,128)(2,1)S(1)}, f16[128,1152]{1,0:T(8,128)(2,1)S(1)}, u32[]{:S(2)}, u32[]{:S(2)}) collective-permute-start(f16[128,1152]{1,0:T(8,128)(2,1)S(1)} %get-tuple-element.14), channel_id=1, source_target_pairs={{0,16},{16,32},{32,48},{48,0},{1,17},{17,33},{33,49},{49,1},{2,18}... | collective-permute-start | bytes 884744 | tf_op jit(solution)/shard_map/ppermute | solution.py:111
  127.5 14.9 %collective-permute-start.8 = (f16[128,1152]{1,0:T(8,128)(2,1)S(1)}, f16[128,1152]{1,0:T(8,128)(2,1)S(1)}, u32[]{:S(2)}, u32[]{:S(2)}) collective-permute-start(f16[128,1152]{1,0:T(8,128)(2,1)S(1)} %get-tuple-element.15), channel_id=1, source_target_pairs={{0,32},{16,48},{32,0},{48,16},{1,33},{17,49},{33,1},{49,17},{2,34}... | collective-permute-start | bytes 884744 | tf_op jit(solution)/shard_map/ppermute | solution.py:111
  143.6 24.9 %copy-start.7 = (bf16[32,1152]{1,0:T(8,128)(2,1)S(1)}, bf16[32,1152]{1,0:T(8,128)(2,1)}, u32[]{:S(2)}) copy-start(bf16[32,1152]{1,0:T(8,128)(2,1)} %param.3) | copy-start | bytes 221188
  143.6 24.9 %copy-start.11 = (f32[32]{0:T(128)S(1)}, f32[32]{0:T(128)}, u32[]{:S(2)}) copy-start(f32[32]{0:T(128)} %copy-done.10) | copy-start | bytes 388
  144.6 26.5 %all-to-all-start.4 = ((f16[4,32,1280]{2,1,0:T(8,128)(2,1)}), f16[4,32,1280]{2,1,0:T(8,128)(2,1)S(1)}, u32[]{:S(2)}, u32[]{:S(2)}) async-start(f16[4,32,1280]{2,1,0:T(8,128)(2,1)} %bitcast.3), calls=%async_computation.4 | async-start | bytes 655360 | tf_op jit(solution)/shard_map/all_to_all | solution.py:153
  148.1 14.6 %collective-permute-start.10 = (f16[32,1152]{1,0:T(8,128)(2,1)S(1)}, f16[32,1152]{1,0:T(8,128)(2,1)S(1)}, u32[]{:S(2)}, u32[]{:S(2)}) collective-permute-start(f16[32,1152]{1,0:T(8,128)(2,1)S(1)} %get-tuple-element.16), channel_id=1, source_target_pairs={{0,6},{2,0},{4,2},{6,4},{1,7},{3,1},{5,3},{7,5},{8,14},{10,8},{12,... | collective-permute-start | bytes 221192 | tf_op jit(solution)/shard_map/ppermute | solution.py:111
  151.5 14.6 %collective-permute-start.12 = (f16[32,1152]{1,0:T(8,128)(2,1)S(1)}, f16[32,1152]{1,0:T(8,128)(2,1)S(1)}, u32[]{:S(2)}, u32[]{:S(2)}) collective-permute-start(f16[32,1152]{1,0:T(8,128)(2,1)S(1)} %get-tuple-element.17), channel_id=1, source_target_pairs={{0,2},{2,4},{4,6},{6,0},{1,3},{3,5},{5,7},{7,1},{8,10},{10,12},{12... | collective-permute-start | bytes 221192 | tf_op jit(solution)/shard_map/ppermute | solution.py:111
  154.0 14.5 %collective-permute-start.11 = (f16[32,1152]{1,0:T(8,128)(2,1)S(1)}, f16[32,1152]{1,0:T(8,128)(2,1)S(1)}, u32[]{:S(2)}, u32[]{:S(2)}) collective-permute-start(f16[32,1152]{1,0:T(8,128)(2,1)S(1)} %get-tuple-element.18), channel_id=1, source_target_pairs={{0,4},{2,6},{4,0},{6,2},{1,5},{3,7},{5,1},{7,3},{8,12},{10,14},{12... | collective-permute-start | bytes 221192 | tf_op jit(solution)/shard_map/ppermute | solution.py:111
  (6 other events, 19.7 us)
where the time goes:
time: 176 us; the launch traced here: 175 us
  starting transfers between devices  66 us (38%)
  waiting for transfers between devices  38.8 us (22%)
  blocking collectives  34.4 us (20%)
  other arithmetic  10.9 us (6%)
  matrix products  7.94 us (5%)
  local copies, waits for them, and re-layouts  7.29 us (4%)
  Pallas kernels  5.16 us (3%)
  between operations  4.13 us (2%)
    ppermute x12, starting transfers between devices, turned(): lax.ppermute(value, axis, [(k, (k + steps) % SIDE) for k in range(SIDE)])  40.7 us
    all_to_all x1, blocking collectives, step(): got = lax.all_to_all(normalized_slots(texts), ZB, 0, 0, tiled=True)  34.4 us
    ppermute x12, waiting for transfers between devices, turned(): lax.ppermute(value, axis, [(k, (k + steps) % SIDE) for k in range(SIDE)])  32.7 us
    all_to_all x2, starting transfers between devices, sent_and_summed(): got = lax.all_to_all(parts, axis, 0, 0, tiled=True)  8.55 us
    all_to_all x1, starting transfers between devices, over_image_group(): return jnp.sum(lax.all_to_all(sent, axes, 0, 0, tiled=True)[:, 0, 0])  7.93 us
    pallas_call x1, Pallas kernels, pair_terms(): pl.pallas_call(pair_kernel, out_shape=(pltpu.VMEM((2 * half, images), jnp...  5.04 us
    all_to_all x1, starting transfers between devices, step(): lax.all_to_all(sent, 'y', 0, 0, tiled=True).reshape(16 * rows, width)  4.91 us
    unnamed x24, local copies, waits for them, and re-layouts  4.68 us
  transfers between devices with their start and end apart: 18, of which 11 were waited for; matrix products, arithmetic and copies ran while one was open for 8% of the time, Pallas kernels for 0%

commit v1 on v0

--- a/solution.py
+++ b/solution.py
@@ -13,6 +13,7 @@
 EPS = 1e-06
 ROWS_AXES = ("x", "zb", "za", "c", "y", "zh")
 ZB = ("zh", "zb")
+IMAGE_GROUP = ("x", "za", "c")
 SIDE = 4
 DIGITS = 7
 BASE = 512.0
@@ -44,16 +45,21 @@
     )(values)
 
 
-def pair_kernel(codes_ref, *refs):
+def pair_kernel(own_text_ref, masked_ref, arrived_ref, *refs):
+    del arrived_ref
     part_refs, (own_ref, other_ref) = refs[:SIDE], refs[SIDE : SIDE + 2]
     coef_ref, own_sums_ref, other_sums_ref, loss_ref, group_ref = refs[SIDE + 2 :]
     near = part_refs[0].shape[0]
     for k in range(SIDE):
         group_ref[k * near : (k + 1) * near] = part_refs[k][...]
     group = group_ref[...]
-    width = group.shape[1]
+    images, _ = group.shape
     half = own_ref.shape[0]
-    loss = jnp.zeros((8, group.shape[0]), jnp.float32)
+    rows = 2 * half // masked_ref.shape[0]
+    shape = (CHUNK, images)
+    columns = lax.broadcasted_iota(jnp.int32, shape, 1)
+    diagonal = columns - lax.broadcasted_iota(jnp.int32, shape, 0)
+    loss = jnp.zeros((8, images), jnp.float32)
     for texts_ref, sums_ref, base in ((other_ref, other_sums_ref, half), (own_ref, own_sums_ref, 0)):
         for at in range(0, half, CHUNK):
             logits = TEMP * lax.dot_general(
@@ -63,44 +69,48 @@
                 preferred_element_type=jnp.float32,
             )
             logits = logits + BIAS
-            codes = codes_ref[base + at : base + at + CHUNK].astype(jnp.float32)
+            first = (base + at) // rows
+            masked = masked_ref[first : first + CHUNK // rows]
+            masked = jnp.broadcast_to(masked[:, None], (CHUNK // rows, rows, images)).reshape(shape)
+            valid = masked < 0.5
             small = jnp.exp(-jnp.abs(logits))
             soft = jnp.maximum(logits, 0.0) + jnp.log1p(small)
             sigmoid = jnp.where(logits >= 0.0, 1.0, small) / (1.0 + small)
-            matched = codes > 1.5
-            terms = jnp.where(codes > 0.5, soft - jnp.where(matched, logits, 0.0), 0.0)
-            loss = loss + jnp.sum(terms.reshape(CHUNK // 8, 8, terms.shape[1]), axis=0)
-            coef = jnp.where(codes > 0.5, sigmoid - jnp.where(matched, 1.0, 0.0), 0.0)
-            coef = coef.astype(jnp.bfloat16)
+            if base == 0:
+                matched = (diagonal == at - own_text_ref[0, 0] * rows) & (columns < rows)
+                soft = soft - jnp.where(matched, logits, 0.0)
+                sigmoid = sigmoid - jnp.where(matched, 1.0, 0.0)
+                valid = valid | matched
+            terms = jnp.where(valid, soft, 0.0)
+            loss = loss + jnp.sum(terms.reshape(CHUNK // 8, 8, images), axis=0)
+            coef = jnp.where(valid, sigmoid, 0.0).astype(jnp.bfloat16)
             coef_ref[base + at : base + at + CHUNK] = coef
-            sums_ref[at : at + CHUNK, :width] = jnp.dot(
-                coef, group, preferred_element_type=jnp.float32
-            )
-    own_sums_ref[:, width:] = jnp.zeros((half, own_sums_ref.shape[1] - width), jnp.float32)
-    loss_ref[...] = loss
+            sums_ref[at : at + CHUNK] = jnp.dot(coef, group, preferred_element_type=jnp.float32)
+    total = jnp.sum(jnp.sum(loss, axis=0, keepdims=True), axis=1, keepdims=True)
+    loss_ref[...] = jnp.broadcast_to(total[None], loss_ref.shape)
 
 
 def placed(value):
     return pltpu.with_memory_space_constraint(value, pltpu.VMEM)
 
 
-def pair_terms(codes, parts, own_texts, other_texts):
+def pair_terms(own_text, masked, arrived, parts, own_texts, other_texts, peers):
     near, width = parts[0].shape
     half = own_texts.shape[0]
     images = SIDE * near
     return pl.pallas_call(
         pair_kernel,
         out_shape=(
-            pltpu.VMEM((2 * half, images), jnp.bfloat16),
-            pltpu.VMEM((half, width + SPARE), jnp.float32),
+            jax.ShapeDtypeStruct((2 * half, images), jnp.bfloat16),
+            jax.ShapeDtypeStruct((half, width), jnp.float32),
             pltpu.VMEM((half, width), jnp.float32),
-            pltpu.VMEM((8, images), jnp.float32),
+            pltpu.VMEM((peers, 8, 128), jnp.float32),
         ),
-        in_specs=[VMEM] * (SIDE + 3),
+        in_specs=[pl.BlockSpec(memory_space=pltpu.SMEM)] + [VMEM] * (SIDE + 4),
         out_specs=(VMEM,) * 4,
         scratch_shapes=[pltpu.VMEM((images, width), jnp.bfloat16)],
         compiler_params=pltpu.CompilerParams(vmem_limit_bytes=20 * 2**20),
-    )(*(placed(a) for a in (codes, *parts, own_texts, other_texts)))
+    )(own_text, *(placed(a) for a in (masked, arrived, *parts, own_texts, other_texts)))
 
 
 def swapped(value):
@@ -120,14 +130,7 @@
     got = [turned(parts[k].astype(jnp.float16), axis, -k) for k in range(1, SIDE)]
     for part in got:
         sums = sums + part.astype(jnp.float32)
-    return sums
-
-
-def over_image_group(total):
-    axes = ("x", "za", "c")
-    count = lax.axis_size(axes)
-    sent = jnp.broadcast_to(total, (count, 8, 128))
-    return jnp.sum(lax.all_to_all(sent, axes, 0, 0, tiled=True)[:, 0, 0])
+    return lax.optimization_barrier(sums)
 
 
 def to_row(total, lanes, first):
@@ -173,17 +176,10 @@
     return lax.dot_general(left, chosen, (((1,), (1,)), ((), ())))
 
 
-def pair_codes(tile_mask, rows):
-    own_text = lax.axis_index("y") * 4 + lax.axis_index(ZB)
-    masked = block_mask(tile_mask)
+def mask_rows(tile_mask, rows):
     i = jnp.arange(16 * rows, dtype=jnp.int32)
-    j = jnp.arange(32 * rows, dtype=jnp.int32)
-    left = (j[:, None] // rows == jnp.arange(32)[None]).astype(jnp.float32)
     right = (jnp.arange(16)[:, None] == i[None] // rows).astype(jnp.float32)
-    masked = jnp.dot(jnp.dot(left, masked), right)
-    matched = i[None] == (j - own_text * rows)[:, None]
-    matched = matched & (i < rows)[None]
-    return jnp.where(matched, 2.0, jnp.where(masked < 0.5, 1.0, 0.0)).astype(jnp.bfloat16)
+    return jnp.dot(block_mask(tile_mask), right)
 
 
 def back(values, inverse, grads):
@@ -205,22 +201,29 @@
     sent = jnp.broadcast_to(got.reshape(1, SIDE * rows, width), (SIDE, SIDE * rows, width))
     own_texts = lax.all_to_all(sent, "y", 0, 0, tiled=True).reshape(16 * rows, width)
     other_texts = swapped(own_texts)
-    codes = pair_codes(tile_mask, rows)
-
-    coef, own_sums, other_sums, loss = pair_terms(codes, parts, own_texts, other_texts)
+    arrived = parts[1][:16, :128] + parts[2][:16, :128] + parts[3][:16, :128]
+    masked = mask_rows(tile_mask, rows)
+    own_text = (lax.axis_index("y") * SIDE + lax.axis_index(ZB)).reshape(1, 1)
+    peers = lax.axis_size(IMAGE_GROUP)
+    coef, own_sums, other_sums, loss = pair_terms(
+        own_text, masked, arrived, parts, own_texts, other_texts, peers
+    )
     other_sums = swapped(other_sums)
-    loss = over_image_group(jnp.sum(loss))
+    loss = lax.all_to_all(loss, IMAGE_GROUP, 0, 0, tiled=True)
+    loss = jnp.sum(loss[:, 0, 0])
     image_parts = lax.dot_general(
         coef[: 16 * rows], own_texts, (((0,), (0,)), ((), ())), preferred_element_type=jnp.float32
     ) + lax.dot_general(
         coef[16 * rows :], other_texts, (((0,), (0,)), ((), ())), preferred_element_type=jnp.float32
     )
-
-    lanes = lax.broadcasted_iota(jnp.int32, (1, width + SPARE), 1)
-    row = to_row(loss, lanes, width)
-    text_parts = own_sums + jnp.pad(other_sums, ((0, 0), (0, SPARE)))
-    text_parts = jnp.where(lanes >= width, row, text_parts).astype(jnp.float16)
-    text_parts = sent_and_summed(text_parts.reshape(SIDE, SIDE * rows, -1), "y")
+    payload = jnp.pad((own_sums + other_sums).astype(jnp.float16), ((0, 0), (0, SPARE)))
+    payload = lax.optimization_barrier(payload)
+    lanes = lax.broadcasted_iota(jnp.int32, (1, SPARE), 1)
+    row = to_row(loss, lanes, 0).astype(jnp.float16)
+    payload = lax.dynamic_update_slice(
+        payload, jnp.broadcast_to(row, (payload.shape[0], SPARE)), (0, width)
+    )
+    text_parts = sent_and_summed(payload.reshape(SIDE, SIDE * rows, -1), "y")
     image_parts = turned_and_summed(image_parts.reshape(SIDE, SIDE * rows, width), "x")
     text_parts = text_parts.astype(jnp.float16).reshape(SIDE, rows, -1)
     text_sums = sent_and_summed(text_parts, ZB)

time: 176 us -> 177 us (level)
  the two profiles are of different devices: /device:TPU:8 before, /device:TPU:34 now
where the time goes in v1:
time: 177 us; the launch traced here: 176 us
  starting transfers between devices  63.7 us (36%)
  waiting for transfers between devices  41.7 us (24%)
  blocking collectives  37.1 us (21%)
  other arithmetic  10.2 us (6%)
  local copies, waits for them, and re-layouts  7.44 us (4%)
  Pallas kernels  6.48 us (4%)
  matrix products  4.8 us (3%)
  between operations  4.15 us (2%)
    ppermute x12, starting transfers between devices, turned(): lax.ppermute(value, axis, [(k, (k + steps) % SIDE) for k in range(SIDE)])  41.7 us
    all_to_all x1, blocking collectives, step(): got = lax.all_to_all(normalized_slots(texts), ZB, 0, 0, tiled=True)  37.1 us
    all_to_all x2, waiting for transfers between devices, sent_and_summed(): got = lax.all_to_all(parts, axis, 0, 0, tiled=True)  24.1 us
    ppermute x12, waiting for transfers between devices, turned(): lax.ppermute(value, axis, [(k, (k + steps) % SIDE) for k in range(SIDE)])  10.7 us
    all_to_all x2, starting transfers between devices, sent_and_summed(): got = lax.all_to_all(parts, axis, 0, 0, tiled=True)  7.12 us
    all_to_all x1, waiting for transfers between devices, step(): lax.all_to_all(sent, 'y', 0, 0, tiled=True).reshape(16 * rows, width)  6.95 us
    all_to_all x1, starting transfers between devices, step(): loss = lax.all_to_all(loss, IMAGE_GROUP, 0, 0, tiled=True)  6.42 us
    pallas_call x1, Pallas kernels, pair_terms(): pl.pallas_call(pair_kernel, out_shape=(jax.ShapeDtypeStruct((2 * half, im...  6.36 us
  transfers between devices with their start and end apart: 18, of which 6 were waited for; matrix products, arithmetic and copies ran while one was open for 9% of the time, Pallas kernels for 0%

profile of v1, /device:TPU:34, one launch (start us, length us, event | category | flops | bytes accessed | tf_op | source)
XLA Modules:
  0.0 175.5 jit_solution(841624226631351234)
XLA Ops:
  1.6 37.1 %all_to_all.25 = bf16[4,32,1152]{2,1,0:T(8,128)(2,1)S(1)} all-to-all(bf16[4,32,1152]{2,1,0:T(8,128)(2,1)S(1)} %shard_map.58), channel_id=1, replica_groups=mesh['y'=4,'zh'=2,'x'=4,'zb'=2,'za'=4,'c'=2] {'zh','zb'}, dimensions={0} | all-to-all | bytes 589824 | tf_op jit(solution)/shard_map/all_to_all | solution.py:192
  39.9 4.6 %all-to-all-start.1 = ((bf16[4,128,1152]{2,1,0:T(8,128)(2,1)}), bf16[4,128,1152]{2,1,0:T(8,128)(2,1)S(1)}, u32[]{:S(2)}, u32[]{:S(2)}) async-start(bf16[4,128,1152]{2,1,0:T(8,128)(2,1)} %broadcast_in_dim.91), calls=%async_computation.1 | async-start | bytes 2359296 | tf_op jit(solution)/shard_map/all_to_all | solution.py:202
  44.7 1.9 %collective-permute-start.2 = (bf16[32,1152]{1,0:T(8,128)(2,1)S(1)}, bf16[32,1152]{1,0:T(8,128)(2,1)S(1)}, u32[]{:S(2)}, u32[]{:S(2)}) collective-permute-start(bf16[32,1152]{1,0:T(8,128)(2,1)S(1)} %fusion.10), channel_id=1, source_target_pairs={{0,6},{2,0},{4,2},{6,4},{1,7},{3,1},{5,3},{7,5},{8,14},{10,8},{12,... | collective-permute-start | bytes 221192 | tf_op jit(solution)/shard_map/ppermute | solution.py:121
  46.6 4.4 %collective-permute-start.1 = (bf16[32,1152]{1,0:T(8,128)(2,1)S(1)}, bf16[32,1152]{1,0:T(8,128)(2,1)S(1)}, u32[]{:S(2)}, u32[]{:S(2)}) collective-permute-start(bf16[32,1152]{1,0:T(8,128)(2,1)S(1)} %fusion.10), channel_id=1, source_target_pairs={{0,4},{2,6},{4,0},{6,2},{1,5},{3,7},{5,1},{7,3},{8,12},{10,14},{12... | collective-permute-start | bytes 221192 | tf_op jit(solution)/shard_map/ppermute | solution.py:121
  52.9 7.0 %all-to-all-done.1 = bf16[4,128,1152]{2,1,0:T(8,128)(2,1)S(1)} async-done(((bf16[4,128,1152]{2,1,0:T(8,128)(2,1)}), bf16[4,128,1152]{2,1,0:T(8,128)(2,1)S(1)}, u32[]{:S(2)}, u32[]{:S(2)}) %all-to-all-start.1) | async-done | bytes 1179680 | tf_op jit(solution)/shard_map/all_to_all | solution.py:202
  62.1 2.4 %collective-permute-start.5 = (bf16[128,1152]{1,0:T(8,128)(2,1)S(1)}, bf16[128,1152]{1,0:T(8,128)(2,1)S(1)}, u32[]{:S(2)}, u32[]{:S(2)}) collective-permute-start(bf16[128,1152]{1,0:T(8,128)(2,1)S(1)} %pad_maximum_fusion.refs_0_), channel_id=1, source_target_pairs={{0,48},{16,0},{32,16},{48,32},{1,49},{17,1},{33,17},{49,33},{2,50}... | collective-permute-start | bytes 884744 | tf_op jit(solution)/shard_map/ppermute | solution.py:121
  64.6 4.3 %collective-permute-start.4 = (bf16[128,1152]{1,0:T(8,128)(2,1)S(1)}, bf16[128,1152]{1,0:T(8,128)(2,1)S(1)}, u32[]{:S(2)}, u32[]{:S(2)}) collective-permute-start(bf16[128,1152]{1,0:T(8,128)(2,1)S(1)} %pad_maximum_fusion.refs_0_), channel_id=1, source_target_pairs={{0,32},{16,48},{32,0},{48,16},{1,33},{17,49},{33,1},{49,17},{2,34}... | collective-permute-start | bytes 884744 | tf_op jit(solution)/shard_map/ppermute | solution.py:121
  68.9 3.7 %collective-permute-start.3 = (bf16[128,1152]{1,0:T(8,128)(2,1)S(1)}, bf16[128,1152]{1,0:T(8,128)(2,1)}, u32[]{:S(2)}, u32[]{:S(2)}) collective-permute-start(bf16[128,1152]{1,0:T(8,128)(2,1)S(1)} %pad_maximum_fusion.refs_0_), channel_id=1, source_target_pairs={{0,16},{16,32},{32,48},{48,0},{1,17},{17,33},{33,49},{49,1},{2,18}... | collective-permute-start | bytes 884744 | tf_op jit(solution)/shard_map/ppermute | solution.py:121
  73.4 7.2 %collective-permute-done.4.refs_2_ = bf16[128,1152]{1,0:T(8,128)(2,1)S(1)} collective-permute-done((bf16[128,1152]{1,0:T(8,128)(2,1)S(1)}, bf16[128,1152]{1,0:T(8,128)(2,1)S(1)}, u32[]{:S(2)}, u32[]{:S(2)}) %collective-permute-start.4) | collective-permute-done | bytes 294944 | tf_op jit(solution)/shard_map/ppermute | solution.py:121
  80.7 2.9 %collective-permute-done.3.refs_1_ = bf16[128,1152]{1,0:T(8,128)(2,1)} collective-permute-done((bf16[128,1152]{1,0:T(8,128)(2,1)S(1)}, bf16[128,1152]{1,0:T(8,128)(2,1)}, u32[]{:S(2)}, u32[]{:S(2)}) %collective-permute-start.3) | collective-permute-done | bytes 294944 | tf_op jit(solution)/shard_map/ppermute | solution.py:121
  84.3 6.4 %shard_map.59 = (bf16[1024,512]{1,0:T(8,128)(2,1)S(1)}, f32[512,1152]{1,0:T(8,128)S(1)}, f32[512,1152]{1,0:T(8,128)}, f32[32,8,128]{2,1,0:T(8,128)}) custom-call(s32[1,1]{1,0:T(1,128)} %bitcast.own_text_ref, f32[32,512]{1,0:T(8,128)S(1)} %fusion.masked_ref, bf16[16,128]{1,0:T(8,128)(2,1)S(1)} %slice_add_fusion.2.arrived_ref, ...), custom_call_target="tpu_custom_call" | custom-call | tf_op jit(solution)/shard_map/pallas_call | solution.py:101
  96.4 6.4 %all-to-all-start.2 = ((f32[32,8,128]{2,1,0:T(8,128)}), f32[32,8,128]{2,1,0:T(8,128)}, u32[]{:S(2)}, u32[]{:S(2)}) async-start(f32[32,8,128]{2,1,0:T(8,128)} %get-tuple-element.10), calls=%async_computation.2 | async-start | bytes 262144 | tf_op jit(solution)/shard_map/all_to_all | solution.py:212
  102.8 2.0 %fusion.5 = f32[512,1152]{1,0:T(8,128)S(1)} fusion(bf16[512,1152]{1,0:T(8,128)(2,1)S(1)} %collective-permute-done.6.refs_5_, bf16[1024,512]{1,0:T(8,128)(2,1)} %copy-done.5), kind=kOutput, calls=%fused_computation.9 | convolution fusion | flops 603979776 | bytes 4063232 | tf_op jit(solution)/shard_map/dot_general | solution.py:216
  104.8 2.3 %fusion.56 = (f16[512,1152]{1,0:T(8,128)(2,1)S(1)}, f32[512,1152]{1,0:T(8,128)}) fusion(f32[512,1152]{1,0:T(8,128)S(1)} %fusion.5, bf16[512,1152]{1,0:T(8,128)(2,1)S(1)} %bitcast.14, bf16[1024,512]{1,0:T(8,128)(2,1)S(1)} %copy-done.6), kind=kOutput, calls=%fused_computation.120 | convolution fusion | flops 605159424 | bytes 7602176 | tf_op jit(solution)/shard_map/dot_general | solution.py:214
  108.2 2.6 %collective-permute-start.7 = (f16[128,1152]{1,0:T(8,128)(2,1)}, f16[128,1152]{1,0:T(8,128)(2,1)}, u32[]{:S(2)}, u32[]{:S(2)}) collective-permute-start(f16[128,1152]{1,0:T(8,128)(2,1)} %get-tuple-element.11), channel_id=1, source_target_pairs={{0,48},{16,0},{32,16},{48,32},{1,49},{17,1},{33,17},{49,33},{2,50}... | collective-permute-start | bytes 884744 | tf_op jit(solution)/shard_map/ppermute | solution.py:121
  110.7 3.3 %collective-permute-start.9 = (f16[128,1152]{1,0:T(8,128)(2,1)}, f16[128,1152]{1,0:T(8,128)(2,1)}, u32[]{:S(2)}, u32[]{:S(2)}) collective-permute-start(f16[128,1152]{1,0:T(8,128)(2,1)} %get-tuple-element.12), channel_id=1, source_target_pairs={{0,16},{16,32},{32,48},{48,0},{1,17},{17,33},{33,49},{49,1},{2,18}... | collective-permute-start | bytes 884744 | tf_op jit(solution)/shard_map/ppermute | solution.py:121
  114.0 5.2 %collective-permute-start.8 = (f16[128,1152]{1,0:T(8,128)(2,1)}, f16[128,1152]{1,0:T(8,128)(2,1)}, u32[]{:S(2)}, u32[]{:S(2)}) collective-permute-start(f16[128,1152]{1,0:T(8,128)(2,1)} %get-tuple-element.13), channel_id=1, source_target_pairs={{0,32},{16,48},{32,0},{48,16},{1,33},{17,49},{33,1},{49,17},{2,34}... | collective-permute-start | bytes 884744 | tf_op jit(solution)/shard_map/ppermute | solution.py:121
  125.4 3.5 %all-to-all-start.3 = ((f16[4,128,1280]{2,1,0:T(8,128)(2,1)}), f16[4,128,1280]{2,1,0:T(8,128)(2,1)S(1)}, u32[]{:S(2)}, u32[]{:S(2)}) async-start(f16[4,128,1280]{2,1,0:T(8,128)(2,1)} %bitcast.3), calls=%async_computation.3 | async-start | bytes 2621440 | tf_op jit(solution)/shard_map/all_to_all | solution.py:156
  130.5 2.5 %collective-permute-start.10 = (f16[32,1152]{1,0:T(8,128)(2,1)S(1)}, f16[32,1152]{1,0:T(8,128)(2,1)S(1)}, u32[]{:S(2)}, u32[]{:S(2)}) collective-permute-start(f16[32,1152]{1,0:T(8,128)(2,1)S(1)} %get-tuple-element.14), channel_id=1, source_target_pairs={{0,6},{2,0},{4,2},{6,4},{1,7},{3,1},{5,3},{7,5},{8,14},{10,8},{12,... | collective-permute-start | bytes 221192 | tf_op jit(solution)/shard_map/ppermute | solution.py:121
  133.0 3.4 %collective-permute-start.12 = (f16[32,1152]{1,0:T(8,128)(2,1)S(1)}, f16[32,1152]{1,0:T(8,128)(2,1)S(1)}, u32[]{:S(2)}, u32[]{:S(2)}) collective-permute-start(f16[32,1152]{1,0:T(8,128)(2,1)S(1)} %get-tuple-element.15), channel_id=1, source_target_pairs={{0,2},{2,4},{4,6},{6,0},{1,3},{3,5},{5,7},{7,1},{8,10},{10,12},{12... | collective-permute-start | bytes 221192 | tf_op jit(solution)/shard_map/ppermute | solution.py:121
  136.4 6.1 %collective-permute-start.11 = (f16[32,1152]{1,0:T(8,128)(2,1)S(1)}, f16[32,1152]{1,0:T(8,128)(2,1)S(1)}, u32[]{:S(2)}, u32[]{:S(2)}) collective-permute-start(f16[32,1152]{1,0:T(8,128)(2,1)S(1)} %get-tuple-element.16), channel_id=1, source_target_pairs={{0,4},{2,6},{4,0},{6,2},{1,5},{3,7},{5,1},{7,3},{8,12},{10,14},{12... | collective-permute-start | bytes 221192 | tf_op jit(solution)/shard_map/ppermute | solution.py:121
  142.5 4.1 %all-to-all-done.3 = f16[4,128,1280]{2,1,0:T(8,128)(2,1)S(1)} async-done(((f16[4,128,1280]{2,1,0:T(8,128)(2,1)}), f16[4,128,1280]{2,1,0:T(8,128)(2,1)S(1)}, u32[]{:S(2)}, u32[]{:S(2)}) %all-to-all-start.3) | async-done | bytes 1310752 | tf_op jit(solution)/shard_map/all_to_all | solution.py:156
  147.5 3.6 %all-to-all-start.4 = ((f16[4,32,1280]{2,1,0:T(8,128)(2,1)}), f16[4,32,1280]{2,1,0:T(8,128)(2,1)S(1)}, u32[]{:S(2)}, u32[]{:S(2)}) async-start(f16[4,32,1280]{2,1,0:T(8,128)(2,1)} %bitcast.4), calls=%async_computation.4 | async-start | bytes 655360 | tf_op jit(solution)/shard_map/all_to_all | solution.py:156
  152.1 20.0 %all-to-all-done.4 = f16[4,32,1280]{2,1,0:T(8,128)(2,1)S(1)} async-done(((f16[4,32,1280]{2,1,0:T(8,128)(2,1)}), f16[4,32,1280]{2,1,0:T(8,128)(2,1)S(1)}, u32[]{:S(2)}, u32[]{:S(2)}) %all-to-all-start.4) | async-done | bytes 327712 | tf_op jit(solution)/shard_map/all_to_all | solution.py:156
  (69 shorter events, 24.5 us)
Async XLA Ops:
  39.9 4.6 %copy-start.7 = (bf16[32,1152]{1,0:T(8,128)(2,1)S(1)}, bf16[32,1152]{1,0:T(8,128)(2,1)}, u32[]{:S(2)}) copy-start(bf16[32,1152]{1,0:T(8,128)(2,1)} %param.3) | copy-start | bytes 221188
  39.9 22.0 %copy-start.9 = (s32[128,128]{1,0:T(8,128)S(1)}, s32[128,128]{1,0:T(8,128)}, u32[]{:S(2)}) copy-start(s32[128,128]{1,0:T(8,128)} %param.5) | copy-start | bytes 196612
  39.9 20.0 %all-to-all-start.1 = ((bf16[4,128,1152]{2,1,0:T(8,128)(2,1)}), bf16[4,128,1152]{2,1,0:T(8,128)(2,1)S(1)}, u32[]{:S(2)}, u32[]{:S(2)}) async-start(bf16[4,128,1152]{2,1,0:T(8,128)(2,1)} %broadcast_in_dim.91), calls=%async_computation.1 | async-start | bytes 2359296 | tf_op jit(solution)/shard_map/all_to_all | solution.py:202
  44.7 17.4 %collective-permute-start.2 = (bf16[32,1152]{1,0:T(8,128)(2,1)S(1)}, bf16[32,1152]{1,0:T(8,128)(2,1)S(1)}, u32[]{:S(2)}, u32[]{:S(2)}) collective-permute-start(bf16[32,1152]{1,0:T(8,128)(2,1)S(1)} %fusion.10), channel_id=1, source_target_pairs={{0,6},{2,0},{4,2},{6,4},{1,7},{3,1},{5,3},{7,5},{8,14},{10,8},{12,... | collective-permute-start | bytes 221192 | tf_op jit(solution)/shard_map/ppermute | solution.py:121
  46.6 15.4 %collective-permute-start.1 = (bf16[32,1152]{1,0:T(8,128)(2,1)S(1)}, bf16[32,1152]{1,0:T(8,128)(2,1)S(1)}, u32[]{:S(2)}, u32[]{:S(2)}) collective-permute-start(bf16[32,1152]{1,0:T(8,128)(2,1)S(1)} %fusion.10), channel_id=1, source_target_pairs={{0,4},{2,6},{4,0},{6,2},{1,5},{3,7},{5,1},{7,3},{8,12},{10,14},{12... | collective-permute-start | bytes 221192 | tf_op jit(solution)/shard_map/ppermute | solution.py:121
  51.0 11.1 %collective-permute-start = (bf16[32,1152]{1,0:T(8,128)(2,1)S(1)}, bf16[32,1152]{1,0:T(8,128)(2,1)S(1)}, u32[]{:S(2)}, u32[]{:S(2)}) collective-permute-start(bf16[32,1152]{1,0:T(8,128)(2,1)S(1)} %fusion.10), channel_id=1, source_target_pairs={{0,2},{2,4},{4,6},{6,0},{1,3},{3,5},{5,7},{7,1},{8,10},{10,12},{12... | collective-permute-start | bytes 221192 | tf_op jit(solution)/shard_map/ppermute | solution.py:121
  59.9 24.4 %collective-permute-start.6 = (bf16[512,1152]{1,0:T(8,128)(2,1)S(1)}, bf16[512,1152]{1,0:T(8,128)(2,1)S(1)}, u32[]{:S(2)}, u32[]{:S(2)}) collective-permute-start(bf16[512,1152]{1,0:T(8,128)(2,1)S(1)} %bitcast.12), channel_id=1, source_target_pairs={{0,1},{1,0},{2,3},{3,2},{4,5},{5,4},{6,7},{7,6},{8,9},{9,8},{10,11... | collective-permute-start | bytes 3538952 | tf_op jit(solution)/shard_map/ppermute | solution.py:117
  62.1 11.3 %collective-permute-start.5 = (bf16[128,1152]{1,0:T(8,128)(2,1)S(1)}, bf16[128,1152]{1,0:T(8,128)(2,1)S(1)}, u32[]{:S(2)}, u32[]{:S(2)}) collective-permute-start(bf16[128,1152]{1,0:T(8,128)(2,1)S(1)} %pad_maximum_fusion.refs_0_), channel_id=1, source_target_pairs={{0,48},{16,0},{32,16},{48,32},{1,49},{17,1},{33,17},{49,33},{2,50}... | collective-permute-start | bytes 884744 | tf_op jit(solution)/shard_map/ppermute | solution.py:121
  64.6 16.1 %collective-permute-start.4 = (bf16[128,1152]{1,0:T(8,128)(2,1)S(1)}, bf16[128,1152]{1,0:T(8,128)(2,1)S(1)}, u32[]{:S(2)}, u32[]{:S(2)}) collective-permute-start(bf16[128,1152]{1,0:T(8,128)(2,1)S(1)} %pad_maximum_fusion.refs_0_), channel_id=1, source_target_pairs={{0,32},{16,48},{32,0},{48,16},{1,33},{17,49},{33,1},{49,17},{2,34}... | collective-permute-start | bytes 884744 | tf_op jit(solution)/shard_map/ppermute | solution.py:121
  68.9 14.7 %collective-permute-start.3 = (bf16[128,1152]{1,0:T(8,128)(2,1)S(1)}, bf16[128,1152]{1,0:T(8,128)(2,1)}, u32[]{:S(2)}, u32[]{:S(2)}) collective-permute-start(bf16[128,1152]{1,0:T(8,128)(2,1)S(1)} %pad_maximum_fusion.refs_0_), channel_id=1, source_target_pairs={{0,16},{16,32},{32,48},{48,0},{1,17},{17,33},{33,49},{49,1},{2,18}... | collective-permute-start | bytes 884744 | tf_op jit(solution)/shard_map/ppermute | solution.py:121
  84.3 12.0 %copy-start.3 = (bf16[32,1152]{1,0:T(8,128)(2,1)S(1)}, bf16[32,1152]{1,0:T(8,128)(2,1)}, u32[]{:S(2)}) copy-start(bf16[32,1152]{1,0:T(8,128)(2,1)} %values_ref.1) | copy-start | bytes 221188
  93.0 28.5 %collective-permute-start.13 = (f32[512,1152]{1,0:T(8,128)}, f32[512,1152]{1,0:T(8,128)}, u32[]{:S(2)}, u32[]{:S(2)}) collective-permute-start(f32[512,1152]{1,0:T(8,128)} %get-tuple-element.9), channel_id=1, source_target_pairs={{0,1},{1,0},{2,3},{3,2},{4,5},{5,4},{6,7},{7,6},{8,9},{9,8},{10,11... | collective-permute-start | bytes 7077896 | tf_op jit(solution)/shard_map/ppermute | solution.py:117
  96.4 22.9 %all-to-all-start.2 = ((f32[32,8,128]{2,1,0:T(8,128)}), f32[32,8,128]{2,1,0:T(8,128)}, u32[]{:S(2)}, u32[]{:S(2)}) async-start(f32[32,8,128]{2,1,0:T(8,128)} %get-tuple-element.10), calls=%async_computation.2 | async-start | bytes 262144 | tf_op jit(solution)/shard_map/all_to_all | solution.py:212
  104.8 16.7 %copy-start.1 = (f32[512,1152]{1,0:T(8,128)S(1)}, f32[512,1152]{1,0:T(8,128)}, u32[]{:S(2)}) copy-start(f32[512,1152]{1,0:T(8,128)} %copy-done) | copy-start | bytes 7077892
  108.2 20.8 %collective-permute-start.7 = (f16[128,1152]{1,0:T(8,128)(2,1)}, f16[128,1152]{1,0:T(8,128)(2,1)}, u32[]{:S(2)}, u32[]{:S(2)}) collective-permute-start(f16[128,1152]{1,0:T(8,128)(2,1)} %get-tuple-element.11), channel_id=1, source_target_pairs={{0,48},{16,0},{32,16},{48,32},{1,49},{17,1},{33,17},{49,33},{2,50}... | collective-permute-start | bytes 884744 | tf_op jit(solution)/shard_map/ppermute | solution.py:121
  110.7 18.2 %collective-permute-start.9 = (f16[128,1152]{1,0:T(8,128)(2,1)}, f16[128,1152]{1,0:T(8,128)(2,1)}, u32[]{:S(2)}, u32[]{:S(2)}) collective-permute-start(f16[128,1152]{1,0:T(8,128)(2,1)} %get-tuple-element.12), channel_id=1, source_target_pairs={{0,16},{16,32},{32,48},{48,0},{1,17},{17,33},{33,49},{49,1},{2,18}... | collective-permute-start | bytes 884744 | tf_op jit(solution)/shard_map/ppermute | solution.py:121
  114.0 15.0 %collective-permute-start.8 = (f16[128,1152]{1,0:T(8,128)(2,1)}, f16[128,1152]{1,0:T(8,128)(2,1)}, u32[]{:S(2)}, u32[]{:S(2)}) collective-permute-start(f16[128,1152]{1,0:T(8,128)(2,1)} %get-tuple-element.13), channel_id=1, source_target_pairs={{0,32},{16,48},{32,0},{48,16},{1,33},{17,49},{33,1},{49,17},{2,34}... | collective-permute-start | bytes 884744 | tf_op jit(solution)/shard_map/ppermute | solution.py:121
  125.4 21.1 %all-to-all-start.3 = ((f16[4,128,1280]{2,1,0:T(8,128)(2,1)}), f16[4,128,1280]{2,1,0:T(8,128)(2,1)S(1)}, u32[]{:S(2)}, u32[]{:S(2)}) async-start(f16[4,128,1280]{2,1,0:T(8,128)(2,1)} %bitcast.3), calls=%async_computation.3 | async-start | bytes 2621440 | tf_op jit(solution)/shard_map/all_to_all | solution.py:156
  130.5 20.6 %collective-permute-start.10 = (f16[32,1152]{1,0:T(8,128)(2,1)S(1)}, f16[32,1152]{1,0:T(8,128)(2,1)S(1)}, u32[]{:S(2)}, u32[]{:S(2)}) collective-permute-start(f16[32,1152]{1,0:T(8,128)(2,1)S(1)} %get-tuple-element.14), channel_id=1, source_target_pairs={{0,6},{2,0},{4,2},{6,4},{1,7},{3,1},{5,3},{7,5},{8,14},{10,8},{12,... | collective-permute-start | bytes 221192 | tf_op jit(solution)/shard_map/ppermute | solution.py:121
  133.0 18.1 %collective-permute-start.12 = (f16[32,1152]{1,0:T(8,128)(2,1)S(1)}, f16[32,1152]{1,0:T(8,128)(2,1)S(1)}, u32[]{:S(2)}, u32[]{:S(2)}) collective-permute-start(f16[32,1152]{1,0:T(8,128)(2,1)S(1)} %get-tuple-element.15), channel_id=1, source_target_pairs={{0,2},{2,4},{4,6},{6,0},{1,3},{3,5},{5,7},{7,1},{8,10},{10,12},{12... | collective-permute-start | bytes 221192 | tf_op jit(solution)/shard_map/ppermute | solution.py:121
  136.4 14.7 %collective-permute-start.11 = (f16[32,1152]{1,0:T(8,128)(2,1)S(1)}, f16[32,1152]{1,0:T(8,128)(2,1)S(1)}, u32[]{:S(2)}, u32[]{:S(2)}) collective-permute-start(f16[32,1152]{1,0:T(8,128)(2,1)S(1)} %get-tuple-element.16), channel_id=1, source_target_pairs={{0,4},{2,6},{4,0},{6,2},{1,5},{3,7},{5,1},{7,3},{8,12},{10,14},{12... | collective-permute-start | bytes 221192 | tf_op jit(solution)/shard_map/ppermute | solution.py:121
  146.7 4.4 %copy-start.8 = (bf16[32,1152]{1,0:T(8,128)(2,1)S(1)}, bf16[32,1152]{1,0:T(8,128)(2,1)}, u32[]{:S(2)}) copy-start(bf16[32,1152]{1,0:T(8,128)(2,1)} %param.3) | copy-start | bytes 221188
  147.5 25.3 %copy-start.4 = (bf16[32,1152]{1,0:T(8,128)(2,1)S(1)}, bf16[32,1152]{1,0:T(8,128)(2,1)}, u32[]{:S(2)}) copy-start(bf16[32,1152]{1,0:T(8,128)(2,1)} %values_ref.1) | copy-start | bytes 221188
  147.5 24.6 %all-to-all-start.4 = ((f16[4,32,1280]{2,1,0:T(8,128)(2,1)}), f16[4,32,1280]{2,1,0:T(8,128)(2,1)S(1)}, u32[]{:S(2)}, u32[]{:S(2)}) async-start(f16[4,32,1280]{2,1,0:T(8,128)(2,1)} %bitcast.4), calls=%async_computation.4 | async-start | bytes 655360 | tf_op jit(solution)/shard_map/all_to_all | solution.py:156
  (4 other events, 5.3 us)

commit v2 on v1

--- a/solution.py
+++ b/solution.py
@@ -48,7 +48,7 @@
 def pair_kernel(own_text_ref, masked_ref, arrived_ref, *refs):
     del arrived_ref
     part_refs, (own_ref, other_ref) = refs[:SIDE], refs[SIDE : SIDE + 2]
-    coef_ref, own_sums_ref, other_sums_ref, loss_ref, group_ref = refs[SIDE + 2 :]
+    coef_ref, loss_ref, group_ref = refs[SIDE + 2 :]
     near = part_refs[0].shape[0]
     for k in range(SIDE):
         group_ref[k * near : (k + 1) * near] = part_refs[k][...]
@@ -60,7 +60,7 @@
     columns = lax.broadcasted_iota(jnp.int32, shape, 1)
     diagonal = columns - lax.broadcasted_iota(jnp.int32, shape, 0)
     loss = jnp.zeros((8, images), jnp.float32)
-    for texts_ref, sums_ref, base in ((other_ref, other_sums_ref, half), (own_ref, own_sums_ref, 0)):
+    for texts_ref, base in ((other_ref, half), (own_ref, 0)):
         for at in range(0, half, CHUNK):
             logits = TEMP * lax.dot_general(
                 texts_ref[at : at + CHUNK],
@@ -85,13 +85,8 @@
             loss = loss + jnp.sum(terms.reshape(CHUNK // 8, 8, images), axis=0)
             coef = jnp.where(valid, sigmoid, 0.0).astype(jnp.bfloat16)
             coef_ref[base + at : base + at + CHUNK] = coef
-            sums_ref[at : at + CHUNK] = jnp.dot(coef, group, preferred_element_type=jnp.float32)
     total = jnp.sum(jnp.sum(loss, axis=0, keepdims=True), axis=1, keepdims=True)
     loss_ref[...] = jnp.broadcast_to(total[None], loss_ref.shape)
-
-
-def placed(value):
-    return pltpu.with_memory_space_constraint(value, pltpu.VMEM)
 
 
 def pair_terms(own_text, masked, arrived, parts, own_texts, other_texts, peers):
@@ -101,16 +96,14 @@
     return pl.pallas_call(
         pair_kernel,
         out_shape=(
-            jax.ShapeDtypeStruct((2 * half, images), jnp.bfloat16),
-            jax.ShapeDtypeStruct((half, width), jnp.float32),
-            pltpu.VMEM((half, width), jnp.float32),
-            pltpu.VMEM((peers, 8, 128), jnp.float32),
+            pltpu.HBM((2 * half, images), jnp.bfloat16),
+            pltpu.HBM((peers, 8, 128), jnp.float32),
+            jax.ShapeDtypeStruct((images, width), jnp.bfloat16),
         ),
         in_specs=[pl.BlockSpec(memory_space=pltpu.SMEM)] + [VMEM] * (SIDE + 4),
-        out_specs=(VMEM,) * 4,
-        scratch_shapes=[pltpu.VMEM((images, width), jnp.bfloat16)],
+        out_specs=(VMEM,) * 3,
         compiler_params=pltpu.CompilerParams(vmem_limit_bytes=20 * 2**20),
-    )(own_text, *(placed(a) for a in (masked, arrived, *parts, own_texts, other_texts)))
+    )(own_text, masked, arrived, *parts, own_texts, other_texts)
 
 
 def swapped(value):
@@ -133,15 +126,26 @@
     return lax.optimization_barrier(sums)
 
 
-def to_row(total, lanes, first):
-    row = jnp.zeros(lanes.shape, jnp.float32)
-    rest = total * (1.0 / TOP)
+def digits_kernel(got_ref, row_ref):
+    rest = jnp.sum(got_ref[...], axis=0) * (1.0 / TOP)
+    lanes = lax.broadcasted_iota(jnp.int32, rest.shape, 1)
+    row = jnp.zeros(rest.shape, jnp.float32)
     for k in range(DIGITS):
         rest = rest * BASE
         digit = jnp.floor(rest)
         rest = rest - digit
-        row = jnp.where(lanes == first + k, digit, row)
-    return row
+        row = jnp.where(lanes == k, digit, row)
+    row_ref[...] = row
+
+
+def digit_row(got):
+    return pl.pallas_call(
+        digits_kernel,
+        out_shape=jax.ShapeDtypeStruct(got.shape[1:], jnp.float32),
+        in_specs=[VMEM],
+        out_specs=VMEM,
+        compiler_params=pltpu.CompilerParams(vmem_limit_bytes=4 * 2**20),
+    )(got)[:1]
 
 
 def from_row(row):
@@ -154,7 +158,10 @@
 
 def sent_and_summed(parts, axis):
     got = lax.all_to_all(parts, axis, 0, 0, tiled=True)
-    return jnp.sum(got.astype(jnp.float32), axis=0)
+    sums = got[0].astype(jnp.float32)
+    for k in range(1, SIDE):
+        sums = sums + got[k].astype(jnp.float32)
+    return sums
 
 
 def block_mask(tile_mask):
@@ -205,24 +212,23 @@
     masked = mask_rows(tile_mask, rows)
     own_text = (lax.axis_index("y") * SIDE + lax.axis_index(ZB)).reshape(1, 1)
     peers = lax.axis_size(IMAGE_GROUP)
-    coef, own_sums, other_sums, loss = pair_terms(
+    coef, loss, group = pair_terms(
         own_text, masked, arrived, parts, own_texts, other_texts, peers
     )
+    loss = lax.all_to_all(loss, IMAGE_GROUP, 0, 0, tiled=True)
+    other_sums = jnp.dot(coef[16 * rows :], group, preferred_element_type=jnp.float32)
     other_sums = swapped(other_sums)
-    loss = lax.all_to_all(loss, IMAGE_GROUP, 0, 0, tiled=True)
-    loss = jnp.sum(loss[:, 0, 0])
     image_parts = lax.dot_general(
         coef[: 16 * rows], own_texts, (((0,), (0,)), ((), ())), preferred_element_type=jnp.float32
     ) + lax.dot_general(
         coef[16 * rows :], other_texts, (((0,), (0,)), ((), ())), preferred_element_type=jnp.float32
     )
-    payload = jnp.pad((own_sums + other_sums).astype(jnp.float16), ((0, 0), (0, SPARE)))
-    payload = lax.optimization_barrier(payload)
-    lanes = lax.broadcasted_iota(jnp.int32, (1, SPARE), 1)
-    row = to_row(loss, lanes, 0).astype(jnp.float16)
-    payload = lax.dynamic_update_slice(
-        payload, jnp.broadcast_to(row, (payload.shape[0], SPARE)), (0, width)
-    )
+    own_sums = jnp.dot(coef[: 16 * rows], group, preferred_element_type=jnp.float32)
+    payload = lax.optimization_barrier((own_sums + other_sums).astype(jnp.float16))
+    row = digit_row(loss)
+    lanes = lax.broadcasted_iota(jnp.int32, (1, width + SPARE), 1)
+    row = jnp.pad(row, ((0, 0), (width, 0))).astype(jnp.float16)
+    payload = jnp.where(lanes >= width, row, jnp.pad(payload, ((0, 0), (0, SPARE))))
     text_parts = sent_and_summed(payload.reshape(SIDE, SIDE * rows, -1), "y")
     image_parts = turned_and_summed(image_parts.reshape(SIDE, SIDE * rows, width), "x")
     text_parts = text_parts.astype(jnp.float16).reshape(SIDE, rows, -1)

time: 177 us -> 181 us (1.023)
  matrix products: 4.8 us -> 11.4 us
  local copies, waits for them, and re-layouts: 7.44 us -> 10.7 us
  other arithmetic: 10.2 us -> 8.28 us
    dot_general x0 -> x2, matrix products: none -> 5.88 us  [the longest x1 3.37 us: step(): jnp.dot(coef[16 * rows:], group, preferred_element_type=jnp.float32)]
    unnamed x20 -> x34, local copies, waits for them, and re-layouts: 3.3 us -> 8.46 us
    convert_element_type x3 -> x0, other arithmetic: 2.66 us -> none  [the longest x1 1.9 us: step(): (own_sums + other_sums).astype(jnp.float16)]
    pallas_call x1 -> x2, Pallas kernels: 6.36 us -> 4.9 us  [the longest x1 3.94 us: pair_terms(): pl.pallas_call(pair_kernel, out_shape=(pltpu.HBM((2 * half, images), jnp....]
  transfers between devices with their start and end apart: 18 -> 18, of which waited for: 6 -> 5; matrix products, arithmetic and copies ran while one was open for 9% -> 9% of each run, Pallas kernels for 0% -> 1%
where the time goes in v2:
time: 181 us; the launch traced here: 180 us
  starting transfers between devices  63.8 us (35%)
  waiting for transfers between devices  40.1 us (22%)
  blocking collectives  37.1 us (20%)
  matrix products  11.4 us (6%)
  local copies, waits for them, and re-layouts  10.7 us (6%)
  other arithmetic  8.28 us (5%)
  Pallas kernels  5.02 us (3%)
  between operations  3.48 us (2%)
    ppermute x12, starting transfers between devices, turned(): lax.ppermute(value, axis, [(k, (k + steps) % SIDE) for k in range(SIDE)])  41.8 us
    all_to_all x1, blocking collectives, step(): got = lax.all_to_all(normalized_slots(texts), ZB, 0, 0, tiled=True)  37.1 us
    all_to_all x2, waiting for transfers between devices, sent_and_summed(): got = lax.all_to_all(parts, axis, 0, 0, tiled=True)  23.9 us
    ppermute x12, waiting for transfers between devices, turned(): lax.ppermute(value, axis, [(k, (k + steps) % SIDE) for k in range(SIDE)])  9.22 us
    unnamed x34, local copies, waits for them, and re-layouts  8.46 us
    all_to_all x2, starting transfers between devices, sent_and_summed(): got = lax.all_to_all(parts, axis, 0, 0, tiled=True)  7.12 us
    all_to_all x1, waiting for transfers between devices, step(): lax.all_to_all(sent, 'y', 0, 0, tiled=True).reshape(16 * rows, width)  6.95 us
    all_to_all x1, starting transfers between devices, step(): loss = lax.all_to_all(loss, IMAGE_GROUP, 0, 0, tiled=True)  6.42 us
  transfers between devices with their start and end apart: 18, of which 5 were waited for; matrix products, arithmetic and copies ran while one was open for 9% of the time, Pallas kernels for 1%

profile of v2, /device:TPU:34, one launch (start us, length us, event | category | flops | bytes accessed | tf_op | source)
XLA Modules:
  0.0 179.8 jit_solution(10021927429806837727)
XLA Ops:
  1.6 37.1 %all_to_all.25 = bf16[4,32,1152]{2,1,0:T(8,128)(2,1)S(1)} all-to-all(bf16[4,32,1152]{2,1,0:T(8,128)(2,1)S(1)} %shard_map.58), channel_id=1, replica_groups=mesh['y'=4,'zh'=2,'x'=4,'zb'=2,'za'=4,'c'=2] {'zh','zb'}, dimensions={0} | all-to-all | bytes 589824 | tf_op jit(solution)/shard_map/all_to_all | solution.py:199
  39.9 4.6 %all-to-all-start.1 = ((bf16[4,128,1152]{2,1,0:T(8,128)(2,1)}), bf16[4,128,1152]{2,1,0:T(8,128)(2,1)S(1)}, u32[]{:S(2)}, u32[]{:S(2)}) async-start(bf16[4,128,1152]{2,1,0:T(8,128)(2,1)} %broadcast_in_dim.81), calls=%async_computation.1 | async-start | bytes 2359296 | tf_op jit(solution)/shard_map/all_to_all | solution.py:209
  46.6 4.4 %collective-permute-start.1 = (bf16[32,1152]{1,0:T(8,128)(2,1)S(1)}, bf16[32,1152]{1,0:T(8,128)(2,1)S(1)}, u32[]{:S(2)}, u32[]{:S(2)}) collective-permute-start(bf16[32,1152]{1,0:T(8,128)(2,1)S(1)} %fusion.14), channel_id=1, source_target_pairs={{0,4},{2,6},{4,0},{6,2},{1,5},{3,7},{5,1},{7,3},{8,12},{10,14},{12... | collective-permute-start | bytes 221192 | tf_op jit(solution)/shard_map/ppermute | solution.py:114
  53.0 7.0 %all-to-all-done.1 = bf16[4,128,1152]{2,1,0:T(8,128)(2,1)S(1)} async-done(((bf16[4,128,1152]{2,1,0:T(8,128)(2,1)}), bf16[4,128,1152]{2,1,0:T(8,128)(2,1)S(1)}, u32[]{:S(2)}, u32[]{:S(2)}) %all-to-all-start.1) | async-done | bytes 1179680 | tf_op jit(solution)/shard_map/all_to_all | solution.py:209
  62.1 2.4 %collective-permute-start.5 = (bf16[128,1152]{1,0:T(8,128)(2,1)S(1)}, bf16[128,1152]{1,0:T(8,128)(2,1)S(1)}, u32[]{:S(2)}, u32[]{:S(2)}) collective-permute-start(bf16[128,1152]{1,0:T(8,128)(2,1)S(1)} %pad_maximum_fusion.refs_0_), channel_id=1, source_target_pairs={{0,48},{16,0},{32,16},{48,32},{1,49},{17,1},{33,17},{49,33},{2,50}... | collective-permute-start | bytes 884744 | tf_op jit(solution)/shard_map/ppermute | solution.py:114
  64.6 4.3 %collective-permute-start.4 = (bf16[128,1152]{1,0:T(8,128)(2,1)S(1)}, bf16[128,1152]{1,0:T(8,128)(2,1)S(1)}, u32[]{:S(2)}, u32[]{:S(2)}) collective-permute-start(bf16[128,1152]{1,0:T(8,128)(2,1)S(1)} %pad_maximum_fusion.refs_0_), channel_id=1, source_target_pairs={{0,32},{16,48},{32,0},{48,16},{1,33},{17,49},{33,1},{49,17},{2,34}... | collective-permute-start | bytes 884744 | tf_op jit(solution)/shard_map/ppermute | solution.py:114
  68.9 3.7 %collective-permute-start.3 = (bf16[128,1152]{1,0:T(8,128)(2,1)S(1)}, bf16[128,1152]{1,0:T(8,128)(2,1)S(1)}, u32[]{:S(2)}, u32[]{:S(2)}) collective-permute-start(bf16[128,1152]{1,0:T(8,128)(2,1)S(1)} %pad_maximum_fusion.refs_0_), channel_id=1, source_target_pairs={{0,16},{16,32},{32,48},{48,0},{1,17},{17,33},{33,49},{49,1},{2,18}... | collective-permute-start | bytes 884744 | tf_op jit(solution)/shard_map/ppermute | solution.py:114
  74.3 6.4 %collective-permute-done.4.refs_2_ = bf16[128,1152]{1,0:T(8,128)(2,1)S(1)} collective-permute-done((bf16[128,1152]{1,0:T(8,128)(2,1)S(1)}, bf16[128,1152]{1,0:T(8,128)(2,1)S(1)}, u32[]{:S(2)}, u32[]{:S(2)}) %collective-permute-start.4) | collective-permute-done | bytes 294944 | tf_op jit(solution)/shard_map/ppermute | solution.py:114
  80.7 2.8 %collective-permute-done.3.refs_1_ = bf16[128,1152]{1,0:T(8,128)(2,1)S(1)} collective-permute-done((bf16[128,1152]{1,0:T(8,128)(2,1)S(1)}, bf16[128,1152]{1,0:T(8,128)(2,1)S(1)}, u32[]{:S(2)}, u32[]{:S(2)}) %collective-permute-start.3) | collective-permute-done | bytes 294944 | tf_op jit(solution)/shard_map/ppermute | solution.py:114
  90.3 3.9 %shard_map.59 = (bf16[1024,512]{1,0:T(8,128)(2,1)}, f32[32,8,128]{2,1,0:T(8,128)}, bf16[512,1152]{1,0:T(8,128)(2,1)S(1)}) custom-call(s32[1,1]{1,0:T(1,128)} %bitcast.own_text_ref, f32[32,512]{1,0:T(8,128)S(1)} %copy-done.10, bf16[16,128]{1,0:T(8,128)(2,1)S(1)} %slice_add_fusion.2.arrived_ref, bf16[128,1152]{1,0:T(8,128)(2,1)S(1)} %copy-done.1, ...), custom_call_target="tpu_custom_call" | custom-call | tf_op jit(solution)/shard_map/pallas_call | solution.py:96
  94.3 3.4 %fusion.6 = f32[512,1152]{1,0:T(8,128)} fusion(bf16[512,1152]{1,0:T(8,128)(2,1)S(1)} %get-tuple-element.8, bf16[1024,512]{1,0:T(8,128)(2,1)} %get-tuple-element.6), kind=kOutput, calls=%fused_computation.10 | convolution fusion | flops 603979776 | bytes 4063232 | tf_op jit(solution)/shard_map/dot_general | solution.py:219
  101.9 6.4 %all-to-all-start.2 = ((f32[32,8,128]{2,1,0:T(8,128)}), f32[32,8,128]{2,1,0:T(8,128)}, u32[]{:S(2)}, u32[]{:S(2)}) async-start(f32[32,8,128]{2,1,0:T(8,128)} %get-tuple-element.7), calls=%async_computation.2 | async-start | bytes 262144 | tf_op jit(solution)/shard_map/all_to_all | solution.py:218
  110.4 2.4 %fusion.66 = (f16[512,1152]{1,0:T(8,128)(2,1)S(1)}, f32[512,1152]{1,0:T(8,128)}) fusion(f32[512,1152]{1,0:T(8,128)S(1)} %fusion.8, bf16[512,1152]{1,0:T(8,128)(2,1)S(1)} %bitcast.18, bf16[1024,512]{1,0:T(8,128)(2,1)S(1)} %copy-done.11), kind=kOutput, calls=%fused_computation.124 | convolution fusion | flops 605159424 | bytes 7602176 | tf_op jit(solution)/shard_map/dot_general | solution.py:221
  113.7 2.5 %collective-permute-start.7 = (f16[128,1152]{1,0:T(8,128)(2,1)}, f16[128,1152]{1,0:T(8,128)(2,1)}, u32[]{:S(2)}, u32[]{:S(2)}) collective-permute-start(f16[128,1152]{1,0:T(8,128)(2,1)} %get-tuple-element.9), channel_id=1, source_target_pairs={{0,48},{16,0},{32,16},{48,32},{1,49},{17,1},{33,17},{49,33},{2,50}... | collective-permute-start | bytes 884744 | tf_op jit(solution)/shard_map/ppermute | solution.py:114
  116.3 3.3 %collective-permute-start.9 = (f16[128,1152]{1,0:T(8,128)(2,1)}, f16[128,1152]{1,0:T(8,128)(2,1)}, u32[]{:S(2)}, u32[]{:S(2)}) collective-permute-start(f16[128,1152]{1,0:T(8,128)(2,1)} %get-tuple-element.10), channel_id=1, source_target_pairs={{0,16},{16,32},{32,48},{48,0},{1,17},{17,33},{33,49},{49,1},{2,18}... | collective-permute-start | bytes 884744 | tf_op jit(solution)/shard_map/ppermute | solution.py:114
  119.6 5.2 %collective-permute-start.8 = (f16[128,1152]{1,0:T(8,128)(2,1)}, f16[128,1152]{1,0:T(8,128)(2,1)}, u32[]{:S(2)}, u32[]{:S(2)}) collective-permute-start(f16[128,1152]{1,0:T(8,128)(2,1)} %get-tuple-element.11), channel_id=1, source_target_pairs={{0,32},{16,48},{32,0},{48,16},{1,33},{17,49},{33,1},{49,17},{2,34}... | collective-permute-start | bytes 884744 | tf_op jit(solution)/shard_map/ppermute | solution.py:114
  125.9 2.5 %fusion = f16[512,1152]{1,0:T(8,128)(2,1)S(1)} fusion(f32[512,1152]{1,0:T(8,128)} %collective-permute-done.13, bf16[512,1152]{1,0:T(8,128)(2,1)S(1)} %get-tuple-element.8, bf16[1024,512]{1,0:T(8,128)(2,1)S(1)} %copy-done.12), kind=kOutput, calls=%fused_computation.2 | convolution fusion | flops 605159424 | bytes 5242880 | tf_op jit(solution)/shard_map/dot_general | solution.py:226
  129.7 3.5 %all-to-all-start.3 = ((f16[4,128,1280]{2,1,0:T(8,128)(2,1)}), f16[4,128,1280]{2,1,0:T(8,128)(2,1)S(1)}, u32[]{:S(2)}, u32[]{:S(2)}) async-start(f16[4,128,1280]{2,1,0:T(8,128)(2,1)} %bitcast.19), calls=%async_computation.3 | async-start | bytes 2621440 | tf_op jit(solution)/shard_map/all_to_all | solution.py:160
  134.8 2.5 %collective-permute-start.10 = (f16[32,1152]{1,0:T(8,128)(2,1)S(1)}, f16[32,1152]{1,0:T(8,128)(2,1)S(1)}, u32[]{:S(2)}, u32[]{:S(2)}) collective-permute-start(f16[32,1152]{1,0:T(8,128)(2,1)S(1)} %get-tuple-element.12), channel_id=1, source_target_pairs={{0,6},{2,0},{4,2},{6,4},{1,7},{3,1},{5,3},{7,5},{8,14},{10,8},{12,... | collective-permute-start | bytes 221192 | tf_op jit(solution)/shard_map/ppermute | solution.py:114
  137.3 3.4 %collective-permute-start.12 = (f16[32,1152]{1,0:T(8,128)(2,1)S(1)}, f16[32,1152]{1,0:T(8,128)(2,1)S(1)}, u32[]{:S(2)}, u32[]{:S(2)}) collective-permute-start(f16[32,1152]{1,0:T(8,128)(2,1)S(1)} %get-tuple-element.13), channel_id=1, source_target_pairs={{0,2},{2,4},{4,6},{6,0},{1,3},{3,5},{5,7},{7,1},{8,10},{10,12},{12... | collective-permute-start | bytes 221192 | tf_op jit(solution)/shard_map/ppermute | solution.py:114
  140.7 6.2 %collective-permute-start.11 = (f16[32,1152]{1,0:T(8,128)(2,1)S(1)}, f16[32,1152]{1,0:T(8,128)(2,1)S(1)}, u32[]{:S(2)}, u32[]{:S(2)}) collective-permute-start(f16[32,1152]{1,0:T(8,128)(2,1)S(1)} %get-tuple-element.14), channel_id=1, source_target_pairs={{0,4},{2,6},{4,0},{6,2},{1,5},{3,7},{5,1},{7,3},{8,12},{10,14},{12... | collective-permute-start | bytes 221192 | tf_op jit(solution)/shard_map/ppermute | solution.py:114
  146.9 3.9 %all-to-all-done.3 = f16[4,128,1280]{2,1,0:T(8,128)(2,1)S(1)} async-done(((f16[4,128,1280]{2,1,0:T(8,128)(2,1)}), f16[4,128,1280]{2,1,0:T(8,128)(2,1)S(1)}, u32[]{:S(2)}, u32[]{:S(2)}) %all-to-all-start.3) | async-done | bytes 1310752 | tf_op jit(solution)/shard_map/all_to_all | solution.py:160
  151.8 3.6 %all-to-all-start.4 = ((f16[4,32,1280]{2,1,0:T(8,128)(2,1)}), f16[4,32,1280]{2,1,0:T(8,128)(2,1)S(1)}, u32[]{:S(2)}, u32[]{:S(2)}) async-start(f16[4,32,1280]{2,1,0:T(8,128)(2,1)} %bitcast.4), calls=%async_computation.4 | async-start | bytes 655360 | tf_op jit(solution)/shard_map/all_to_all | solution.py:160
  156.4 20.0 %all-to-all-done.4 = f16[4,32,1280]{2,1,0:T(8,128)(2,1)S(1)} async-done(((f16[4,32,1280]{2,1,0:T(8,128)(2,1)}), f16[4,32,1280]{2,1,0:T(8,128)(2,1)S(1)}, u32[]{:S(2)}, u32[]{:S(2)}) %all-to-all-start.4) | async-done | bytes 327712 | tf_op jit(solution)/shard_map/all_to_all | solution.py:160
  (85 shorter events, 30.8 us)
Async XLA Ops:
  39.9 4.6 %copy-start.13 = (bf16[32,1152]{1,0:T(8,128)(2,1)S(1)}, bf16[32,1152]{1,0:T(8,128)(2,1)}, u32[]{:S(2)}) copy-start(bf16[32,1152]{1,0:T(8,128)(2,1)} %param.3) | copy-start | bytes 221188
  39.9 22.0 %copy-start.15 = (s32[128,128]{1,0:T(8,128)S(1)}, s32[128,128]{1,0:T(8,128)}, u32[]{:S(2)}) copy-start(s32[128,128]{1,0:T(8,128)} %param.5) | copy-start | bytes 196612
  39.9 20.0 %all-to-all-start.1 = ((bf16[4,128,1152]{2,1,0:T(8,128)(2,1)}), bf16[4,128,1152]{2,1,0:T(8,128)(2,1)S(1)}, u32[]{:S(2)}, u32[]{:S(2)}) async-start(bf16[4,128,1152]{2,1,0:T(8,128)(2,1)} %broadcast_in_dim.81), calls=%async_computation.1 | async-start | bytes 2359296 | tf_op jit(solution)/shard_map/all_to_all | solution.py:209
  44.7 17.4 %collective-permute-start.2 = (bf16[32,1152]{1,0:T(8,128)(2,1)S(1)}, bf16[32,1152]{1,0:T(8,128)(2,1)S(1)}, u32[]{:S(2)}, u32[]{:S(2)}) collective-permute-start(bf16[32,1152]{1,0:T(8,128)(2,1)S(1)} %fusion.14), channel_id=1, source_target_pairs={{0,6},{2,0},{4,2},{6,4},{1,7},{3,1},{5,3},{7,5},{8,14},{10,8},{12,... | collective-permute-start | bytes 221192 | tf_op jit(solution)/shard_map/ppermute | solution.py:114
  46.6 15.4 %collective-permute-start.1 = (bf16[32,1152]{1,0:T(8,128)(2,1)S(1)}, bf16[32,1152]{1,0:T(8,128)(2,1)S(1)}, u32[]{:S(2)}, u32[]{:S(2)}) collective-permute-start(bf16[32,1152]{1,0:T(8,128)(2,1)S(1)} %fusion.14), channel_id=1, source_target_pairs={{0,4},{2,6},{4,0},{6,2},{1,5},{3,7},{5,1},{7,3},{8,12},{10,14},{12... | collective-permute-start | bytes 221192 | tf_op jit(solution)/shard_map/ppermute | solution.py:114
  51.0 11.1 %collective-permute-start = (bf16[32,1152]{1,0:T(8,128)(2,1)S(1)}, bf16[32,1152]{1,0:T(8,128)(2,1)S(1)}, u32[]{:S(2)}, u32[]{:S(2)}) collective-permute-start(bf16[32,1152]{1,0:T(8,128)(2,1)S(1)} %fusion.14), channel_id=1, source_target_pairs={{0,2},{2,4},{4,6},{6,0},{1,3},{3,5},{5,7},{7,1},{8,10},{10,12},{12... | collective-permute-start | bytes 221192 | tf_op jit(solution)/shard_map/ppermute | solution.py:114
  59.9 25.7 %collective-permute-start.6 = (bf16[512,1152]{1,0:T(8,128)(2,1)S(1)}, bf16[512,1152]{1,0:T(8,128)(2,1)S(1)}, u32[]{:S(2)}, u32[]{:S(2)}) collective-permute-start(bf16[512,1152]{1,0:T(8,128)(2,1)S(1)} %bitcast.16), channel_id=1, source_target_pairs={{0,1},{1,0},{2,3},{3,2},{4,5},{5,4},{6,7},{7,6},{8,9},{9,8},{10,11... | collective-permute-start | bytes 3538952 | tf_op jit(solution)/shard_map/ppermute | solution.py:110
  62.1 12.2 %collective-permute-start.5 = (bf16[128,1152]{1,0:T(8,128)(2,1)S(1)}, bf16[128,1152]{1,0:T(8,128)(2,1)S(1)}, u32[]{:S(2)}, u32[]{:S(2)}) collective-permute-start(bf16[128,1152]{1,0:T(8,128)(2,1)S(1)} %pad_maximum_fusion.refs_0_), channel_id=1, source_target_pairs={{0,48},{16,0},{32,16},{48,32},{1,49},{17,1},{33,17},{49,33},{2,50}... | collective-permute-start | bytes 884744 | tf_op jit(solution)/shard_map/ppermute | solution.py:114
  64.6 16.1 %collective-permute-start.4 = (bf16[128,1152]{1,0:T(8,128)(2,1)S(1)}, bf16[128,1152]{1,0:T(8,128)(2,1)S(1)}, u32[]{:S(2)}, u32[]{:S(2)}) collective-permute-start(bf16[128,1152]{1,0:T(8,128)(2,1)S(1)} %pad_maximum_fusion.refs_0_), channel_id=1, source_target_pairs={{0,32},{16,48},{32,0},{48,16},{1,33},{17,49},{33,1},{49,17},{2,34}... | collective-permute-start | bytes 884744 | tf_op jit(solution)/shard_map/ppermute | solution.py:114
  68.9 14.6 %collective-permute-start.3 = (bf16[128,1152]{1,0:T(8,128)(2,1)S(1)}, bf16[128,1152]{1,0:T(8,128)(2,1)S(1)}, u32[]{:S(2)}, u32[]{:S(2)}) collective-permute-start(bf16[128,1152]{1,0:T(8,128)(2,1)S(1)} %pad_maximum_fusion.refs_0_), channel_id=1, source_target_pairs={{0,16},{16,32},{32,48},{48,0},{1,17},{17,33},{33,49},{49,1},{2,18}... | collective-permute-start | bytes 884744 | tf_op jit(solution)/shard_map/ppermute | solution.py:114
  94.3 5.3 %copy-start.16 = (s32[128,128]{1,0:T(8,128)S(1)}, s32[128,128]{1,0:T(8,128)}, u32[]{:S(2)}) copy-start(s32[128,128]{1,0:T(8,128)} %param.5) | copy-start | bytes 196612
  97.7 28.2 %collective-permute-start.13 = (f32[512,1152]{1,0:T(8,128)}, f32[512,1152]{1,0:T(8,128)}, u32[]{:S(2)}, u32[]{:S(2)}) collective-permute-start(f32[512,1152]{1,0:T(8,128)} %fusion.6), channel_id=1, source_target_pairs={{0,1},{1,0},{2,3},{3,2},{4,5},{5,4},{6,7},{7,6},{8,9},{9,8},{10,11... | collective-permute-start | bytes 7077896 | tf_op jit(solution)/shard_map/ppermute | solution.py:110
  101.9 22.9 %all-to-all-start.2 = ((f32[32,8,128]{2,1,0:T(8,128)}), f32[32,8,128]{2,1,0:T(8,128)}, u32[]{:S(2)}, u32[]{:S(2)}) async-start(f32[32,8,128]{2,1,0:T(8,128)} %get-tuple-element.7), calls=%async_computation.2 | async-start | bytes 262144 | tf_op jit(solution)/shard_map/all_to_all | solution.py:218
  112.7 13.1 %copy-start.12 = (bf16[1024,512]{1,0:T(8,128)(2,1)S(1)}, bf16[1024,512]{1,0:T(8,128)(2,1)}, u32[]{:S(2)}) copy-start(bf16[1024,512]{1,0:T(8,128)(2,1)} %get-tuple-element.6) | copy-start | bytes 3145732
  113.7 19.5 %collective-permute-start.7 = (f16[128,1152]{1,0:T(8,128)(2,1)}, f16[128,1152]{1,0:T(8,128)(2,1)}, u32[]{:S(2)}, u32[]{:S(2)}) collective-permute-start(f16[128,1152]{1,0:T(8,128)(2,1)} %get-tuple-element.9), channel_id=1, source_target_pairs={{0,48},{16,0},{32,16},{48,32},{1,49},{17,1},{33,17},{49,33},{2,50}... | collective-permute-start | bytes 884744 | tf_op jit(solution)/shard_map/ppermute | solution.py:114
  116.3 17.0 %collective-permute-start.9 = (f16[128,1152]{1,0:T(8,128)(2,1)}, f16[128,1152]{1,0:T(8,128)(2,1)}, u32[]{:S(2)}, u32[]{:S(2)}) collective-permute-start(f16[128,1152]{1,0:T(8,128)(2,1)} %get-tuple-element.10), channel_id=1, source_target_pairs={{0,16},{16,32},{32,48},{48,0},{1,17},{17,33},{33,49},{49,1},{2,18}... | collective-permute-start | bytes 884744 | tf_op jit(solution)/shard_map/ppermute | solution.py:114
  119.6 13.7 %collective-permute-start.8 = (f16[128,1152]{1,0:T(8,128)(2,1)}, f16[128,1152]{1,0:T(8,128)(2,1)}, u32[]{:S(2)}, u32[]{:S(2)}) collective-permute-start(f16[128,1152]{1,0:T(8,128)(2,1)} %get-tuple-element.11), channel_id=1, source_target_pairs={{0,32},{16,48},{32,0},{48,16},{1,33},{17,49},{33,1},{49,17},{2,34}... | collective-permute-start | bytes 884744 | tf_op jit(solution)/shard_map/ppermute | solution.py:114
  129.7 21.1 %all-to-all-start.3 = ((f16[4,128,1280]{2,1,0:T(8,128)(2,1)}), f16[4,128,1280]{2,1,0:T(8,128)(2,1)S(1)}, u32[]{:S(2)}, u32[]{:S(2)}) async-start(f16[4,128,1280]{2,1,0:T(8,128)(2,1)} %bitcast.19), calls=%async_computation.3 | async-start | bytes 2621440 | tf_op jit(solution)/shard_map/all_to_all | solution.py:160
  134.8 20.5 %collective-permute-start.10 = (f16[32,1152]{1,0:T(8,128)(2,1)S(1)}, f16[32,1152]{1,0:T(8,128)(2,1)S(1)}, u32[]{:S(2)}, u32[]{:S(2)}) collective-permute-start(f16[32,1152]{1,0:T(8,128)(2,1)S(1)} %get-tuple-element.12), channel_id=1, source_target_pairs={{0,6},{2,0},{4,2},{6,4},{1,7},{3,1},{5,3},{7,5},{8,14},{10,8},{12,... | collective-permute-start | bytes 221192 | tf_op jit(solution)/shard_map/ppermute | solution.py:114
  137.3 18.1 %collective-permute-start.12 = (f16[32,1152]{1,0:T(8,128)(2,1)S(1)}, f16[32,1152]{1,0:T(8,128)(2,1)S(1)}, u32[]{:S(2)}, u32[]{:S(2)}) collective-permute-start(f16[32,1152]{1,0:T(8,128)(2,1)S(1)} %get-tuple-element.13), channel_id=1, source_target_pairs={{0,2},{2,4},{4,6},{6,0},{1,3},{3,5},{5,7},{7,1},{8,10},{10,12},{12... | collective-permute-start | bytes 221192 | tf_op jit(solution)/shard_map/ppermute | solution.py:114
  140.7 14.7 %copy-start.14 = (bf16[32,1152]{1,0:T(8,128)(2,1)S(1)}, bf16[32,1152]{1,0:T(8,128)(2,1)}, u32[]{:S(2)}) copy-start(bf16[32,1152]{1,0:T(8,128)(2,1)} %param.3) | copy-start | bytes 221188
  140.7 14.7 %collective-permute-start.11 = (f16[32,1152]{1,0:T(8,128)(2,1)S(1)}, f16[32,1152]{1,0:T(8,128)(2,1)S(1)}, u32[]{:S(2)}, u32[]{:S(2)}) collective-permute-start(f16[32,1152]{1,0:T(8,128)(2,1)S(1)} %get-tuple-element.14), channel_id=1, source_target_pairs={{0,4},{2,6},{4,0},{6,2},{1,5},{3,7},{5,1},{7,3},{8,12},{10,14},{12... | collective-permute-start | bytes 221192 | tf_op jit(solution)/shard_map/ppermute | solution.py:114
  151.8 25.3 %copy-start.3 = (bf16[32,1152]{1,0:T(8,128)(2,1)S(1)}, bf16[32,1152]{1,0:T(8,128)(2,1)}, u32[]{:S(2)}) copy-start(bf16[32,1152]{1,0:T(8,128)(2,1)} %values_ref.1) | copy-start | bytes 221188
  151.8 24.6 %all-to-all-start.4 = ((f16[4,32,1280]{2,1,0:T(8,128)(2,1)}), f16[4,32,1280]{2,1,0:T(8,128)(2,1)S(1)}, u32[]{:S(2)}, u32[]{:S(2)}) async-start(f16[4,32,1280]{2,1,0:T(8,128)(2,1)} %bitcast.4), calls=%async_computation.4 | async-start | bytes 655360 | tf_op jit(solution)/shard_map/all_to_all | solution.py:160
  (11 other events, 10.5 us)

commit v3 on v2

--- a/solution.py
+++ b/solution.py
@@ -22,6 +22,7 @@
 CHUNK = 256
 
 VMEM = pl.BlockSpec(memory_space=pltpu.VMEM)
+HBM = pl.BlockSpec(memory_space=pltpu.HBM)
 
 
 def inverse_norm(values):
@@ -45,13 +46,19 @@
     )(values)
 
 
-def pair_kernel(own_text_ref, masked_ref, arrived_ref, *refs):
-    del arrived_ref
+def pair_kernel(own_text_ref, masked_hbm_ref, *refs):
     part_refs, (own_ref, other_ref) = refs[:SIDE], refs[SIDE : SIDE + 2]
-    coef_ref, loss_ref, group_ref = refs[SIDE + 2 :]
+    coef_ref, loss_ref, group_ref, masked_ref, arrived = refs[SIDE + 2 :]
     near = part_refs[0].shape[0]
-    for k in range(SIDE):
-        group_ref[k * near : (k + 1) * near] = part_refs[k][...]
+    copies = [
+        pltpu.make_async_copy(part_refs[k], group_ref.at[pl.ds(k * near, near)], arrived.at[k])
+        for k in range(SIDE)
+    ]
+    copies.append(pltpu.make_async_copy(masked_hbm_ref, masked_ref, arrived.at[SIDE]))
+    for copy in copies:
+        copy.start()
+    for copy in copies:
+        copy.wait()
     group = group_ref[...]
     images, _ = group.shape
     half = own_ref.shape[0]
@@ -89,7 +96,11 @@
     loss_ref[...] = jnp.broadcast_to(total[None], loss_ref.shape)
 
 
-def pair_terms(own_text, masked, arrived, parts, own_texts, other_texts, peers):
+def held(value):
+    return pltpu.with_memory_space_constraint(value, pltpu.HBM)
+
+
+def pair_terms(own_text, masked, parts, own_texts, other_texts, peers):
     near, width = parts[0].shape
     half = own_texts.shape[0]
     images = SIDE * near
@@ -100,10 +111,14 @@
             pltpu.HBM((peers, 8, 128), jnp.float32),
             jax.ShapeDtypeStruct((images, width), jnp.bfloat16),
         ),
-        in_specs=[pl.BlockSpec(memory_space=pltpu.SMEM)] + [VMEM] * (SIDE + 4),
+        in_specs=[pl.BlockSpec(memory_space=pltpu.SMEM)] + [HBM] * (SIDE + 1) + [VMEM] * 2,
         out_specs=(VMEM,) * 3,
+        scratch_shapes=[
+            pltpu.VMEM(masked.shape, jnp.float32),
+            pltpu.SemaphoreType.DMA((SIDE + 1,)),
+        ],
         compiler_params=pltpu.CompilerParams(vmem_limit_bytes=20 * 2**20),
-    )(own_text, masked, arrived, *parts, own_texts, other_texts)
+    )(own_text, *(held(a) for a in (masked, *parts)), own_texts, other_texts)
 
 
 def swapped(value):
@@ -208,12 +223,11 @@
     sent = jnp.broadcast_to(got.reshape(1, SIDE * rows, width), (SIDE, SIDE * rows, width))
     own_texts = lax.all_to_all(sent, "y", 0, 0, tiled=True).reshape(16 * rows, width)
     other_texts = swapped(own_texts)
-    arrived = parts[1][:16, :128] + parts[2][:16, :128] + parts[3][:16, :128]
     masked = mask_rows(tile_mask, rows)
     own_text = (lax.axis_index("y") * SIDE + lax.axis_index(ZB)).reshape(1, 1)
     peers = lax.axis_size(IMAGE_GROUP)
     coef, loss, group = pair_terms(
-        own_text, masked, arrived, parts, own_texts, other_texts, peers
+        own_text, masked, parts, own_texts, other_texts, peers
     )
     loss = lax.all_to_all(loss, IMAGE_GROUP, 0, 0, tiled=True)
     other_sums = jnp.dot(coef[16 * rows :], group, preferred_element_type=jnp.float32)

time: 181 us -> 190 us (1.050)
  waiting for transfers between devices: 40.1 us -> 51.5 us
  local copies, waits for them, and re-layouts: 10.7 us -> 3.81 us
  starting transfers between devices: 63.8 us -> 66.6 us
    all_to_all x1, waiting for transfers between devices: 6.95 us -> 15.3 us  [step(): lax.all_to_all(sent, 'y', 0, 0, tiled=True).reshape(16 * rows, width)]
    unnamed x34 -> x24, local copies, waits for them, and re-layouts: 8.46 us -> 1.6 us
    ppermute x12, waiting for transfers between devices: 9.22 us -> 12.2 us  [turned(): lax.ppermute(value, axis, [(k, (k + steps) % SIDE) for k in range(SIDE)])]
    all_to_all x1, starting transfers between devices: 6.42 us -> 9.21 us  [step(): loss = lax.all_to_all(loss, IMAGE_GROUP, 0, 0, tiled=True)]
  transfers between devices with their start and end apart: 18 -> 18, of which waited for: 5 -> 7; matrix products, arithmetic and copies ran while one was open for 9% -> 8% of each run, Pallas kernels for 1% -> 1%
where the time goes in v3:
time: 190 us; the launch traced here: 188 us
  starting transfers between devices  66.6 us (35%)
  waiting for transfers between devices  51.5 us (27%)
  blocking collectives  37.1 us (20%)
  matrix products  11.3 us (6%)
  other arithmetic  8.29 us (4%)
  Pallas kernels  6.26 us (3%)
  local copies, waits for them, and re-layouts  3.81 us (2%)
  between operations  3.47 us (2%)
    ppermute x12, starting transfers between devices, turned(): lax.ppermute(value, axis, [(k, (k + steps) % SIDE) for k in range(SIDE)])  41.9 us
    all_to_all x1, blocking collectives, step(): got = lax.all_to_all(normalized_slots(texts), ZB, 0, 0, tiled=True)  37.1 us
    all_to_all x2, waiting for transfers between devices, sent_and_summed(): got = lax.all_to_all(parts, axis, 0, 0, tiled=True)  23.9 us
    all_to_all x1, waiting for transfers between devices, step(): lax.all_to_all(sent, 'y', 0, 0, tiled=True).reshape(16 * rows, width)  15.3 us
    ppermute x12, waiting for transfers between devices, turned(): lax.ppermute(value, axis, [(k, (k + steps) % SIDE) for k in range(SIDE)])  12.2 us
    all_to_all x1, starting transfers between devices, step(): loss = lax.all_to_all(loss, IMAGE_GROUP, 0, 0, tiled=True)  9.21 us
    all_to_all x2, starting transfers between devices, sent_and_summed(): got = lax.all_to_all(parts, axis, 0, 0, tiled=True)  7.12 us
    pallas_call x1, Pallas kernels, pair_terms(): pl.pallas_call(pair_kernel, out_shape=(pltpu.HBM((2 * half, images), jnp....  5.18 us
  transfers between devices with their start and end apart: 18, of which 7 were waited for; matrix products, arithmetic and copies ran while one was open for 8% of the time, Pallas kernels for 1%

profile of v3, /device:TPU:34, one launch (start us, length us, event | category | flops | bytes accessed | tf_op | source)
XLA Modules:
  0.0 188.4 jit_solution(806066399222840641)
XLA Ops:
  1.6 37.1 %all_to_all.25 = bf16[4,32,1152]{2,1,0:T(8,128)(2,1)S(1)} all-to-all(bf16[4,32,1152]{2,1,0:T(8,128)(2,1)S(1)} %shard_map.58), channel_id=1, replica_groups=mesh['y'=4,'zh'=2,'x'=4,'zb'=2,'za'=4,'c'=2] {'zh','zb'}, dimensions={0} | all-to-all | bytes 589824 | tf_op jit(solution)/shard_map/all_to_all | solution.py:214
  39.9 4.6 %all-to-all-start.1 = ((bf16[4,128,1152]{2,1,0:T(8,128)(2,1)}), bf16[4,128,1152]{2,1,0:T(8,128)(2,1)S(1)}, u32[]{:S(2)}, u32[]{:S(2)}) async-start(bf16[4,128,1152]{2,1,0:T(8,128)(2,1)} %broadcast_in_dim.81), calls=%async_computation.1 | async-start | bytes 2359296 | tf_op jit(solution)/shard_map/all_to_all | solution.py:224
  44.6 15.3 %all-to-all-done.1 = bf16[4,128,1152]{2,1,0:T(8,128)(2,1)S(1)} async-done(((bf16[4,128,1152]{2,1,0:T(8,128)(2,1)}), bf16[4,128,1152]{2,1,0:T(8,128)(2,1)S(1)}, u32[]{:S(2)}, u32[]{:S(2)}) %all-to-all-start.1) | async-done | bytes 1179680 | tf_op jit(solution)/shard_map/all_to_all | solution.py:224
  63.8 4.4 %collective-permute-start.1 = (bf16[32,1152]{1,0:T(8,128)(2,1)S(1)}, bf16[32,1152]{1,0:T(8,128)(2,1)S(1)}, u32[]{:S(2)}, u32[]{:S(2)}) collective-permute-start(bf16[32,1152]{1,0:T(8,128)(2,1)S(1)} %fusion.14), channel_id=1, source_target_pairs={{0,4},{2,6},{4,0},{6,2},{1,5},{3,7},{5,1},{7,3},{8,12},{10,14},{12... | collective-permute-start | bytes 221192 | tf_op jit(solution)/shard_map/ppermute | solution.py:129
  74.5 2.4 %collective-permute-start.5 = (bf16[128,1152]{1,0:T(8,128)(2,1)S(1)}, bf16[128,1152]{1,0:T(8,128)(2,1)S(1)}, u32[]{:S(2)}, u32[]{:S(2)}) collective-permute-start(bf16[128,1152]{1,0:T(8,128)(2,1)S(1)} %pad_maximum_fusion.refs_0_), channel_id=1, source_target_pairs={{0,48},{16,0},{32,16},{48,32},{1,49},{17,1},{33,17},{49,33},{2,50}... | collective-permute-start | bytes 884744 | tf_op jit(solution)/shard_map/ppermute | solution.py:129
  76.9 4.3 %collective-permute-start.4 = (bf16[128,1152]{1,0:T(8,128)(2,1)S(1)}, bf16[128,1152]{1,0:T(8,128)(2,1)S(1)}, u32[]{:S(2)}, u32[]{:S(2)}) collective-permute-start(bf16[128,1152]{1,0:T(8,128)(2,1)S(1)} %pad_maximum_fusion.refs_0_), channel_id=1, source_target_pairs={{0,32},{16,48},{32,0},{48,16},{1,33},{17,49},{33,1},{49,17},{2,34}... | collective-permute-start | bytes 884744 | tf_op jit(solution)/shard_map/ppermute | solution.py:129
  81.3 3.7 %collective-permute-start.3 = (bf16[128,1152]{1,0:T(8,128)(2,1)S(1)}, bf16[128,1152]{1,0:T(8,128)(2,1)S(1)}, u32[]{:S(2)}, u32[]{:S(2)}) collective-permute-start(bf16[128,1152]{1,0:T(8,128)(2,1)S(1)} %pad_maximum_fusion.refs_0_), channel_id=1, source_target_pairs={{0,16},{16,32},{32,48},{48,0},{1,17},{17,33},{33,49},{49,1},{2,18}... | collective-permute-start | bytes 884744 | tf_op jit(solution)/shard_map/ppermute | solution.py:129
  86.0 5.4 %collective-permute-done.4.refs_2_ = bf16[128,1152]{1,0:T(8,128)(2,1)S(1)} collective-permute-done((bf16[128,1152]{1,0:T(8,128)(2,1)S(1)}, bf16[128,1152]{1,0:T(8,128)(2,1)S(1)}, u32[]{:S(2)}, u32[]{:S(2)}) %collective-permute-start.4) | collective-permute-done | bytes 294944 | tf_op jit(solution)/shard_map/ppermute | solution.py:129
  91.3 2.8 %collective-permute-done.3.refs_1_ = bf16[128,1152]{1,0:T(8,128)(2,1)S(1)} collective-permute-done((bf16[128,1152]{1,0:T(8,128)(2,1)S(1)}, bf16[128,1152]{1,0:T(8,128)(2,1)S(1)}, u32[]{:S(2)}, u32[]{:S(2)}) %collective-permute-start.3) | collective-permute-done | bytes 294944 | tf_op jit(solution)/shard_map/ppermute | solution.py:129
  94.8 5.2 %shard_map.59 = (bf16[1024,512]{1,0:T(8,128)(2,1)}, f32[32,8,128]{2,1,0:T(8,128)}, bf16[512,1152]{1,0:T(8,128)(2,1)S(1)}) custom-call(s32[1,1]{1,0:T(1,128)} %bitcast.own_text_ref, f32[32,512]{1,0:T(8,128)} %fusion.1.masked_hbm_ref, bf16[128,1152]{1,0:T(8,128)(2,1)} %copy-done.6, bf16[128,1152]{1,0:T(8,128)(2,1)} %copy-done.9, bf16[128,1152]{1,0:T(8,128)(2,1)} %copy-done.8, ...), custom_call_target="tpu_custom_call" | custom-call | tf_op jit(solution)/shard_map/pallas_call | solution.py:107
  100.0 3.4 %fusion.6 = f32[512,1152]{1,0:T(8,128)} fusion(bf16[512,1152]{1,0:T(8,128)(2,1)S(1)} %get-tuple-element.8, bf16[1024,512]{1,0:T(8,128)(2,1)} %get-tuple-element.6), kind=kOutput, calls=%fused_computation.10 | convolution fusion | flops 603979776 | bytes 4063232 | tf_op jit(solution)/shard_map/dot_general | solution.py:233
  107.7 9.2 %all-to-all-start.2 = ((f32[32,8,128]{2,1,0:T(8,128)}), f32[32,8,128]{2,1,0:T(8,128)}, u32[]{:S(2)}, u32[]{:S(2)}) async-start(f32[32,8,128]{2,1,0:T(8,128)} %get-tuple-element.7), calls=%async_computation.2 | async-start | bytes 262144 | tf_op jit(solution)/shard_map/all_to_all | solution.py:232
  118.9 2.3 %fusion.66 = (f16[512,1152]{1,0:T(8,128)(2,1)S(1)}, f32[512,1152]{1,0:T(8,128)}) fusion(f32[512,1152]{1,0:T(8,128)S(1)} %fusion.8, bf16[512,1152]{1,0:T(8,128)(2,1)S(1)} %bitcast.18, bf16[1024,512]{1,0:T(8,128)(2,1)S(1)} %copy-done.2), kind=kOutput, calls=%fused_computation.122 | convolution fusion | flops 605159424 | bytes 7602176 | tf_op jit(solution)/shard_map/dot_general | solution.py:235
  122.2 2.4 %collective-permute-start.7 = (f16[128,1152]{1,0:T(8,128)(2,1)}, f16[128,1152]{1,0:T(8,128)(2,1)}, u32[]{:S(2)}, u32[]{:S(2)}) collective-permute-start(f16[128,1152]{1,0:T(8,128)(2,1)} %get-tuple-element.9), channel_id=1, source_target_pairs={{0,48},{16,0},{32,16},{48,32},{1,49},{17,1},{33,17},{49,33},{2,50}... | collective-permute-start | bytes 884744 | tf_op jit(solution)/shard_map/ppermute | solution.py:129
  124.7 3.4 %collective-permute-start.9 = (f16[128,1152]{1,0:T(8,128)(2,1)}, f16[128,1152]{1,0:T(8,128)(2,1)}, u32[]{:S(2)}, u32[]{:S(2)}) collective-permute-start(f16[128,1152]{1,0:T(8,128)(2,1)} %get-tuple-element.10), channel_id=1, source_target_pairs={{0,16},{16,32},{32,48},{48,0},{1,17},{17,33},{33,49},{49,1},{2,18}... | collective-permute-start | bytes 884744 | tf_op jit(solution)/shard_map/ppermute | solution.py:129
  128.1 5.3 %collective-permute-start.8 = (f16[128,1152]{1,0:T(8,128)(2,1)}, f16[128,1152]{1,0:T(8,128)(2,1)}, u32[]{:S(2)}, u32[]{:S(2)}) collective-permute-start(f16[128,1152]{1,0:T(8,128)(2,1)} %get-tuple-element.11), channel_id=1, source_target_pairs={{0,32},{16,48},{32,0},{48,16},{1,33},{17,49},{33,1},{49,17},{2,34}... | collective-permute-start | bytes 884744 | tf_op jit(solution)/shard_map/ppermute | solution.py:129
  134.4 2.5 %fusion = f16[512,1152]{1,0:T(8,128)(2,1)S(1)} fusion(f32[512,1152]{1,0:T(8,128)} %collective-permute-done.13, bf16[512,1152]{1,0:T(8,128)(2,1)S(1)} %get-tuple-element.8, bf16[1024,512]{1,0:T(8,128)(2,1)S(1)} %copy-done.3), kind=kOutput, calls=%fused_computation.2 | convolution fusion | flops 605159424 | bytes 5242880 | tf_op jit(solution)/shard_map/dot_general | solution.py:240
  138.3 3.5 %all-to-all-start.3 = ((f16[4,128,1280]{2,1,0:T(8,128)(2,1)}), f16[4,128,1280]{2,1,0:T(8,128)(2,1)S(1)}, u32[]{:S(2)}, u32[]{:S(2)}) async-start(f16[4,128,1280]{2,1,0:T(8,128)(2,1)} %bitcast.19), calls=%async_computation.3 | async-start | bytes 2621440 | tf_op jit(solution)/shard_map/all_to_all | solution.py:175
  143.4 2.5 %collective-permute-start.10 = (f16[32,1152]{1,0:T(8,128)(2,1)S(1)}, f16[32,1152]{1,0:T(8,128)(2,1)S(1)}, u32[]{:S(2)}, u32[]{:S(2)}) collective-permute-start(f16[32,1152]{1,0:T(8,128)(2,1)S(1)} %get-tuple-element.12), channel_id=1, source_target_pairs={{0,6},{2,0},{4,2},{6,4},{1,7},{3,1},{5,3},{7,5},{8,14},{10,8},{12,... | collective-permute-start | bytes 221192 | tf_op jit(solution)/shard_map/ppermute | solution.py:129
  145.9 3.4 %collective-permute-start.12 = (f16[32,1152]{1,0:T(8,128)(2,1)S(1)}, f16[32,1152]{1,0:T(8,128)(2,1)S(1)}, u32[]{:S(2)}, u32[]{:S(2)}) collective-permute-start(f16[32,1152]{1,0:T(8,128)(2,1)S(1)} %get-tuple-element.13), channel_id=1, source_target_pairs={{0,2},{2,4},{4,6},{6,0},{1,3},{3,5},{5,7},{7,1},{8,10},{10,12},{12... | collective-permute-start | bytes 221192 | tf_op jit(solution)/shard_map/ppermute | solution.py:129
  149.3 6.2 %collective-permute-start.11 = (f16[32,1152]{1,0:T(8,128)(2,1)S(1)}, f16[32,1152]{1,0:T(8,128)(2,1)S(1)}, u32[]{:S(2)}, u32[]{:S(2)}) collective-permute-start(f16[32,1152]{1,0:T(8,128)(2,1)S(1)} %get-tuple-element.14), channel_id=1, source_target_pairs={{0,4},{2,6},{4,0},{6,2},{1,5},{3,7},{5,1},{7,3},{8,12},{10,14},{12... | collective-permute-start | bytes 221192 | tf_op jit(solution)/shard_map/ppermute | solution.py:129
  155.5 3.9 %all-to-all-done.3 = f16[4,128,1280]{2,1,0:T(8,128)(2,1)S(1)} async-done(((f16[4,128,1280]{2,1,0:T(8,128)(2,1)}), f16[4,128,1280]{2,1,0:T(8,128)(2,1)S(1)}, u32[]{:S(2)}, u32[]{:S(2)}) %all-to-all-start.3) | async-done | bytes 1310752 | tf_op jit(solution)/shard_map/all_to_all | solution.py:175
  160.4 3.6 %all-to-all-start.4 = ((f16[4,32,1280]{2,1,0:T(8,128)(2,1)}), f16[4,32,1280]{2,1,0:T(8,128)(2,1)S(1)}, u32[]{:S(2)}, u32[]{:S(2)}) async-start(f16[4,32,1280]{2,1,0:T(8,128)(2,1)} %bitcast.4), calls=%async_computation.4 | async-start | bytes 655360 | tf_op jit(solution)/shard_map/all_to_all | solution.py:175
  165.0 20.0 %all-to-all-done.4 = f16[4,32,1280]{2,1,0:T(8,128)(2,1)S(1)} async-done(((f16[4,32,1280]{2,1,0:T(8,128)(2,1)}), f16[4,32,1280]{2,1,0:T(8,128)(2,1)S(1)}, u32[]{:S(2)}, u32[]{:S(2)}) %all-to-all-start.4) | async-done | bytes 327712 | tf_op jit(solution)/shard_map/all_to_all | solution.py:175
  (74 shorter events, 28.1 us)
Async XLA Ops:
  39.9 30.3 %copy-start.10 = (s32[128,128]{1,0:T(8,128)S(1)}, s32[128,128]{1,0:T(8,128)}, u32[]{:S(2)}) copy-start(s32[128,128]{1,0:T(8,128)} %param.5) | copy-start | bytes 196612
  39.9 20.0 %all-to-all-start.1 = ((bf16[4,128,1152]{2,1,0:T(8,128)(2,1)}), bf16[4,128,1152]{2,1,0:T(8,128)(2,1)S(1)}, u32[]{:S(2)}, u32[]{:S(2)}) async-start(bf16[4,128,1152]{2,1,0:T(8,128)(2,1)} %broadcast_in_dim.81), calls=%async_computation.1 | async-start | bytes 2359296 | tf_op jit(solution)/shard_map/all_to_all | solution.py:224
  59.9 34.2 %collective-permute-start.6 = (bf16[512,1152]{1,0:T(8,128)(2,1)S(1)}, bf16[512,1152]{1,0:T(8,128)(2,1)S(1)}, u32[]{:S(2)}, u32[]{:S(2)}) collective-permute-start(bf16[512,1152]{1,0:T(8,128)(2,1)S(1)} %bitcast.16), channel_id=1, source_target_pairs={{0,1},{1,0},{2,3},{3,2},{4,5},{5,4},{6,7},{7,6},{8,9},{9,8},{10,11... | collective-permute-start | bytes 3538952 | tf_op jit(solution)/shard_map/ppermute | solution.py:125
  61.9 8.5 %collective-permute-start.2 = (bf16[32,1152]{1,0:T(8,128)(2,1)S(1)}, bf16[32,1152]{1,0:T(8,128)(2,1)S(1)}, u32[]{:S(2)}, u32[]{:S(2)}) collective-permute-start(bf16[32,1152]{1,0:T(8,128)(2,1)S(1)} %fusion.14), channel_id=1, source_target_pairs={{0,6},{2,0},{4,2},{6,4},{1,7},{3,1},{5,3},{7,5},{8,14},{10,8},{12,... | collective-permute-start | bytes 221192 | tf_op jit(solution)/shard_map/ppermute | solution.py:129
  63.8 8.4 %collective-permute-start.1 = (bf16[32,1152]{1,0:T(8,128)(2,1)S(1)}, bf16[32,1152]{1,0:T(8,128)(2,1)S(1)}, u32[]{:S(2)}, u32[]{:S(2)}) collective-permute-start(bf16[32,1152]{1,0:T(8,128)(2,1)S(1)} %fusion.14), channel_id=1, source_target_pairs={{0,4},{2,6},{4,0},{6,2},{1,5},{3,7},{5,1},{7,3},{8,12},{10,14},{12... | collective-permute-start | bytes 221192 | tf_op jit(solution)/shard_map/ppermute | solution.py:129
  68.2 6.2 %collective-permute-start = (bf16[32,1152]{1,0:T(8,128)(2,1)S(1)}, bf16[32,1152]{1,0:T(8,128)(2,1)S(1)}, u32[]{:S(2)}, u32[]{:S(2)}) collective-permute-start(bf16[32,1152]{1,0:T(8,128)(2,1)S(1)} %fusion.14), channel_id=1, source_target_pairs={{0,2},{2,4},{4,6},{6,0},{1,3},{3,5},{5,7},{7,1},{8,10},{10,12},{12... | collective-permute-start | bytes 221192 | tf_op jit(solution)/shard_map/ppermute | solution.py:129
  74.5 19.6 %copy-start.6 = (bf16[128,1152]{1,0:T(8,128)(2,1)}, bf16[128,1152]{1,0:T(8,128)(2,1)S(1)}, u32[]{:S(2)}) copy-start(bf16[128,1152]{1,0:T(8,128)(2,1)S(1)} %pad_maximum_fusion.refs_0_) | copy-start | bytes 884740
  74.5 11.5 %collective-permute-start.5 = (bf16[128,1152]{1,0:T(8,128)(2,1)S(1)}, bf16[128,1152]{1,0:T(8,128)(2,1)S(1)}, u32[]{:S(2)}, u32[]{:S(2)}) collective-permute-start(bf16[128,1152]{1,0:T(8,128)(2,1)S(1)} %pad_maximum_fusion.refs_0_), channel_id=1, source_target_pairs={{0,48},{16,0},{32,16},{48,32},{1,49},{17,1},{33,17},{49,33},{2,50}... | collective-permute-start | bytes 884744 | tf_op jit(solution)/shard_map/ppermute | solution.py:129
  76.9 14.4 %collective-permute-start.4 = (bf16[128,1152]{1,0:T(8,128)(2,1)S(1)}, bf16[128,1152]{1,0:T(8,128)(2,1)S(1)}, u32[]{:S(2)}, u32[]{:S(2)}) collective-permute-start(bf16[128,1152]{1,0:T(8,128)(2,1)S(1)} %pad_maximum_fusion.refs_0_), channel_id=1, source_target_pairs={{0,32},{16,48},{32,0},{48,16},{1,33},{17,49},{33,1},{49,17},{2,34}... | collective-permute-start | bytes 884744 | tf_op jit(solution)/shard_map/ppermute | solution.py:129
  81.3 12.8 %collective-permute-start.3 = (bf16[128,1152]{1,0:T(8,128)(2,1)S(1)}, bf16[128,1152]{1,0:T(8,128)(2,1)S(1)}, u32[]{:S(2)}, u32[]{:S(2)}) collective-permute-start(bf16[128,1152]{1,0:T(8,128)(2,1)S(1)} %pad_maximum_fusion.refs_0_), channel_id=1, source_target_pairs={{0,16},{16,32},{32,48},{48,0},{1,17},{17,33},{33,49},{49,1},{2,18}... | collective-permute-start | bytes 884744 | tf_op jit(solution)/shard_map/ppermute | solution.py:129
  86.0 8.2 %copy-start.7 = (bf16[128,1152]{1,0:T(8,128)(2,1)}, bf16[128,1152]{1,0:T(8,128)(2,1)S(1)}, u32[]{:S(2)}) copy-start(bf16[128,1152]{1,0:T(8,128)(2,1)S(1)} %collective-permute-done.5.refs_3_) | copy-start | bytes 884740
  103.4 31.0 %collective-permute-start.13 = (f32[512,1152]{1,0:T(8,128)}, f32[512,1152]{1,0:T(8,128)}, u32[]{:S(2)}, u32[]{:S(2)}) collective-permute-start(f32[512,1152]{1,0:T(8,128)} %fusion.6), channel_id=1, source_target_pairs={{0,1},{1,0},{2,3},{3,2},{4,5},{5,4},{6,7},{7,6},{8,9},{9,8},{10,11... | collective-permute-start | bytes 7077896 | tf_op jit(solution)/shard_map/ppermute | solution.py:125
  107.7 25.7 %all-to-all-start.2 = ((f32[32,8,128]{2,1,0:T(8,128)}), f32[32,8,128]{2,1,0:T(8,128)}, u32[]{:S(2)}, u32[]{:S(2)}) async-start(f32[32,8,128]{2,1,0:T(8,128)} %get-tuple-element.7), calls=%async_computation.2 | async-start | bytes 262144 | tf_op jit(solution)/shard_map/all_to_all | solution.py:232
  121.2 13.2 %copy-start.3 = (bf16[1024,512]{1,0:T(8,128)(2,1)S(1)}, bf16[1024,512]{1,0:T(8,128)(2,1)}, u32[]{:S(2)}) copy-start(bf16[1024,512]{1,0:T(8,128)(2,1)} %get-tuple-element.6) | copy-start | bytes 3145732
  122.2 19.6 %collective-permute-start.7 = (f16[128,1152]{1,0:T(8,128)(2,1)}, f16[128,1152]{1,0:T(8,128)(2,1)}, u32[]{:S(2)}, u32[]{:S(2)}) collective-permute-start(f16[128,1152]{1,0:T(8,128)(2,1)} %get-tuple-element.9), channel_id=1, source_target_pairs={{0,48},{16,0},{32,16},{48,32},{1,49},{17,1},{33,17},{49,33},{2,50}... | collective-permute-start | bytes 884744 | tf_op jit(solution)/shard_map/ppermute | solution.py:129
  124.7 17.2 %collective-permute-start.9 = (f16[128,1152]{1,0:T(8,128)(2,1)}, f16[128,1152]{1,0:T(8,128)(2,1)}, u32[]{:S(2)}, u32[]{:S(2)}) collective-permute-start(f16[128,1152]{1,0:T(8,128)(2,1)} %get-tuple-element.10), channel_id=1, source_target_pairs={{0,16},{16,32},{32,48},{48,0},{1,17},{17,33},{33,49},{49,1},{2,18}... | collective-permute-start | bytes 884744 | tf_op jit(solution)/shard_map/ppermute | solution.py:129
  128.1 13.8 %collective-permute-start.8 = (f16[128,1152]{1,0:T(8,128)(2,1)}, f16[128,1152]{1,0:T(8,128)(2,1)}, u32[]{:S(2)}, u32[]{:S(2)}) collective-permute-start(f16[128,1152]{1,0:T(8,128)(2,1)} %get-tuple-element.11), channel_id=1, source_target_pairs={{0,32},{16,48},{32,0},{48,16},{1,33},{17,49},{33,1},{49,17},{2,34}... | collective-permute-start | bytes 884744 | tf_op jit(solution)/shard_map/ppermute | solution.py:129
  138.3 21.1 %all-to-all-start.3 = ((f16[4,128,1280]{2,1,0:T(8,128)(2,1)}), f16[4,128,1280]{2,1,0:T(8,128)(2,1)S(1)}, u32[]{:S(2)}, u32[]{:S(2)}) async-start(f16[4,128,1280]{2,1,0:T(8,128)(2,1)} %bitcast.19), calls=%async_computation.3 | async-start | bytes 2621440 | tf_op jit(solution)/shard_map/all_to_all | solution.py:175
  143.4 20.5 %collective-permute-start.10 = (f16[32,1152]{1,0:T(8,128)(2,1)S(1)}, f16[32,1152]{1,0:T(8,128)(2,1)S(1)}, u32[]{:S(2)}, u32[]{:S(2)}) collective-permute-start(f16[32,1152]{1,0:T(8,128)(2,1)S(1)} %get-tuple-element.12), channel_id=1, source_target_pairs={{0,6},{2,0},{4,2},{6,4},{1,7},{3,1},{5,3},{7,5},{8,14},{10,8},{12,... | collective-permute-start | bytes 221192 | tf_op jit(solution)/shard_map/ppermute | solution.py:129
  145.9 18.1 %collective-permute-start.12 = (f16[32,1152]{1,0:T(8,128)(2,1)S(1)}, f16[32,1152]{1,0:T(8,128)(2,1)S(1)}, u32[]{:S(2)}, u32[]{:S(2)}) collective-permute-start(f16[32,1152]{1,0:T(8,128)(2,1)S(1)} %get-tuple-element.13), channel_id=1, source_target_pairs={{0,2},{2,4},{4,6},{6,0},{1,3},{3,5},{5,7},{7,1},{8,10},{10,12},{12... | collective-permute-start | bytes 221192 | tf_op jit(solution)/shard_map/ppermute | solution.py:129
  149.3 14.7 %copy-start.5 = (bf16[32,1152]{1,0:T(8,128)(2,1)S(1)}, bf16[32,1152]{1,0:T(8,128)(2,1)}, u32[]{:S(2)}) copy-start(bf16[32,1152]{1,0:T(8,128)(2,1)} %param.3) | copy-start | bytes 221188
  149.3 14.7 %collective-permute-start.11 = (f16[32,1152]{1,0:T(8,128)(2,1)S(1)}, f16[32,1152]{1,0:T(8,128)(2,1)S(1)}, u32[]{:S(2)}, u32[]{:S(2)}) collective-permute-start(f16[32,1152]{1,0:T(8,128)(2,1)S(1)} %get-tuple-element.14), channel_id=1, source_target_pairs={{0,4},{2,6},{4,0},{6,2},{1,5},{3,7},{5,1},{7,3},{8,12},{10,14},{12... | collective-permute-start | bytes 221192 | tf_op jit(solution)/shard_map/ppermute | solution.py:129
  160.4 25.3 %copy-start.1 = (bf16[32,1152]{1,0:T(8,128)(2,1)S(1)}, bf16[32,1152]{1,0:T(8,128)(2,1)}, u32[]{:S(2)}) copy-start(bf16[32,1152]{1,0:T(8,128)(2,1)} %values_ref.1) | copy-start | bytes 221188
  160.4 24.6 %all-to-all-start.4 = ((f16[4,32,1280]{2,1,0:T(8,128)(2,1)}), f16[4,32,1280]{2,1,0:T(8,128)(2,1)S(1)}, u32[]{:S(2)}, u32[]{:S(2)}) async-start(f16[4,32,1280]{2,1,0:T(8,128)(2,1)} %bitcast.4), calls=%async_computation.4 | async-start | bytes 655360 | tf_op jit(solution)/shard_map/all_to_all | solution.py:175
  (6 other events, 16.3 us)

commit v4 on v3

--- a/solution.py
+++ b/solution.py
@@ -29,21 +29,42 @@
     return lax.rsqrt(jnp.sum(values * values, axis=-1, keepdims=True) + EPS)
 
 
-def slots_kernel(values_ref, slots_ref):
-    values = values_ref[...].astype(jnp.float32)
-    unit = (values * inverse_norm(values)).astype(jnp.bfloat16)
+def held(value):
+    return pltpu.with_memory_space_constraint(value, pltpu.HBM)
+
+
+def slots_kernel(texts_hbm_ref, images_hbm_ref, slots_ref, images_ref, fetched_ref, arrived):
+    copies = [
+        pltpu.make_async_copy(source, fetched_ref.at[k], arrived.at[k])
+        for k, source in enumerate((texts_hbm_ref, images_hbm_ref))
+    ]
+    for copy in copies:
+        copy.start()
+    units = []
+    for k, copy in enumerate(copies):
+        copy.wait()
+        values = fetched_ref[k].astype(jnp.float32)
+        units.append((values * inverse_norm(values)).astype(jnp.bfloat16))
     for k in range(SIDE):
-        slots_ref[k] = unit
-
-
-def normalized_slots(values):
+        slots_ref[k] = units[0]
+    images_ref[...] = units[1]
+
+
+def normalized(texts, images):
     return pl.pallas_call(
         slots_kernel,
-        out_shape=pltpu.VMEM((SIDE, *values.shape), jnp.bfloat16),
-        in_specs=[VMEM],
-        out_specs=VMEM,
+        out_shape=(
+            jax.ShapeDtypeStruct((SIDE, *texts.shape), jnp.bfloat16),
+            jax.ShapeDtypeStruct(images.shape, jnp.bfloat16),
+        ),
+        in_specs=[HBM] * 2,
+        out_specs=(VMEM,) * 2,
+        scratch_shapes=[
+            pltpu.VMEM((2, *texts.shape), jnp.bfloat16),
+            pltpu.SemaphoreType.DMA((2,)),
+        ],
         compiler_params=pltpu.CompilerParams(vmem_limit_bytes=4 * 2**20),
-    )(values)
+    )(held(texts), held(images))
 
 
 def pair_kernel(own_text_ref, masked_hbm_ref, *refs):
@@ -96,10 +117,6 @@
     loss_ref[...] = jnp.broadcast_to(total[None], loss_ref.shape)
 
 
-def held(value):
-    return pltpu.with_memory_space_constraint(value, pltpu.HBM)
-
-
 def pair_terms(own_text, masked, parts, own_texts, other_texts, peers):
     near, width = parts[0].shape
     half = own_texts.shape[0]
@@ -211,12 +228,12 @@
 
 def step(images, texts, tile_mask):
     rows, width = images.shape
-    got = lax.all_to_all(normalized_slots(texts), ZB, 0, 0, tiled=True)
+    slots, image_bf = normalized(texts, images)
+    got = lax.all_to_all(slots, ZB, 0, 0, tiled=True)
     images = images.astype(jnp.float32)
     texts = texts.astype(jnp.float32)
     image_inverse = inverse_norm(images)
     text_inverse = inverse_norm(texts)
-    image_bf = (images * image_inverse).astype(jnp.bfloat16)
     near = all_turned(image_bf, "za")
     near = jnp.concatenate(near, axis=0)
     parts = all_turned(near, "x")

time: 190 us -> 176 us (0.926)
  waiting for transfers between devices: 51.5 us -> 41.2 us
  starting transfers between devices: 66.6 us -> 63.9 us
  local copies, waits for them, and re-layouts: 3.81 us -> 1.43 us
    all_to_all x1, waiting for transfers between devices: 15.3 us -> 7.16 us  [step(): lax.all_to_all(sent, 'y', 0, 0, tiled=True).reshape(16 * rows, width)]
    all_to_all x1, starting transfers between devices: 9.21 us -> 6.43 us  [step(): loss = lax.all_to_all(loss, IMAGE_GROUP, 0, 0, tiled=True)]
    ppermute x12, waiting for transfers between devices: 12.2 us -> 10 us  [turned(): lax.ppermute(value, axis, [(k, (k + steps) % SIDE) for k in range(SIDE)])]
  transfers between devices with their start and end apart: 18 -> 18, of which waited for: 7 -> 5; matrix products, arithmetic and copies ran while one was open for 8% -> 9% of each run, Pallas kernels for 1% -> 1%
where the time goes in v4:
time: 176 us; the launch traced here: 175 us
  starting transfers between devices  63.9 us (36%)
  waiting for transfers between devices  41.2 us (23%)
  blocking collectives  37.1 us (21%)
  matrix products  11.3 us (6%)
  other arithmetic  8.98 us (5%)
  Pallas kernels  7.27 us (4%)
  between operations  3.5 us (2%)
    ppermute x12, starting transfers between devices, turned(): lax.ppermute(value, axis, [(k, (k + steps) % SIDE) for k in range(SIDE)])  42 us
    all_to_all x1, blocking collectives, step(): got = lax.all_to_all(slots, ZB, 0, 0, tiled=True)  37.1 us
    all_to_all x2, waiting for transfers between devices, sent_and_summed(): got = lax.all_to_all(parts, axis, 0, 0, tiled=True)  24 us
    ppermute x12, waiting for transfers between devices, turned(): lax.ppermute(value, axis, [(k, (k + steps) % SIDE) for k in range(SIDE)])  10 us
    all_to_all x1, waiting for transfers between devices, step(): lax.all_to_all(sent, 'y', 0, 0, tiled=True).reshape(16 * rows, width)  7.16 us
    all_to_all x2, starting transfers between devices, sent_and_summed(): got = lax.all_to_all(parts, axis, 0, 0, tiled=True)  7.12 us
    all_to_all x1, starting transfers between devices, step(): loss = lax.all_to_all(loss, IMAGE_GROUP, 0, 0, tiled=True)  6.43 us
    pallas_call x1, Pallas kernels, pair_terms(): pl.pallas_call(pair_kernel, out_shape=(pltpu.HBM((2 * half, images), jnp....  5.18 us
  transfers between devices with their start and end apart: 18, of which 5 were waited for; matrix products, arithmetic and copies ran while one was open for 9% of the time, Pallas kernels for 1%

profile of v4, /device:TPU:34, one launch (start us, length us, event | category | flops | bytes accessed | tf_op | source)
XLA Modules:
  0.0 174.8 jit_solution(11832917244812434285)
XLA Ops:
  1.8 37.1 %all_to_all.25 = bf16[4,32,1152]{2,1,0:T(8,128)(2,1)S(1)} all-to-all(bf16[4,32,1152]{2,1,0:T(8,128)(2,1)S(1)} %get-tuple-element.9), channel_id=1, replica_groups=mesh['y'=4,'zh'=2,'x'=4,'zb'=2,'za'=4,'c'=2] {'zh','zb'}, dimensions={0} | all-to-all | bytes 589824 | tf_op jit(solution)/shard_map/all_to_all | solution.py:232
  40.0 4.6 %all-to-all-start.1 = ((bf16[4,128,1152]{2,1,0:T(8,128)(2,1)}), bf16[4,128,1152]{2,1,0:T(8,128)(2,1)S(1)}, u32[]{:S(2)}, u32[]{:S(2)}) async-start(bf16[4,128,1152]{2,1,0:T(8,128)(2,1)} %broadcast_in_dim.81), calls=%async_computation.1 | async-start | bytes 2359296 | tf_op jit(solution)/shard_map/all_to_all | solution.py:241
  46.5 4.4 %collective-permute-start.1 = (bf16[32,1152]{1,0:T(8,128)(2,1)S(1)}, bf16[32,1152]{1,0:T(8,128)(2,1)S(1)}, u32[]{:S(2)}, u32[]{:S(2)}) collective-permute-start(bf16[32,1152]{1,0:T(8,128)(2,1)S(1)} %get-tuple-element.8), channel_id=1, source_target_pairs={{0,4},{2,6},{4,0},{6,2},{1,5},{3,7},{5,1},{7,3},{8,12},{10,14},{12... | collective-permute-start | bytes 221192 | tf_op jit(solution)/shard_map/ppermute | solution.py:146
  52.9 7.2 %all-to-all-done.1 = bf16[4,128,1152]{2,1,0:T(8,128)(2,1)S(1)} async-done(((bf16[4,128,1152]{2,1,0:T(8,128)(2,1)}), bf16[4,128,1152]{2,1,0:T(8,128)(2,1)S(1)}, u32[]{:S(2)}, u32[]{:S(2)}) %all-to-all-start.1) | async-done | bytes 1179680 | tf_op jit(solution)/shard_map/all_to_all | solution.py:241
  62.2 2.4 %collective-permute-start.5 = (bf16[128,1152]{1,0:T(8,128)(2,1)S(1)}, bf16[128,1152]{1,0:T(8,128)(2,1)S(1)}, u32[]{:S(2)}, u32[]{:S(2)}) collective-permute-start(bf16[128,1152]{1,0:T(8,128)(2,1)S(1)} %constant_dynamic-update-slice_fusion.refs_0_), channel_id=1, source_target_pairs={{0,48},{16,0},{32,16},{48,32},{1,49},{17,1},{33,17},{49,33},{2,50}... | collective-permute-start | bytes 884744 | tf_op jit(solution)/shard_map/ppermute | solution.py:146
  64.7 4.3 %collective-permute-start.4 = (bf16[128,1152]{1,0:T(8,128)(2,1)S(1)}, bf16[128,1152]{1,0:T(8,128)(2,1)S(1)}, u32[]{:S(2)}, u32[]{:S(2)}) collective-permute-start(bf16[128,1152]{1,0:T(8,128)(2,1)S(1)} %constant_dynamic-update-slice_fusion.refs_0_), channel_id=1, source_target_pairs={{0,32},{16,48},{32,0},{48,16},{1,33},{17,49},{33,1},{49,17},{2,34}... | collective-permute-start | bytes 884744 | tf_op jit(solution)/shard_map/ppermute | solution.py:146
  69.0 3.7 %collective-permute-start.3 = (bf16[128,1152]{1,0:T(8,128)(2,1)S(1)}, bf16[128,1152]{1,0:T(8,128)(2,1)}, u32[]{:S(2)}, u32[]{:S(2)}) collective-permute-start(bf16[128,1152]{1,0:T(8,128)(2,1)S(1)} %constant_dynamic-update-slice_fusion.refs_0_), channel_id=1, source_target_pairs={{0,16},{16,32},{32,48},{48,0},{1,17},{17,33},{33,49},{49,1},{2,18}... | collective-permute-start | bytes 884744 | tf_op jit(solution)/shard_map/ppermute | solution.py:146
  73.7 7.1 %collective-permute-done.4.refs_2_ = bf16[128,1152]{1,0:T(8,128)(2,1)S(1)} collective-permute-done((bf16[128,1152]{1,0:T(8,128)(2,1)S(1)}, bf16[128,1152]{1,0:T(8,128)(2,1)S(1)}, u32[]{:S(2)}, u32[]{:S(2)}) %collective-permute-start.4) | collective-permute-done | bytes 294944 | tf_op jit(solution)/shard_map/ppermute | solution.py:146
  80.8 2.9 %collective-permute-done.3.refs_1_ = bf16[128,1152]{1,0:T(8,128)(2,1)} collective-permute-done((bf16[128,1152]{1,0:T(8,128)(2,1)S(1)}, bf16[128,1152]{1,0:T(8,128)(2,1)}, u32[]{:S(2)}, u32[]{:S(2)}) %collective-permute-start.3) | collective-permute-done | bytes 294944 | tf_op jit(solution)/shard_map/ppermute | solution.py:146
  83.7 5.2 %shard_map.59 = (bf16[1024,512]{1,0:T(8,128)(2,1)}, f32[32,8,128]{2,1,0:T(8,128)}, bf16[512,1152]{1,0:T(8,128)(2,1)S(1)}) custom-call(s32[1,1]{1,0:T(1,128)} %bitcast.own_text_ref, f32[32,512]{1,0:T(8,128)} %fusion.1.masked_hbm_ref, bf16[128,1152]{1,0:T(8,128)(2,1)} %copy-done.4, bf16[128,1152]{1,0:T(8,128)(2,1)} %collective-permute-done.3.refs_1_, ...), custom_call_target="tpu_custom_call" | custom-call | tf_op jit(solution)/shard_map/pallas_call | solution.py:124
  88.9 3.4 %fusion.6 = f32[512,1152]{1,0:T(8,128)} fusion(bf16[512,1152]{1,0:T(8,128)(2,1)S(1)} %get-tuple-element.12, bf16[1024,512]{1,0:T(8,128)(2,1)} %get-tuple-element.10), kind=kOutput, calls=%fused_computation.10 | convolution fusion | flops 603979776 | bytes 4063232 | tf_op jit(solution)/shard_map/dot_general | solution.py:250
  97.6 6.4 %all-to-all-start.2 = ((f32[32,8,128]{2,1,0:T(8,128)}), f32[32,8,128]{2,1,0:T(8,128)}, u32[]{:S(2)}, u32[]{:S(2)}) async-start(f32[32,8,128]{2,1,0:T(8,128)} %get-tuple-element.11), calls=%async_computation.2 | async-start | bytes 262144 | tf_op jit(solution)/shard_map/all_to_all | solution.py:249
  106.1 2.3 %fusion.65 = (f16[512,1152]{1,0:T(8,128)(2,1)S(1)}, f32[512,1152]{1,0:T(8,128)}) fusion(f32[512,1152]{1,0:T(8,128)S(1)} %fusion.8, bf16[512,1152]{1,0:T(8,128)(2,1)S(1)} %bitcast.18, bf16[1024,512]{1,0:T(8,128)(2,1)S(1)} %copy-done), kind=kOutput, calls=%fused_computation.124 | convolution fusion | flops 605159424 | bytes 7602176 | tf_op jit(solution)/shard_map/dot_general | solution.py:252
  108.5 2.7 %collective-permute-start.7 = (f16[128,1152]{1,0:T(8,128)(2,1)S(1)}, f16[128,1152]{1,0:T(8,128)(2,1)S(1)}, u32[]{:S(2)}, u32[]{:S(2)}) collective-permute-start(f16[128,1152]{1,0:T(8,128)(2,1)S(1)} %get-tuple-element.13), channel_id=1, source_target_pairs={{0,48},{16,0},{32,16},{48,32},{1,49},{17,1},{33,17},{49,33},{2,50}... | collective-permute-start | bytes 884744 | tf_op jit(solution)/shard_map/ppermute | solution.py:146
  111.2 3.3 %collective-permute-start.9 = (f16[128,1152]{1,0:T(8,128)(2,1)S(1)}, f16[128,1152]{1,0:T(8,128)(2,1)}, u32[]{:S(2)}, u32[]{:S(2)}) collective-permute-start(f16[128,1152]{1,0:T(8,128)(2,1)S(1)} %get-tuple-element.14), channel_id=1, source_target_pairs={{0,16},{16,32},{32,48},{48,0},{1,17},{17,33},{33,49},{49,1},{2,18}... | collective-permute-start | bytes 884744 | tf_op jit(solution)/shard_map/ppermute | solution.py:146
  114.5 5.2 %collective-permute-start.8 = (f16[128,1152]{1,0:T(8,128)(2,1)S(1)}, f16[128,1152]{1,0:T(8,128)(2,1)}, u32[]{:S(2)}, u32[]{:S(2)}) collective-permute-start(f16[128,1152]{1,0:T(8,128)(2,1)S(1)} %get-tuple-element.15), channel_id=1, source_target_pairs={{0,32},{16,48},{32,0},{48,16},{1,33},{17,49},{33,1},{49,17},{2,34}... | collective-permute-start | bytes 884744 | tf_op jit(solution)/shard_map/ppermute | solution.py:146
  120.8 2.5 %fusion = f16[512,1152]{1,0:T(8,128)(2,1)S(1)} fusion(f32[512,1152]{1,0:T(8,128)} %collective-permute-done.13, bf16[512,1152]{1,0:T(8,128)(2,1)S(1)} %get-tuple-element.12, bf16[1024,512]{1,0:T(8,128)(2,1)S(1)} %copy-done.1), kind=kOutput, calls=%fused_computation.2 | convolution fusion | flops 605159424 | bytes 5242880 | tf_op jit(solution)/shard_map/dot_general | solution.py:257
  124.7 3.5 %all-to-all-start.3 = ((f16[4,128,1280]{2,1,0:T(8,128)(2,1)}), f16[4,128,1280]{2,1,0:T(8,128)(2,1)S(1)}, u32[]{:S(2)}, u32[]{:S(2)}) async-start(f16[4,128,1280]{2,1,0:T(8,128)(2,1)} %bitcast.3), calls=%async_computation.3 | async-start | bytes 2621440 | tf_op jit(solution)/shard_map/all_to_all | solution.py:192
  129.7 2.5 %collective-permute-start.10 = (f16[32,1152]{1,0:T(8,128)(2,1)S(1)}, f16[32,1152]{1,0:T(8,128)(2,1)S(1)}, u32[]{:S(2)}, u32[]{:S(2)}) collective-permute-start(f16[32,1152]{1,0:T(8,128)(2,1)S(1)} %get-tuple-element.16), channel_id=1, source_target_pairs={{0,6},{2,0},{4,2},{6,4},{1,7},{3,1},{5,3},{7,5},{8,14},{10,8},{12,... | collective-permute-start | bytes 221192 | tf_op jit(solution)/shard_map/ppermute | solution.py:146
  132.2 3.4 %collective-permute-start.12 = (f16[32,1152]{1,0:T(8,128)(2,1)S(1)}, f16[32,1152]{1,0:T(8,128)(2,1)S(1)}, u32[]{:S(2)}, u32[]{:S(2)}) collective-permute-start(f16[32,1152]{1,0:T(8,128)(2,1)S(1)} %get-tuple-element.17), channel_id=1, source_target_pairs={{0,2},{2,4},{4,6},{6,0},{1,3},{3,5},{5,7},{7,1},{8,10},{10,12},{12... | collective-permute-start | bytes 221192 | tf_op jit(solution)/shard_map/ppermute | solution.py:146
  135.6 6.2 %collective-permute-start.11 = (f16[32,1152]{1,0:T(8,128)(2,1)S(1)}, f16[32,1152]{1,0:T(8,128)(2,1)S(1)}, u32[]{:S(2)}, u32[]{:S(2)}) collective-permute-start(f16[32,1152]{1,0:T(8,128)(2,1)S(1)} %get-tuple-element.18), channel_id=1, source_target_pairs={{0,4},{2,6},{4,0},{6,2},{1,5},{3,7},{5,1},{7,3},{8,12},{10,14},{12... | collective-permute-start | bytes 221192 | tf_op jit(solution)/shard_map/ppermute | solution.py:146
  141.8 4.0 %all-to-all-done.3 = f16[4,128,1280]{2,1,0:T(8,128)(2,1)S(1)} async-done(((f16[4,128,1280]{2,1,0:T(8,128)(2,1)}), f16[4,128,1280]{2,1,0:T(8,128)(2,1)S(1)}, u32[]{:S(2)}, u32[]{:S(2)}) %all-to-all-start.3) | async-done | bytes 1310752 | tf_op jit(solution)/shard_map/all_to_all | solution.py:192
  146.8 3.6 %all-to-all-start.4 = ((f16[4,32,1280]{2,1,0:T(8,128)(2,1)}), f16[4,32,1280]{2,1,0:T(8,128)(2,1)S(1)}, u32[]{:S(2)}, u32[]{:S(2)}) async-start(f16[4,32,1280]{2,1,0:T(8,128)(2,1)} %bitcast.4), calls=%async_computation.4 | async-start | bytes 655360 | tf_op jit(solution)/shard_map/all_to_all | solution.py:192
  151.4 20.0 %all-to-all-done.4 = f16[4,32,1280]{2,1,0:T(8,128)(2,1)S(1)} async-done(((f16[4,32,1280]{2,1,0:T(8,128)(2,1)}), f16[4,32,1280]{2,1,0:T(8,128)(2,1)S(1)}, u32[]{:S(2)}, u32[]{:S(2)}) %all-to-all-start.4) | async-done | bytes 327712 | tf_op jit(solution)/shard_map/all_to_all | solution.py:192
  (70 shorter events, 23.3 us)
Async XLA Ops:
  40.0 22.0 %copy-start.7 = (s32[128,128]{1,0:T(8,128)S(1)}, s32[128,128]{1,0:T(8,128)}, u32[]{:S(2)}) copy-start(s32[128,128]{1,0:T(8,128)} %param.5) | copy-start | bytes 196612
  40.0 20.0 %all-to-all-start.1 = ((bf16[4,128,1152]{2,1,0:T(8,128)(2,1)}), bf16[4,128,1152]{2,1,0:T(8,128)(2,1)S(1)}, u32[]{:S(2)}, u32[]{:S(2)}) async-start(bf16[4,128,1152]{2,1,0:T(8,128)(2,1)} %broadcast_in_dim.81), calls=%async_computation.1 | async-start | bytes 2359296 | tf_op jit(solution)/shard_map/all_to_all | solution.py:241
  44.6 17.6 %collective-permute-start.2 = (bf16[32,1152]{1,0:T(8,128)(2,1)S(1)}, bf16[32,1152]{1,0:T(8,128)(2,1)S(1)}, u32[]{:S(2)}, u32[]{:S(2)}) collective-permute-start(bf16[32,1152]{1,0:T(8,128)(2,1)S(1)} %get-tuple-element.8), channel_id=1, source_target_pairs={{0,6},{2,0},{4,2},{6,4},{1,7},{3,1},{5,3},{7,5},{8,14},{10,8},{12,... | collective-permute-start | bytes 221192 | tf_op jit(solution)/shard_map/ppermute | solution.py:146
  46.5 15.7 %collective-permute-start.1 = (bf16[32,1152]{1,0:T(8,128)(2,1)S(1)}, bf16[32,1152]{1,0:T(8,128)(2,1)S(1)}, u32[]{:S(2)}, u32[]{:S(2)}) collective-permute-start(bf16[32,1152]{1,0:T(8,128)(2,1)S(1)} %get-tuple-element.8), channel_id=1, source_target_pairs={{0,4},{2,6},{4,0},{6,2},{1,5},{3,7},{5,1},{7,3},{8,12},{10,14},{12... | collective-permute-start | bytes 221192 | tf_op jit(solution)/shard_map/ppermute | solution.py:146
  50.9 11.3 %collective-permute-start = (bf16[32,1152]{1,0:T(8,128)(2,1)S(1)}, bf16[32,1152]{1,0:T(8,128)(2,1)S(1)}, u32[]{:S(2)}, u32[]{:S(2)}) collective-permute-start(bf16[32,1152]{1,0:T(8,128)(2,1)S(1)} %get-tuple-element.8), channel_id=1, source_target_pairs={{0,2},{2,4},{4,6},{6,0},{1,3},{3,5},{5,7},{7,1},{8,10},{10,12},{12... | collective-permute-start | bytes 221192 | tf_op jit(solution)/shard_map/ppermute | solution.py:146
  60.0 23.7 %collective-permute-start.6 = (bf16[512,1152]{1,0:T(8,128)(2,1)S(1)}, bf16[512,1152]{1,0:T(8,128)(2,1)S(1)}, u32[]{:S(2)}, u32[]{:S(2)}) collective-permute-start(bf16[512,1152]{1,0:T(8,128)(2,1)S(1)} %bitcast.16), channel_id=1, source_target_pairs={{0,1},{1,0},{2,3},{3,2},{4,5},{5,4},{6,7},{7,6},{8,9},{9,8},{10,11... | collective-permute-start | bytes 3538952 | tf_op jit(solution)/shard_map/ppermute | solution.py:142
  62.2 21.5 %copy-start.4 = (bf16[128,1152]{1,0:T(8,128)(2,1)}, bf16[128,1152]{1,0:T(8,128)(2,1)S(1)}, u32[]{:S(2)}) copy-start(bf16[128,1152]{1,0:T(8,128)(2,1)S(1)} %constant_dynamic-update-slice_fusion.refs_0_) | copy-start | bytes 884740
  62.2 11.5 %collective-permute-start.5 = (bf16[128,1152]{1,0:T(8,128)(2,1)S(1)}, bf16[128,1152]{1,0:T(8,128)(2,1)S(1)}, u32[]{:S(2)}, u32[]{:S(2)}) collective-permute-start(bf16[128,1152]{1,0:T(8,128)(2,1)S(1)} %constant_dynamic-update-slice_fusion.refs_0_), channel_id=1, source_target_pairs={{0,48},{16,0},{32,16},{48,32},{1,49},{17,1},{33,17},{49,33},{2,50}... | collective-permute-start | bytes 884744 | tf_op jit(solution)/shard_map/ppermute | solution.py:146
  64.7 16.1 %collective-permute-start.4 = (bf16[128,1152]{1,0:T(8,128)(2,1)S(1)}, bf16[128,1152]{1,0:T(8,128)(2,1)S(1)}, u32[]{:S(2)}, u32[]{:S(2)}) collective-permute-start(bf16[128,1152]{1,0:T(8,128)(2,1)S(1)} %constant_dynamic-update-slice_fusion.refs_0_), channel_id=1, source_target_pairs={{0,32},{16,48},{32,0},{48,16},{1,33},{17,49},{33,1},{49,17},{2,34}... | collective-permute-start | bytes 884744 | tf_op jit(solution)/shard_map/ppermute | solution.py:146
  69.0 14.7 %collective-permute-start.3 = (bf16[128,1152]{1,0:T(8,128)(2,1)S(1)}, bf16[128,1152]{1,0:T(8,128)(2,1)}, u32[]{:S(2)}, u32[]{:S(2)}) collective-permute-start(bf16[128,1152]{1,0:T(8,128)(2,1)S(1)} %constant_dynamic-update-slice_fusion.refs_0_), channel_id=1, source_target_pairs={{0,16},{16,32},{32,48},{48,0},{1,17},{17,33},{33,49},{49,1},{2,18}... | collective-permute-start | bytes 884744 | tf_op jit(solution)/shard_map/ppermute | solution.py:146
  73.7 10.0 %copy-start.5 = (bf16[128,1152]{1,0:T(8,128)(2,1)}, bf16[128,1152]{1,0:T(8,128)(2,1)S(1)}, u32[]{:S(2)}) copy-start(bf16[128,1152]{1,0:T(8,128)(2,1)S(1)} %collective-permute-done.5.refs_3_) | copy-start | bytes 884740
  92.3 28.5 %collective-permute-start.13 = (f32[512,1152]{1,0:T(8,128)}, f32[512,1152]{1,0:T(8,128)}, u32[]{:S(2)}, u32[]{:S(2)}) collective-permute-start(f32[512,1152]{1,0:T(8,128)} %fusion.6), channel_id=1, source_target_pairs={{0,1},{1,0},{2,3},{3,2},{4,5},{5,4},{6,7},{7,6},{8,9},{9,8},{10,11... | collective-permute-start | bytes 7077896 | tf_op jit(solution)/shard_map/ppermute | solution.py:142
  97.6 22.2 %all-to-all-start.2 = ((f32[32,8,128]{2,1,0:T(8,128)}), f32[32,8,128]{2,1,0:T(8,128)}, u32[]{:S(2)}, u32[]{:S(2)}) async-start(f32[32,8,128]{2,1,0:T(8,128)} %get-tuple-element.11), calls=%async_computation.2 | async-start | bytes 262144 | tf_op jit(solution)/shard_map/all_to_all | solution.py:249
  108.4 12.4 %copy-start.1 = (bf16[1024,512]{1,0:T(8,128)(2,1)S(1)}, bf16[1024,512]{1,0:T(8,128)(2,1)}, u32[]{:S(2)}) copy-start(bf16[1024,512]{1,0:T(8,128)(2,1)} %get-tuple-element.10) | copy-start | bytes 3145732
  108.5 19.7 %collective-permute-start.7 = (f16[128,1152]{1,0:T(8,128)(2,1)S(1)}, f16[128,1152]{1,0:T(8,128)(2,1)S(1)}, u32[]{:S(2)}, u32[]{:S(2)}) collective-permute-start(f16[128,1152]{1,0:T(8,128)(2,1)S(1)} %get-tuple-element.13), channel_id=1, source_target_pairs={{0,48},{16,0},{32,16},{48,32},{1,49},{17,1},{33,17},{49,33},{2,50}... | collective-permute-start | bytes 884744 | tf_op jit(solution)/shard_map/ppermute | solution.py:146
  111.2 17.0 %collective-permute-start.9 = (f16[128,1152]{1,0:T(8,128)(2,1)S(1)}, f16[128,1152]{1,0:T(8,128)(2,1)}, u32[]{:S(2)}, u32[]{:S(2)}) collective-permute-start(f16[128,1152]{1,0:T(8,128)(2,1)S(1)} %get-tuple-element.14), channel_id=1, source_target_pairs={{0,16},{16,32},{32,48},{48,0},{1,17},{17,33},{33,49},{49,1},{2,18}... | collective-permute-start | bytes 884744 | tf_op jit(solution)/shard_map/ppermute | solution.py:146
  114.5 13.7 %collective-permute-start.8 = (f16[128,1152]{1,0:T(8,128)(2,1)S(1)}, f16[128,1152]{1,0:T(8,128)(2,1)}, u32[]{:S(2)}, u32[]{:S(2)}) collective-permute-start(f16[128,1152]{1,0:T(8,128)(2,1)S(1)} %get-tuple-element.15), channel_id=1, source_target_pairs={{0,32},{16,48},{32,0},{48,16},{1,33},{17,49},{33,1},{49,17},{2,34}... | collective-permute-start | bytes 884744 | tf_op jit(solution)/shard_map/ppermute | solution.py:146
  124.7 21.1 %all-to-all-start.3 = ((f16[4,128,1280]{2,1,0:T(8,128)(2,1)}), f16[4,128,1280]{2,1,0:T(8,128)(2,1)S(1)}, u32[]{:S(2)}, u32[]{:S(2)}) async-start(f16[4,128,1280]{2,1,0:T(8,128)(2,1)} %bitcast.3), calls=%async_computation.3 | async-start | bytes 2621440 | tf_op jit(solution)/shard_map/all_to_all | solution.py:192
  129.7 20.6 %collective-permute-start.10 = (f16[32,1152]{1,0:T(8,128)(2,1)S(1)}, f16[32,1152]{1,0:T(8,128)(2,1)S(1)}, u32[]{:S(2)}, u32[]{:S(2)}) collective-permute-start(f16[32,1152]{1,0:T(8,128)(2,1)S(1)} %get-tuple-element.16), channel_id=1, source_target_pairs={{0,6},{2,0},{4,2},{6,4},{1,7},{3,1},{5,3},{7,5},{8,14},{10,8},{12,... | collective-permute-start | bytes 221192 | tf_op jit(solution)/shard_map/ppermute | solution.py:146
  132.2 18.2 %collective-permute-start.12 = (f16[32,1152]{1,0:T(8,128)(2,1)S(1)}, f16[32,1152]{1,0:T(8,128)(2,1)S(1)}, u32[]{:S(2)}, u32[]{:S(2)}) collective-permute-start(f16[32,1152]{1,0:T(8,128)(2,1)S(1)} %get-tuple-element.17), channel_id=1, source_target_pairs={{0,2},{2,4},{4,6},{6,0},{1,3},{3,5},{5,7},{7,1},{8,10},{10,12},{12... | collective-permute-start | bytes 221192 | tf_op jit(solution)/shard_map/ppermute | solution.py:146
  135.6 14.8 %copy-start.2 = (bf16[32,1152]{1,0:T(8,128)(2,1)S(1)}, bf16[32,1152]{1,0:T(8,128)(2,1)}, u32[]{:S(2)}) copy-start(bf16[32,1152]{1,0:T(8,128)(2,1)} %images_hbm_ref.1) | copy-start | bytes 221188
  135.6 14.8 %collective-permute-start.11 = (f16[32,1152]{1,0:T(8,128)(2,1)S(1)}, f16[32,1152]{1,0:T(8,128)(2,1)S(1)}, u32[]{:S(2)}, u32[]{:S(2)}) collective-permute-start(f16[32,1152]{1,0:T(8,128)(2,1)S(1)} %get-tuple-element.18), channel_id=1, source_target_pairs={{0,4},{2,6},{4,0},{6,2},{1,5},{3,7},{5,1},{7,3},{8,12},{10,14},{12... | collective-permute-start | bytes 221192 | tf_op jit(solution)/shard_map/ppermute | solution.py:146
  146.8 25.3 %copy-start.3 = (bf16[32,1152]{1,0:T(8,128)(2,1)S(1)}, bf16[32,1152]{1,0:T(8,128)(2,1)}, u32[]{:S(2)}) copy-start(bf16[32,1152]{1,0:T(8,128)(2,1)} %texts_hbm_ref.1) | copy-start | bytes 221188
  146.8 24.6 %all-to-all-start.4 = ((f16[4,32,1280]{2,1,0:T(8,128)(2,1)}), f16[4,32,1280]{2,1,0:T(8,128)(2,1)S(1)}, u32[]{:S(2)}, u32[]{:S(2)}) async-start(f16[4,32,1280]{2,1,0:T(8,128)(2,1)} %bitcast.4), calls=%async_computation.4 | async-start | bytes 655360 | tf_op jit(solution)/shard_map/all_to_all | solution.py:192
  (3 other events, 10.2 us)

commit v5 on v4

--- a/solution.py
+++ b/solution.py
@@ -67,19 +67,7 @@
     )(held(texts), held(images))
 
 
-def pair_kernel(own_text_ref, masked_hbm_ref, *refs):
-    part_refs, (own_ref, other_ref) = refs[:SIDE], refs[SIDE : SIDE + 2]
-    coef_ref, loss_ref, group_ref, masked_ref, arrived = refs[SIDE + 2 :]
-    near = part_refs[0].shape[0]
-    copies = [
-        pltpu.make_async_copy(part_refs[k], group_ref.at[pl.ds(k * near, near)], arrived.at[k])
-        for k in range(SIDE)
-    ]
-    copies.append(pltpu.make_async_copy(masked_hbm_ref, masked_ref, arrived.at[SIDE]))
-    for copy in copies:
-        copy.start()
-    for copy in copies:
-        copy.wait()
+def pair_kernel(own_text_ref, masked_ref, group_ref, own_ref, other_ref, coef_ref, loss_ref):
     group = group_ref[...]
     images, _ = group.shape
     half = own_ref.shape[0]
@@ -117,25 +105,19 @@
     loss_ref[...] = jnp.broadcast_to(total[None], loss_ref.shape)
 
 
-def pair_terms(own_text, masked, parts, own_texts, other_texts, peers):
-    near, width = parts[0].shape
+def pair_terms(own_text, masked, group, own_texts, other_texts, peers):
+    images = group.shape[0]
     half = own_texts.shape[0]
-    images = SIDE * near
     return pl.pallas_call(
         pair_kernel,
         out_shape=(
             pltpu.HBM((2 * half, images), jnp.bfloat16),
             pltpu.HBM((peers, 8, 128), jnp.float32),
-            jax.ShapeDtypeStruct((images, width), jnp.bfloat16),
         ),
-        in_specs=[pl.BlockSpec(memory_space=pltpu.SMEM)] + [HBM] * (SIDE + 1) + [VMEM] * 2,
-        out_specs=(VMEM,) * 3,
-        scratch_shapes=[
-            pltpu.VMEM(masked.shape, jnp.float32),
-            pltpu.SemaphoreType.DMA((SIDE + 1,)),
-        ],
+        in_specs=[pl.BlockSpec(memory_space=pltpu.SMEM)] + [VMEM] * 4,
+        out_specs=(VMEM,) * 2,
         compiler_params=pltpu.CompilerParams(vmem_limit_bytes=20 * 2**20),
-    )(own_text, *(held(a) for a in (masked, *parts)), own_texts, other_texts)
+    )(own_text, masked, group, own_texts, other_texts)
 
 
 def swapped(value):
@@ -146,13 +128,13 @@
     return lax.ppermute(value, axis, [(k, (k + steps) % SIDE) for k in range(SIDE)])
 
 
-def all_turned(block, axis):
-    return [block] + [turned(block, axis, k) for k in range(1, SIDE)]
-
-
-def turned_and_summed(parts, axis):
+def all_turned(block, axis, way):
+    return [block] + [turned(block, axis, way * k) for k in range(1, SIDE)]
+
+
+def turned_and_summed(parts, axis, way):
     sums = parts[0]
-    got = [turned(parts[k].astype(jnp.float16), axis, -k) for k in range(1, SIDE)]
+    got = [turned(parts[k].astype(jnp.float16), axis, -way * k) for k in range(1, SIDE)]
     for part in got:
         sums = sums + part.astype(jnp.float32)
     return lax.optimization_barrier(sums)
@@ -204,7 +186,7 @@
         return (((xs * 2 + zbs) * 4 + zas) * 2 + cs) * 2 + ys // 2
 
     k = jnp.arange(16, dtype=jnp.int32)
-    image_tiles = tile_of((x - k // 4) % 4, zb, (za - k % 4) % 4, c, y)
+    image_tiles = tile_of((x + k // 4) % 4, zb, (za - k % 4) % 4, c, y)
     k = jnp.arange(32, dtype=jnp.int32)
     text_cores = jnp.where(k < 16, c, 1 - c)
     text_tiles = tile_of(x, k % 2, za, text_cores, (k // 4) % 4)
@@ -234,18 +216,17 @@
     texts = texts.astype(jnp.float32)
     image_inverse = inverse_norm(images)
     text_inverse = inverse_norm(texts)
-    near = all_turned(image_bf, "za")
+    near = all_turned(image_bf, "za", 1)
     near = jnp.concatenate(near, axis=0)
-    parts = all_turned(near, "x")
+    parts = all_turned(near, "x", -1)
     sent = jnp.broadcast_to(got.reshape(1, SIDE * rows, width), (SIDE, SIDE * rows, width))
     own_texts = lax.all_to_all(sent, "y", 0, 0, tiled=True).reshape(16 * rows, width)
     other_texts = swapped(own_texts)
     masked = mask_rows(tile_mask, rows)
     own_text = (lax.axis_index("y") * SIDE + lax.axis_index(ZB)).reshape(1, 1)
     peers = lax.axis_size(IMAGE_GROUP)
-    coef, loss, group = pair_terms(
-        own_text, masked, parts, own_texts, other_texts, peers
-    )
+    group = jnp.concatenate(parts, axis=0)
+    coef, loss = pair_terms(own_text, masked, group, own_texts, other_texts, peers)
     loss = lax.all_to_all(loss, IMAGE_GROUP, 0, 0, tiled=True)
     other_sums = jnp.dot(coef[16 * rows :], group, preferred_element_type=jnp.float32)
     other_sums = swapped(other_sums)
@@ -261,10 +242,10 @@
     row = jnp.pad(row, ((0, 0), (width, 0))).astype(jnp.float16)
     payload = jnp.where(lanes >= width, row, jnp.pad(payload, ((0, 0), (0, SPARE))))
     text_parts = sent_and_summed(payload.reshape(SIDE, SIDE * rows, -1), "y")
-    image_parts = turned_and_summed(image_parts.reshape(SIDE, SIDE * rows, width), "x")
+    image_parts = turned_and_summed(image_parts.reshape(SIDE, SIDE * rows, width), "x", -1)
     text_parts = text_parts.astype(jnp.float16).reshape(SIDE, rows, -1)
     text_sums = sent_and_summed(text_parts, ZB)
-    image_sums = turned_and_summed(image_parts.reshape(SIDE, rows, width), "za")
+    image_sums = turned_and_summed(image_parts.reshape(SIDE, rows, width), "za", 1)
     loss = from_row(text_sums[0, width:])
 
     zero = tile_mask == 0

time: 176 us -> 178 us (1.011)
  the two profiles are of different devices: /device:TPU:34 before, /device:TPU:32 now
where the time goes in v5:
time: 178 us; the launch traced here: 177 us
  starting transfers between devices  81.2 us (46%)
  waiting for transfers between devices  57.6 us (32%)
  matrix products  11.3 us (6%)
  other arithmetic  8.96 us (5%)
  local copies, waits for them, and re-layouts  7.72 us (4%)
  Pallas kernels  6.65 us (4%)
  between operations  3.45 us (2%)
    ppermute x12, starting transfers between devices, turned(): lax.ppermute(value, axis, [(k, (k + steps) % SIDE) for k in range(SIDE)])  43.3 us
    all_to_all x2, waiting for transfers between devices, sent_and_summed(): got = lax.all_to_all(parts, axis, 0, 0, tiled=True)  23.6 us
    all_to_all x1, starting transfers between devices, step(): got = lax.all_to_all(slots, ZB, 0, 0, tiled=True)  14.2 us
    all_to_all x1, waiting for transfers between devices, step(): got = lax.all_to_all(slots, ZB, 0, 0, tiled=True)  12.6 us
    ppermute x12, waiting for transfers between devices, turned(): lax.ppermute(value, axis, [(k, (k + steps) % SIDE) for k in range(SIDE)])  11 us
    all_to_all x1, waiting for transfers between devices, step(): lax.all_to_all(sent, 'y', 0, 0, tiled=True).reshape(16 * rows, width)  10.4 us
    all_to_all x1, starting transfers between devices, step(): loss = lax.all_to_all(loss, IMAGE_GROUP, 0, 0, tiled=True)  8.22 us
    all_to_all x2, starting transfers between devices, sent_and_summed(): got = lax.all_to_all(parts, axis, 0, 0, tiled=True)  7.12 us
  transfers between devices with their start and end apart: 19, of which 7 were waited for; matrix products, arithmetic and copies ran while one was open for 13% of the time, Pallas kernels for 1%

profile of v5, /device:TPU:32, one launch (start us, length us, event | category | flops | bytes accessed | tf_op | source)
XLA Modules:
  0.0 177.0 jit_solution(12185274221591609786)
XLA Ops:
  2.4 14.2 %all-to-all-start = ((bf16[4,32,1152]{2,1,0:T(8,128)(2,1)}), bf16[4,32,1152]{2,1,0:T(8,128)(2,1)S(1)}, u32[]{:S(2)}, u32[]{:S(2)}) async-start(bf16[4,32,1152]{2,1,0:T(8,128)(2,1)} %get-tuple-element.8), calls=%async_computation | async-start | bytes 589824 | tf_op jit(solution)/shard_map/all_to_all | solution.py:214
  16.6 2.9 %collective-permute-start.2 = (bf16[32,1152]{1,0:T(8,128)(2,1)}, bf16[32,1152]{1,0:T(8,128)(2,1)}, u32[]{:S(2)}, u32[]{:S(2)}) collective-permute-start(bf16[32,1152]{1,0:T(8,128)(2,1)} %get-tuple-element.7), channel_id=1, source_target_pairs={{0,6},{2,0},{4,2},{6,4},{1,7},{3,1},{5,3},{7,5},{8,14},{10,8},{12,... | collective-permute-start | bytes 221192 | tf_op jit(solution)/shard_map/ppermute | solution.py:128
  19.5 3.4 %collective-permute-start.1 = (bf16[32,1152]{1,0:T(8,128)(2,1)}, bf16[32,1152]{1,0:T(8,128)(2,1)S(1)}, u32[]{:S(2)}, u32[]{:S(2)}) collective-permute-start(bf16[32,1152]{1,0:T(8,128)(2,1)} %get-tuple-element.7), channel_id=1, source_target_pairs={{0,4},{2,6},{4,0},{6,2},{1,5},{3,7},{5,1},{7,3},{8,12},{10,14},{12... | collective-permute-start | bytes 221192 | tf_op jit(solution)/shard_map/ppermute | solution.py:128
  22.9 3.8 %collective-permute-start = (bf16[32,1152]{1,0:T(8,128)(2,1)}, bf16[32,1152]{1,0:T(8,128)(2,1)S(1)}, u32[]{:S(2)}, u32[]{:S(2)}) collective-permute-start(bf16[32,1152]{1,0:T(8,128)(2,1)} %get-tuple-element.7), channel_id=1, source_target_pairs={{0,2},{2,4},{4,6},{6,0},{1,3},{3,5},{5,7},{7,1},{8,10},{10,12},{12... | collective-permute-start | bytes 221192 | tf_op jit(solution)/shard_map/ppermute | solution.py:128
  26.8 12.6 %all-to-all-done = bf16[4,32,1152]{2,1,0:T(8,128)(2,1)S(1)} async-done(((bf16[4,32,1152]{2,1,0:T(8,128)(2,1)}), bf16[4,32,1152]{2,1,0:T(8,128)(2,1)S(1)}, u32[]{:S(2)}, u32[]{:S(2)}) %all-to-all-start) | async-done | bytes 294944 | tf_op jit(solution)/shard_map/all_to_all | solution.py:214
  40.6 4.6 %all-to-all-start.1 = ((bf16[4,128,1152]{2,1,0:T(8,128)(2,1)}), bf16[4,128,1152]{2,1,0:T(8,128)(2,1)S(1)}, u32[]{:S(2)}, u32[]{:S(2)}) async-start(bf16[4,128,1152]{2,1,0:T(8,128)(2,1)} %broadcast_in_dim.81), calls=%async_computation.1 | async-start | bytes 2359296 | tf_op jit(solution)/shard_map/all_to_all | solution.py:223
  48.1 10.4 %all-to-all-done.1 = bf16[4,128,1152]{2,1,0:T(8,128)(2,1)S(1)} async-done(((bf16[4,128,1152]{2,1,0:T(8,128)(2,1)}), bf16[4,128,1152]{2,1,0:T(8,128)(2,1)S(1)}, u32[]{:S(2)}, u32[]{:S(2)}) %all-to-all-start.1) | async-done | bytes 1179680 | tf_op jit(solution)/shard_map/all_to_all | solution.py:223
  62.0 4.7 %collective-permute-start.3 = (bf16[128,1152]{1,0:T(8,128)(2,1)}, bf16[128,1152]{1,0:T(8,128)(2,1)}, u32[]{:S(2)}, u32[]{:S(2)}) collective-permute-start(bf16[128,1152]{1,0:T(8,128)(2,1)} %get-tuple-element.17), channel_id=1, source_target_pairs={{0,48},{16,0},{32,16},{48,32},{1,49},{17,1},{33,17},{49,33},{2,50}... | collective-permute-start | bytes 884744 | tf_op jit(solution)/shard_map/ppermute | solution.py:128
  66.7 2.7 %collective-permute-start.4 = (bf16[128,1152]{1,0:T(8,128)(2,1)}, bf16[128,1152]{1,0:T(8,128)(2,1)}, u32[]{:S(2)}, u32[]{:S(2)}) collective-permute-start(bf16[128,1152]{1,0:T(8,128)(2,1)} %get-tuple-element.17), channel_id=1, source_target_pairs={{0,32},{16,48},{32,0},{48,16},{1,33},{17,49},{33,1},{49,17},{2,34}... | collective-permute-start | bytes 884744 | tf_op jit(solution)/shard_map/ppermute | solution.py:128
  70.3 2.9 %collective-permute-start.5 = (bf16[128,1152]{1,0:T(8,128)(2,1)}, bf16[128,1152]{1,0:T(8,128)(2,1)S(1)}, u32[]{:S(2)}, u32[]{:S(2)}) collective-permute-start(bf16[128,1152]{1,0:T(8,128)(2,1)} %get-tuple-element.17), channel_id=1, source_target_pairs={{0,16},{16,32},{32,48},{48,0},{1,17},{17,33},{33,49},{49,1},{2,18}... | collective-permute-start | bytes 884744 | tf_op jit(solution)/shard_map/ppermute | solution.py:128
  73.2 7.0 %collective-permute-done.3 = bf16[128,1152]{1,0:T(8,128)(2,1)} collective-permute-done((bf16[128,1152]{1,0:T(8,128)(2,1)}, bf16[128,1152]{1,0:T(8,128)(2,1)}, u32[]{:S(2)}, u32[]{:S(2)}) %collective-permute-start.3) | collective-permute-done | bytes 294944 | tf_op jit(solution)/shard_map/ppermute | solution.py:128
  82.2 3.5 %collective-permute-done.5 = bf16[128,1152]{1,0:T(8,128)(2,1)S(1)} collective-permute-done((bf16[128,1152]{1,0:T(8,128)(2,1)}, bf16[128,1152]{1,0:T(8,128)(2,1)S(1)}, u32[]{:S(2)}, u32[]{:S(2)}) %collective-permute-start.5) | collective-permute-done | bytes 294944 | tf_op jit(solution)/shard_map/ppermute | solution.py:128
  85.8 3.9 %shard_map.59 = (bf16[1024,512]{1,0:T(8,128)(2,1)}, f32[32,8,128]{2,1,0:T(8,128)}) custom-call(s32[1,1]{1,0:T(1,128)} %bitcast.own_text_ref, f32[32,512]{1,0:T(8,128)S(1)} %copy-done, bf16[512,1152]{1,0:T(8,128)(2,1)S(1)} %constant_dynamic-update-slice_fusion.4.group_ref, bf16[512,1152]{1,0:T(8,128)(2,1)S(1)} %bitcast.17, ...), custom_call_target="tpu_custom_call" | custom-call | tf_op jit(solution)/shard_map/pallas_call | solution.py:111
  89.7 3.4 %fusion.6 = f32[512,1152]{1,0:T(8,128)} fusion(bf16[512,1152]{1,0:T(8,128)(2,1)S(1)} %constant_dynamic-update-slice_fusion.4.group_ref, bf16[1024,512]{1,0:T(8,128)(2,1)} %get-tuple-element.9), kind=kOutput, calls=%fused_computation.10 | convolution fusion | flops 603979776 | bytes 4063232 | tf_op jit(solution)/shard_map/dot_general | solution.py:231
  98.3 8.2 %all-to-all-start.2 = ((f32[32,8,128]{2,1,0:T(8,128)}), f32[32,8,128]{2,1,0:T(8,128)}, u32[]{:S(2)}, u32[]{:S(2)}) async-start(f32[32,8,128]{2,1,0:T(8,128)} %get-tuple-element.10), calls=%async_computation.2 | async-start | bytes 262144 | tf_op jit(solution)/shard_map/all_to_all | solution.py:230
  111.1 3.5 %collective-permute-start.7 = (f16[128,1152]{1,0:T(8,128)(2,1)S(1)}, f16[128,1152]{1,0:T(8,128)(2,1)S(1)}, u32[]{:S(2)}, u32[]{:S(2)}) collective-permute-start(f16[128,1152]{1,0:T(8,128)(2,1)S(1)} %get-tuple-element.11), channel_id=1, source_target_pairs={{0,16},{16,32},{32,48},{48,0},{1,17},{17,33},{33,49},{49,1},{2,18}... | collective-permute-start | bytes 884744 | tf_op jit(solution)/shard_map/ppermute | solution.py:128
  114.6 3.7 %collective-permute-start.9 = (f16[128,1152]{1,0:T(8,128)(2,1)S(1)}, f16[128,1152]{1,0:T(8,128)(2,1)}, u32[]{:S(2)}, u32[]{:S(2)}) collective-permute-start(f16[128,1152]{1,0:T(8,128)(2,1)S(1)} %get-tuple-element.12), channel_id=1, source_target_pairs={{0,48},{16,0},{32,16},{48,32},{1,49},{17,1},{33,17},{49,33},{2,50}... | collective-permute-start | bytes 884744 | tf_op jit(solution)/shard_map/ppermute | solution.py:128
  118.3 3.7 %collective-permute-start.8 = (f16[128,1152]{1,0:T(8,128)(2,1)S(1)}, f16[128,1152]{1,0:T(8,128)(2,1)}, u32[]{:S(2)}, u32[]{:S(2)}) collective-permute-start(f16[128,1152]{1,0:T(8,128)(2,1)S(1)} %get-tuple-element.13), channel_id=1, source_target_pairs={{0,32},{16,48},{32,0},{48,16},{1,33},{17,49},{33,1},{49,17},{2,34}... | collective-permute-start | bytes 884744 | tf_op jit(solution)/shard_map/ppermute | solution.py:128
  126.9 3.5 %all-to-all-start.3 = ((f16[4,128,1280]{2,1,0:T(8,128)(2,1)}), f16[4,128,1280]{2,1,0:T(8,128)(2,1)S(1)}, u32[]{:S(2)}, u32[]{:S(2)}) async-start(f16[4,128,1280]{2,1,0:T(8,128)(2,1)} %bitcast.3), calls=%async_computation.3 | async-start | bytes 2621440 | tf_op jit(solution)/shard_map/all_to_all | solution.py:174
  134.6 3.5 %collective-permute-start.12 = (f16[32,1152]{1,0:T(8,128)(2,1)S(1)}, f16[32,1152]{1,0:T(8,128)(2,1)S(1)}, u32[]{:S(2)}, u32[]{:S(2)}) collective-permute-start(f16[32,1152]{1,0:T(8,128)(2,1)S(1)} %get-tuple-element.15), channel_id=1, source_target_pairs={{0,2},{2,4},{4,6},{6,0},{1,3},{3,5},{5,7},{7,1},{8,10},{10,12},{12... | collective-permute-start | bytes 221192 | tf_op jit(solution)/shard_map/ppermute | solution.py:128
  138.2 6.2 %collective-permute-start.11 = (f16[32,1152]{1,0:T(8,128)(2,1)S(1)}, f16[32,1152]{1,0:T(8,128)(2,1)S(1)}, u32[]{:S(2)}, u32[]{:S(2)}) collective-permute-start(f16[32,1152]{1,0:T(8,128)(2,1)S(1)} %get-tuple-element.16), channel_id=1, source_target_pairs={{0,4},{2,6},{4,0},{6,2},{1,5},{3,7},{5,1},{7,3},{8,12},{10,14},{12... | collective-permute-start | bytes 221192 | tf_op jit(solution)/shard_map/ppermute | solution.py:128
  144.4 3.6 %all-to-all-done.3 = f16[4,128,1280]{2,1,0:T(8,128)(2,1)S(1)} async-done(((f16[4,128,1280]{2,1,0:T(8,128)(2,1)}), f16[4,128,1280]{2,1,0:T(8,128)(2,1)S(1)}, u32[]{:S(2)}, u32[]{:S(2)}) %all-to-all-start.3) | async-done | bytes 1310752 | tf_op jit(solution)/shard_map/all_to_all | solution.py:174
  148.9 3.6 %all-to-all-start.4 = ((f16[4,32,1280]{2,1,0:T(8,128)(2,1)}), f16[4,32,1280]{2,1,0:T(8,128)(2,1)S(1)}, u32[]{:S(2)}, u32[]{:S(2)}) async-start(f16[4,32,1280]{2,1,0:T(8,128)(2,1)} %bitcast.4), calls=%async_computation.4 | async-start | bytes 655360 | tf_op jit(solution)/shard_map/all_to_all | solution.py:174
  153.5 20.0 %all-to-all-done.4 = f16[4,32,1280]{2,1,0:T(8,128)(2,1)S(1)} async-done(((f16[4,32,1280]{2,1,0:T(8,128)(2,1)}), f16[4,32,1280]{2,1,0:T(8,128)(2,1)S(1)}, u32[]{:S(2)}, u32[]{:S(2)}) %all-to-all-start.4) | async-done | bytes 327712 | tf_op jit(solution)/shard_map/all_to_all | solution.py:174
  (70 shorter events, 34.0 us)
Async XLA Ops:
  2.4 37.0 %all-to-all-start = ((bf16[4,32,1152]{2,1,0:T(8,128)(2,1)}), bf16[4,32,1152]{2,1,0:T(8,128)(2,1)S(1)}, u32[]{:S(2)}, u32[]{:S(2)}) async-start(bf16[4,32,1152]{2,1,0:T(8,128)(2,1)} %get-tuple-element.8), calls=%async_computation | async-start | bytes 589824 | tf_op jit(solution)/shard_map/all_to_all | solution.py:214
  16.6 43.8 %collective-permute-start.2 = (bf16[32,1152]{1,0:T(8,128)(2,1)}, bf16[32,1152]{1,0:T(8,128)(2,1)}, u32[]{:S(2)}, u32[]{:S(2)}) collective-permute-start(bf16[32,1152]{1,0:T(8,128)(2,1)} %get-tuple-element.7), channel_id=1, source_target_pairs={{0,6},{2,0},{4,2},{6,4},{1,7},{3,1},{5,3},{7,5},{8,14},{10,8},{12,... | collective-permute-start | bytes 221192 | tf_op jit(solution)/shard_map/ppermute | solution.py:128
  19.5 28.0 %collective-permute-start.1 = (bf16[32,1152]{1,0:T(8,128)(2,1)}, bf16[32,1152]{1,0:T(8,128)(2,1)S(1)}, u32[]{:S(2)}, u32[]{:S(2)}) collective-permute-start(bf16[32,1152]{1,0:T(8,128)(2,1)} %get-tuple-element.7), channel_id=1, source_target_pairs={{0,4},{2,6},{4,0},{6,2},{1,5},{3,7},{5,1},{7,3},{8,12},{10,14},{12... | collective-permute-start | bytes 221192 | tf_op jit(solution)/shard_map/ppermute | solution.py:128
  22.9 24.0 %collective-permute-start = (bf16[32,1152]{1,0:T(8,128)(2,1)}, bf16[32,1152]{1,0:T(8,128)(2,1)S(1)}, u32[]{:S(2)}, u32[]{:S(2)}) collective-permute-start(bf16[32,1152]{1,0:T(8,128)(2,1)} %get-tuple-element.7), channel_id=1, source_target_pairs={{0,2},{2,4},{4,6},{6,0},{1,3},{3,5},{5,7},{7,1},{8,10},{10,12},{12... | collective-permute-start | bytes 221192 | tf_op jit(solution)/shard_map/ppermute | solution.py:128
  40.6 18.0 %all-to-all-start.1 = ((bf16[4,128,1152]{2,1,0:T(8,128)(2,1)}), bf16[4,128,1152]{2,1,0:T(8,128)(2,1)S(1)}, u32[]{:S(2)}, u32[]{:S(2)}) async-start(bf16[4,128,1152]{2,1,0:T(8,128)(2,1)} %broadcast_in_dim.81), calls=%async_computation.1 | async-start | bytes 2359296 | tf_op jit(solution)/shard_map/all_to_all | solution.py:223
  58.5 27.2 %collective-permute-start.6 = (bf16[512,1152]{1,0:T(8,128)(2,1)S(1)}, bf16[512,1152]{1,0:T(8,128)(2,1)S(1)}, u32[]{:S(2)}, u32[]{:S(2)}) collective-permute-start(bf16[512,1152]{1,0:T(8,128)(2,1)S(1)} %bitcast.16), channel_id=1, source_target_pairs={{0,1},{1,0},{2,3},{3,2},{4,5},{5,4},{6,7},{7,6},{8,9},{9,8},{10,11... | collective-permute-start | bytes 3538952 | tf_op jit(solution)/shard_map/ppermute | solution.py:124
  62.0 18.2 %collective-permute-start.3 = (bf16[128,1152]{1,0:T(8,128)(2,1)}, bf16[128,1152]{1,0:T(8,128)(2,1)}, u32[]{:S(2)}, u32[]{:S(2)}) collective-permute-start(bf16[128,1152]{1,0:T(8,128)(2,1)} %get-tuple-element.17), channel_id=1, source_target_pairs={{0,48},{16,0},{32,16},{48,32},{1,49},{17,1},{33,17},{49,33},{2,50}... | collective-permute-start | bytes 884744 | tf_op jit(solution)/shard_map/ppermute | solution.py:128
  66.7 14.6 %collective-permute-start.4 = (bf16[128,1152]{1,0:T(8,128)(2,1)}, bf16[128,1152]{1,0:T(8,128)(2,1)}, u32[]{:S(2)}, u32[]{:S(2)}) collective-permute-start(bf16[128,1152]{1,0:T(8,128)(2,1)} %get-tuple-element.17), channel_id=1, source_target_pairs={{0,32},{16,48},{32,0},{48,16},{1,33},{17,49},{33,1},{49,17},{2,34}... | collective-permute-start | bytes 884744 | tf_op jit(solution)/shard_map/ppermute | solution.py:128
  70.3 15.5 %copy-start = (f32[32,512]{1,0:T(8,128)S(1)}, f32[32,512]{1,0:T(8,128)}, u32[]{:S(2)}) copy-start(f32[32,512]{1,0:T(8,128)} %fusion.1.masked_ref) | copy-start | bytes 196612
  70.3 15.4 %collective-permute-start.5 = (bf16[128,1152]{1,0:T(8,128)(2,1)}, bf16[128,1152]{1,0:T(8,128)(2,1)S(1)}, u32[]{:S(2)}, u32[]{:S(2)}) collective-permute-start(bf16[128,1152]{1,0:T(8,128)(2,1)} %get-tuple-element.17), channel_id=1, source_target_pairs={{0,16},{16,32},{32,48},{48,0},{1,17},{17,33},{33,49},{49,1},{2,18}... | collective-permute-start | bytes 884744 | tf_op jit(solution)/shard_map/ppermute | solution.py:128
  89.7 5.3 %copy-start.6 = (s32[128,128]{1,0:T(8,128)S(1)}, s32[128,128]{1,0:T(8,128)}, u32[]{:S(2)}) copy-start(s32[128,128]{1,0:T(8,128)} %param.5) | copy-start | bytes 196612
  93.1 29.9 %collective-permute-start.13 = (f32[512,1152]{1,0:T(8,128)}, f32[512,1152]{1,0:T(8,128)}, u32[]{:S(2)}, u32[]{:S(2)}) collective-permute-start(f32[512,1152]{1,0:T(8,128)} %fusion.6), channel_id=1, source_target_pairs={{0,1},{1,0},{2,3},{3,2},{4,5},{5,4},{6,7},{7,6},{8,9},{9,8},{10,11... | collective-permute-start | bytes 7077896 | tf_op jit(solution)/shard_map/ppermute | solution.py:124
  98.3 23.6 %all-to-all-start.2 = ((f32[32,8,128]{2,1,0:T(8,128)}), f32[32,8,128]{2,1,0:T(8,128)}, u32[]{:S(2)}, u32[]{:S(2)}) async-start(f32[32,8,128]{2,1,0:T(8,128)} %get-tuple-element.10), calls=%async_computation.2 | async-start | bytes 262144 | tf_op jit(solution)/shard_map/all_to_all | solution.py:230
  110.9 12.1 %copy-start.2 = (bf16[1024,512]{1,0:T(8,128)(2,1)S(1)}, bf16[1024,512]{1,0:T(8,128)(2,1)}, u32[]{:S(2)}) copy-start(bf16[1024,512]{1,0:T(8,128)(2,1)} %get-tuple-element.9) | copy-start | bytes 3145732
  111.1 19.3 %collective-permute-start.7 = (f16[128,1152]{1,0:T(8,128)(2,1)S(1)}, f16[128,1152]{1,0:T(8,128)(2,1)S(1)}, u32[]{:S(2)}, u32[]{:S(2)}) collective-permute-start(f16[128,1152]{1,0:T(8,128)(2,1)S(1)} %get-tuple-element.11), channel_id=1, source_target_pairs={{0,16},{16,32},{32,48},{48,0},{1,17},{17,33},{33,49},{49,1},{2,18}... | collective-permute-start | bytes 884744 | tf_op jit(solution)/shard_map/ppermute | solution.py:128
  114.6 16.3 %collective-permute-start.9 = (f16[128,1152]{1,0:T(8,128)(2,1)S(1)}, f16[128,1152]{1,0:T(8,128)(2,1)}, u32[]{:S(2)}, u32[]{:S(2)}) collective-permute-start(f16[128,1152]{1,0:T(8,128)(2,1)S(1)} %get-tuple-element.12), channel_id=1, source_target_pairs={{0,48},{16,0},{32,16},{48,32},{1,49},{17,1},{33,17},{49,33},{2,50}... | collective-permute-start | bytes 884744 | tf_op jit(solution)/shard_map/ppermute | solution.py:128
  118.3 12.6 %collective-permute-start.8 = (f16[128,1152]{1,0:T(8,128)(2,1)S(1)}, f16[128,1152]{1,0:T(8,128)(2,1)}, u32[]{:S(2)}, u32[]{:S(2)}) collective-permute-start(f16[128,1152]{1,0:T(8,128)(2,1)S(1)} %get-tuple-element.13), channel_id=1, source_target_pairs={{0,32},{16,48},{32,0},{48,16},{1,33},{17,49},{33,1},{49,17},{2,34}... | collective-permute-start | bytes 884744 | tf_op jit(solution)/shard_map/ppermute | solution.py:128
  126.9 21.1 %all-to-all-start.3 = ((f16[4,128,1280]{2,1,0:T(8,128)(2,1)}), f16[4,128,1280]{2,1,0:T(8,128)(2,1)S(1)}, u32[]{:S(2)}, u32[]{:S(2)}) async-start(f16[4,128,1280]{2,1,0:T(8,128)(2,1)} %bitcast.3), calls=%async_computation.3 | async-start | bytes 2621440 | tf_op jit(solution)/shard_map/all_to_all | solution.py:174
  132.3 20.2 %collective-permute-start.10 = (f16[32,1152]{1,0:T(8,128)(2,1)S(1)}, f16[32,1152]{1,0:T(8,128)(2,1)S(1)}, u32[]{:S(2)}, u32[]{:S(2)}) collective-permute-start(f16[32,1152]{1,0:T(8,128)(2,1)S(1)} %get-tuple-element.14), channel_id=1, source_target_pairs={{0,6},{2,0},{4,2},{6,4},{1,7},{3,1},{5,3},{7,5},{8,14},{10,8},{12,... | collective-permute-start | bytes 221192 | tf_op jit(solution)/shard_map/ppermute | solution.py:128
  134.6 17.9 %collective-permute-start.12 = (f16[32,1152]{1,0:T(8,128)(2,1)S(1)}, f16[32,1152]{1,0:T(8,128)(2,1)S(1)}, u32[]{:S(2)}, u32[]{:S(2)}) collective-permute-start(f16[32,1152]{1,0:T(8,128)(2,1)S(1)} %get-tuple-element.15), channel_id=1, source_target_pairs={{0,2},{2,4},{4,6},{6,0},{1,3},{3,5},{5,7},{7,1},{8,10},{10,12},{12... | collective-permute-start | bytes 221192 | tf_op jit(solution)/shard_map/ppermute | solution.py:128
  138.2 14.4 %copy-start.3 = (bf16[32,1152]{1,0:T(8,128)(2,1)S(1)}, bf16[32,1152]{1,0:T(8,128)(2,1)}, u32[]{:S(2)}) copy-start(bf16[32,1152]{1,0:T(8,128)(2,1)} %images_hbm_ref.1) | copy-start | bytes 221188
  138.2 14.3 %collective-permute-start.11 = (f16[32,1152]{1,0:T(8,128)(2,1)S(1)}, f16[32,1152]{1,0:T(8,128)(2,1)S(1)}, u32[]{:S(2)}, u32[]{:S(2)}) collective-permute-start(f16[32,1152]{1,0:T(8,128)(2,1)S(1)} %get-tuple-element.16), channel_id=1, source_target_pairs={{0,4},{2,6},{4,0},{6,2},{1,5},{3,7},{5,1},{7,3},{8,12},{10,14},{12... | collective-permute-start | bytes 221192 | tf_op jit(solution)/shard_map/ppermute | solution.py:128
  148.9 25.3 %copy-start.4 = (bf16[32,1152]{1,0:T(8,128)(2,1)S(1)}, bf16[32,1152]{1,0:T(8,128)(2,1)}, u32[]{:S(2)}) copy-start(bf16[32,1152]{1,0:T(8,128)(2,1)} %texts_hbm_ref.1) | copy-start | bytes 221188
  148.9 24.6 %all-to-all-start.4 = ((f16[4,32,1280]{2,1,0:T(8,128)(2,1)}), f16[4,32,1280]{2,1,0:T(8,128)(2,1)S(1)}, u32[]{:S(2)}, u32[]{:S(2)}) async-start(f16[4,32,1280]{2,1,0:T(8,128)(2,1)} %bitcast.4), calls=%async_computation.4 | async-start | bytes 655360 | tf_op jit(solution)/shard_map/all_to_all | solution.py:174
  (2 other events, 6.6 us)

commit v6 on v4

--- a/solution.py
+++ b/solution.py
@@ -19,7 +19,7 @@
 BASE = 512.0
 TOP = 2.0**32
 SPARE = 128
-CHUNK = 256
+CHUNK = 512
 
 VMEM = pl.BlockSpec(memory_space=pltpu.VMEM)
 HBM = pl.BlockSpec(memory_space=pltpu.HBM)
@@ -146,13 +146,13 @@
     return lax.ppermute(value, axis, [(k, (k + steps) % SIDE) for k in range(SIDE)])
 
 
-def all_turned(block, axis):
-    return [block] + [turned(block, axis, k) for k in range(1, SIDE)]
-
-
-def turned_and_summed(parts, axis):
+def all_turned(block, axis, way):
+    return [block] + [turned(block, axis, way * k) for k in range(1, SIDE)]
+
+
+def turned_and_summed(parts, axis, way):
     sums = parts[0]
-    got = [turned(parts[k].astype(jnp.float16), axis, -k) for k in range(1, SIDE)]
+    got = [turned(parts[k].astype(jnp.float16), axis, -way * k) for k in range(1, SIDE)]
     for part in got:
         sums = sums + part.astype(jnp.float32)
     return lax.optimization_barrier(sums)
@@ -204,7 +204,7 @@
         return (((xs * 2 + zbs) * 4 + zas) * 2 + cs) * 2 + ys // 2
 
     k = jnp.arange(16, dtype=jnp.int32)
-    image_tiles = tile_of((x - k // 4) % 4, zb, (za - k % 4) % 4, c, y)
+    image_tiles = tile_of((x + k // 4) % 4, zb, (za - k % 4) % 4, c, y)
     k = jnp.arange(32, dtype=jnp.int32)
     text_cores = jnp.where(k < 16, c, 1 - c)
     text_tiles = tile_of(x, k % 2, za, text_cores, (k // 4) % 4)
@@ -234,9 +234,9 @@
     texts = texts.astype(jnp.float32)
     image_inverse = inverse_norm(images)
     text_inverse = inverse_norm(texts)
-    near = all_turned(image_bf, "za")
+    near = all_turned(image_bf, "za", 1)
     near = jnp.concatenate(near, axis=0)
-    parts = all_turned(near, "x")
+    parts = all_turned(near, "x", -1)
     sent = jnp.broadcast_to(got.reshape(1, SIDE * rows, width), (SIDE, SIDE * rows, width))
     own_texts = lax.all_to_all(sent, "y", 0, 0, tiled=True).reshape(16 * rows, width)
     other_texts = swapped(own_texts)
@@ -261,10 +261,10 @@
     row = jnp.pad(row, ((0, 0), (width, 0))).astype(jnp.float16)
     payload = jnp.where(lanes >= width, row, jnp.pad(payload, ((0, 0), (0, SPARE))))
     text_parts = sent_and_summed(payload.reshape(SIDE, SIDE * rows, -1), "y")
-    image_parts = turned_and_summed(image_parts.reshape(SIDE, SIDE * rows, width), "x")
+    image_parts = turned_and_summed(image_parts.reshape(SIDE, SIDE * rows, width), "x", -1)
     text_parts = text_parts.astype(jnp.float16).reshape(SIDE, rows, -1)
     text_sums = sent_and_summed(text_parts, ZB)
-    image_sums = turned_and_summed(image_parts.reshape(SIDE, rows, width), "za")
+    image_sums = turned_and_summed(image_parts.reshape(SIDE, rows, width), "za", 1)
     loss = from_row(text_sums[0, width:])
 
     zero = tile_mask == 0

time: 176 us -> 176 us (level)
  the two profiles are of different devices: /device:TPU:34 before, /device:TPU:32 now
where the time goes in v6:
time: 176 us; the launch traced here: 175 us
  starting transfers between devices  64.6 us (37%)
  waiting for transfers between devices  40.4 us (23%)
  blocking collectives  37.1 us (21%)
  matrix products  11.3 us (6%)
  other arithmetic  8.98 us (5%)
  Pallas kernels  7.37 us (4%)
  between operations  3.49 us (2%)
    ppermute x12, starting transfers between devices, turned(): lax.ppermute(value, axis, [(k, (k + steps) % SIDE) for k in range(SIDE)])  42.5 us
    all_to_all x1, blocking collectives, step(): got = lax.all_to_all(slots, ZB, 0, 0, tiled=True)  37.1 us
    all_to_all x2, waiting for transfers between devices, sent_and_summed(): got = lax.all_to_all(parts, axis, 0, 0, tiled=True)  23.6 us
    ppermute x12, waiting for transfers between devices, turned(): lax.ppermute(value, axis, [(k, (k + steps) % SIDE) for k in range(SIDE)])  9.56 us
    all_to_all x1, waiting for transfers between devices, step(): lax.all_to_all(sent, 'y', 0, 0, tiled=True).reshape(16 * rows, width)  7.16 us
    all_to_all x2, starting transfers between devices, sent_and_summed(): got = lax.all_to_all(parts, axis, 0, 0, tiled=True)  7.12 us
    all_to_all x1, starting transfers between devices, step(): loss = lax.all_to_all(loss, IMAGE_GROUP, 0, 0, tiled=True)  6.53 us
    pallas_call x1, Pallas kernels, pair_terms(): pl.pallas_call(pair_kernel, out_shape=(pltpu.HBM((2 * half, images), jnp....  5.28 us
  transfers between devices with their start and end apart: 18, of which 7 were waited for; matrix products, arithmetic and copies ran while one was open for 9% of the time, Pallas kernels for 1%

profile of v6, /device:TPU:32, one launch (start us, length us, event | category | flops | bytes accessed | tf_op | source)
XLA Modules:
  0.0 174.6 jit_solution(6647925889489361110)
XLA Ops:
  1.8 37.1 %all_to_all.25 = bf16[4,32,1152]{2,1,0:T(8,128)(2,1)S(1)} all-to-all(bf16[4,32,1152]{2,1,0:T(8,128)(2,1)S(1)} %get-tuple-element.9), channel_id=1, replica_groups=mesh['y'=4,'zh'=2,'x'=4,'zb'=2,'za'=4,'c'=2] {'zh','zb'}, dimensions={0} | all-to-all | bytes 589824 | tf_op jit(solution)/shard_map/all_to_all | solution.py:232
  40.0 4.6 %all-to-all-start.1 = ((bf16[4,128,1152]{2,1,0:T(8,128)(2,1)}), bf16[4,128,1152]{2,1,0:T(8,128)(2,1)S(1)}, u32[]{:S(2)}, u32[]{:S(2)}) async-start(bf16[4,128,1152]{2,1,0:T(8,128)(2,1)} %broadcast_in_dim.81), calls=%async_computation.1 | async-start | bytes 2359296 | tf_op jit(solution)/shard_map/all_to_all | solution.py:241
  46.5 4.4 %collective-permute-start.1 = (bf16[32,1152]{1,0:T(8,128)(2,1)S(1)}, bf16[32,1152]{1,0:T(8,128)(2,1)S(1)}, u32[]{:S(2)}, u32[]{:S(2)}) collective-permute-start(bf16[32,1152]{1,0:T(8,128)(2,1)S(1)} %get-tuple-element.8), channel_id=1, source_target_pairs={{0,4},{2,6},{4,0},{6,2},{1,5},{3,7},{5,1},{7,3},{8,12},{10,14},{12... | collective-permute-start | bytes 221192 | tf_op jit(solution)/shard_map/ppermute | solution.py:146
  52.9 7.2 %all-to-all-done.1 = bf16[4,128,1152]{2,1,0:T(8,128)(2,1)S(1)} async-done(((bf16[4,128,1152]{2,1,0:T(8,128)(2,1)}), bf16[4,128,1152]{2,1,0:T(8,128)(2,1)S(1)}, u32[]{:S(2)}, u32[]{:S(2)}) %all-to-all-start.1) | async-done | bytes 1179680 | tf_op jit(solution)/shard_map/all_to_all | solution.py:241
  62.2 3.4 %collective-permute-start.5 = (bf16[128,1152]{1,0:T(8,128)(2,1)S(1)}, bf16[128,1152]{1,0:T(8,128)(2,1)S(1)}, u32[]{:S(2)}, u32[]{:S(2)}) collective-permute-start(bf16[128,1152]{1,0:T(8,128)(2,1)S(1)} %constant_dynamic-update-slice_fusion.refs_0_), channel_id=1, source_target_pairs={{0,16},{16,32},{32,48},{48,0},{1,17},{17,33},{33,49},{49,1},{2,18}... | collective-permute-start | bytes 884744 | tf_op jit(solution)/shard_map/ppermute | solution.py:146
  65.6 4.6 %collective-permute-start.4 = (bf16[128,1152]{1,0:T(8,128)(2,1)S(1)}, bf16[128,1152]{1,0:T(8,128)(2,1)S(1)}, u32[]{:S(2)}, u32[]{:S(2)}) collective-permute-start(bf16[128,1152]{1,0:T(8,128)(2,1)S(1)} %constant_dynamic-update-slice_fusion.refs_0_), channel_id=1, source_target_pairs={{0,32},{16,48},{32,0},{48,16},{1,33},{17,49},{33,1},{49,17},{2,34}... | collective-permute-start | bytes 884744 | tf_op jit(solution)/shard_map/ppermute | solution.py:146
  70.3 3.3 %collective-permute-start.3 = (bf16[128,1152]{1,0:T(8,128)(2,1)S(1)}, bf16[128,1152]{1,0:T(8,128)(2,1)}, u32[]{:S(2)}, u32[]{:S(2)}) collective-permute-start(bf16[128,1152]{1,0:T(8,128)(2,1)S(1)} %constant_dynamic-update-slice_fusion.refs_0_), channel_id=1, source_target_pairs={{0,48},{16,0},{32,16},{48,32},{1,49},{17,1},{33,17},{49,33},{2,50}... | collective-permute-start | bytes 884744 | tf_op jit(solution)/shard_map/ppermute | solution.py:146
  74.8 7.3 %collective-permute-done.4.refs_2_ = bf16[128,1152]{1,0:T(8,128)(2,1)S(1)} collective-permute-done((bf16[128,1152]{1,0:T(8,128)(2,1)S(1)}, bf16[128,1152]{1,0:T(8,128)(2,1)S(1)}, u32[]{:S(2)}, u32[]{:S(2)}) %collective-permute-start.4) | collective-permute-done | bytes 294944 | tf_op jit(solution)/shard_map/ppermute | solution.py:146
  83.7 5.3 %shard_map.59 = (bf16[1024,512]{1,0:T(8,128)(2,1)}, f32[32,8,128]{2,1,0:T(8,128)}, bf16[512,1152]{1,0:T(8,128)(2,1)S(1)}) custom-call(s32[1,1]{1,0:T(1,128)} %bitcast.own_text_ref, f32[32,512]{1,0:T(8,128)} %fusion.1.masked_hbm_ref, bf16[128,1152]{1,0:T(8,128)(2,1)} %copy-done.4, bf16[128,1152]{1,0:T(8,128)(2,1)} %collective-permute-done.3.refs_1_, ...), custom_call_target="tpu_custom_call" | custom-call | tf_op jit(solution)/shard_map/pallas_call | solution.py:124
  89.0 3.4 %fusion.6 = f32[512,1152]{1,0:T(8,128)} fusion(bf16[512,1152]{1,0:T(8,128)(2,1)S(1)} %get-tuple-element.12, bf16[1024,512]{1,0:T(8,128)(2,1)} %get-tuple-element.10), kind=kOutput, calls=%fused_computation.10 | convolution fusion | flops 603979776 | bytes 4063232 | tf_op jit(solution)/shard_map/dot_general | solution.py:250
  97.7 6.5 %all-to-all-start.2 = ((f32[32,8,128]{2,1,0:T(8,128)}), f32[32,8,128]{2,1,0:T(8,128)}, u32[]{:S(2)}, u32[]{:S(2)}) async-start(f32[32,8,128]{2,1,0:T(8,128)} %get-tuple-element.11), calls=%async_computation.2 | async-start | bytes 262144 | tf_op jit(solution)/shard_map/all_to_all | solution.py:249
  104.2 2.0 %fusion.8 = f32[512,1152]{1,0:T(8,128)S(1)} fusion(bf16[512,1152]{1,0:T(8,128)(2,1)S(1)} %collective-permute-done.6.refs_5_, bf16[1024,512]{1,0:T(8,128)(2,1)} %get-tuple-element.10), kind=kOutput, calls=%fused_computation.12 | convolution fusion | flops 603979776 | bytes 4063232 | tf_op jit(solution)/shard_map/dot_general | solution.py:254
  106.2 2.3 %fusion.65 = (f16[512,1152]{1,0:T(8,128)(2,1)S(1)}, f32[512,1152]{1,0:T(8,128)}) fusion(f32[512,1152]{1,0:T(8,128)S(1)} %fusion.8, bf16[512,1152]{1,0:T(8,128)(2,1)S(1)} %bitcast.18, bf16[1024,512]{1,0:T(8,128)(2,1)S(1)} %copy-done), kind=kOutput, calls=%fused_computation.124 | convolution fusion | flops 605159424 | bytes 7602176 | tf_op jit(solution)/shard_map/dot_general | solution.py:252
  108.7 3.5 %collective-permute-start.7 = (f16[128,1152]{1,0:T(8,128)(2,1)S(1)}, f16[128,1152]{1,0:T(8,128)(2,1)S(1)}, u32[]{:S(2)}, u32[]{:S(2)}) collective-permute-start(f16[128,1152]{1,0:T(8,128)(2,1)S(1)} %get-tuple-element.13), channel_id=1, source_target_pairs={{0,16},{16,32},{32,48},{48,0},{1,17},{17,33},{33,49},{49,1},{2,18}... | collective-permute-start | bytes 884744 | tf_op jit(solution)/shard_map/ppermute | solution.py:146
  112.2 3.7 %collective-permute-start.9 = (f16[128,1152]{1,0:T(8,128)(2,1)S(1)}, f16[128,1152]{1,0:T(8,128)(2,1)}, u32[]{:S(2)}, u32[]{:S(2)}) collective-permute-start(f16[128,1152]{1,0:T(8,128)(2,1)S(1)} %get-tuple-element.14), channel_id=1, source_target_pairs={{0,48},{16,0},{32,16},{48,32},{1,49},{17,1},{33,17},{49,33},{2,50}... | collective-permute-start | bytes 884744 | tf_op jit(solution)/shard_map/ppermute | solution.py:146
  115.9 3.7 %collective-permute-start.8 = (f16[128,1152]{1,0:T(8,128)(2,1)S(1)}, f16[128,1152]{1,0:T(8,128)(2,1)}, u32[]{:S(2)}, u32[]{:S(2)}) collective-permute-start(f16[128,1152]{1,0:T(8,128)(2,1)S(1)} %get-tuple-element.15), channel_id=1, source_target_pairs={{0,32},{16,48},{32,0},{48,16},{1,33},{17,49},{33,1},{49,17},{2,34}... | collective-permute-start | bytes 884744 | tf_op jit(solution)/shard_map/ppermute | solution.py:146
  120.6 2.5 %fusion = f16[512,1152]{1,0:T(8,128)(2,1)S(1)} fusion(f32[512,1152]{1,0:T(8,128)} %collective-permute-done.13, bf16[512,1152]{1,0:T(8,128)(2,1)S(1)} %get-tuple-element.12, bf16[1024,512]{1,0:T(8,128)(2,1)S(1)} %copy-done.1), kind=kOutput, calls=%fused_computation.2 | convolution fusion | flops 605159424 | bytes 5242880 | tf_op jit(solution)/shard_map/dot_general | solution.py:257
  124.5 3.5 %all-to-all-start.3 = ((f16[4,128,1280]{2,1,0:T(8,128)(2,1)}), f16[4,128,1280]{2,1,0:T(8,128)(2,1)S(1)}, u32[]{:S(2)}, u32[]{:S(2)}) async-start(f16[4,128,1280]{2,1,0:T(8,128)(2,1)} %bitcast.3), calls=%async_computation.3 | async-start | bytes 2621440 | tf_op jit(solution)/shard_map/all_to_all | solution.py:192
  130.0 2.3 %collective-permute-start.10 = (f16[32,1152]{1,0:T(8,128)(2,1)S(1)}, f16[32,1152]{1,0:T(8,128)(2,1)S(1)}, u32[]{:S(2)}, u32[]{:S(2)}) collective-permute-start(f16[32,1152]{1,0:T(8,128)(2,1)S(1)} %get-tuple-element.16), channel_id=1, source_target_pairs={{0,6},{2,0},{4,2},{6,4},{1,7},{3,1},{5,3},{7,5},{8,14},{10,8},{12,... | collective-permute-start | bytes 221192 | tf_op jit(solution)/shard_map/ppermute | solution.py:146
  132.3 3.5 %collective-permute-start.12 = (f16[32,1152]{1,0:T(8,128)(2,1)S(1)}, f16[32,1152]{1,0:T(8,128)(2,1)S(1)}, u32[]{:S(2)}, u32[]{:S(2)}) collective-permute-start(f16[32,1152]{1,0:T(8,128)(2,1)S(1)} %get-tuple-element.17), channel_id=1, source_target_pairs={{0,2},{2,4},{4,6},{6,0},{1,3},{3,5},{5,7},{7,1},{8,10},{10,12},{12... | collective-permute-start | bytes 221192 | tf_op jit(solution)/shard_map/ppermute | solution.py:146
  135.8 6.2 %collective-permute-start.11 = (f16[32,1152]{1,0:T(8,128)(2,1)S(1)}, f16[32,1152]{1,0:T(8,128)(2,1)S(1)}, u32[]{:S(2)}, u32[]{:S(2)}) collective-permute-start(f16[32,1152]{1,0:T(8,128)(2,1)S(1)} %get-tuple-element.18), channel_id=1, source_target_pairs={{0,4},{2,6},{4,0},{6,2},{1,5},{3,7},{5,1},{7,3},{8,12},{10,14},{12... | collective-permute-start | bytes 221192 | tf_op jit(solution)/shard_map/ppermute | solution.py:146
  142.1 3.6 %all-to-all-done.3 = f16[4,128,1280]{2,1,0:T(8,128)(2,1)S(1)} async-done(((f16[4,128,1280]{2,1,0:T(8,128)(2,1)}), f16[4,128,1280]{2,1,0:T(8,128)(2,1)S(1)}, u32[]{:S(2)}, u32[]{:S(2)}) %all-to-all-start.3) | async-done | bytes 1310752 | tf_op jit(solution)/shard_map/all_to_all | solution.py:192
  146.6 3.6 %all-to-all-start.4 = ((f16[4,32,1280]{2,1,0:T(8,128)(2,1)}), f16[4,32,1280]{2,1,0:T(8,128)(2,1)S(1)}, u32[]{:S(2)}, u32[]{:S(2)}) async-start(f16[4,32,1280]{2,1,0:T(8,128)(2,1)} %bitcast.4), calls=%async_computation.4 | async-start | bytes 655360 | tf_op jit(solution)/shard_map/all_to_all | solution.py:192
  151.2 20.0 %all-to-all-done.4 = f16[4,32,1280]{2,1,0:T(8,128)(2,1)S(1)} async-done(((f16[4,32,1280]{2,1,0:T(8,128)(2,1)}), f16[4,32,1280]{2,1,0:T(8,128)(2,1)S(1)}, u32[]{:S(2)}, u32[]{:S(2)}) %all-to-all-start.4) | async-done | bytes 327712 | tf_op jit(solution)/shard_map/all_to_all | solution.py:192
  (70 shorter events, 23.5 us)
Async XLA Ops:
  40.0 22.0 %copy-start.7 = (s32[128,128]{1,0:T(8,128)S(1)}, s32[128,128]{1,0:T(8,128)}, u32[]{:S(2)}) copy-start(s32[128,128]{1,0:T(8,128)} %param.5) | copy-start | bytes 196612
  40.0 20.0 %all-to-all-start.1 = ((bf16[4,128,1152]{2,1,0:T(8,128)(2,1)}), bf16[4,128,1152]{2,1,0:T(8,128)(2,1)S(1)}, u32[]{:S(2)}, u32[]{:S(2)}) async-start(bf16[4,128,1152]{2,1,0:T(8,128)(2,1)} %broadcast_in_dim.81), calls=%async_computation.1 | async-start | bytes 2359296 | tf_op jit(solution)/shard_map/all_to_all | solution.py:241
  44.6 17.6 %collective-permute-start.2 = (bf16[32,1152]{1,0:T(8,128)(2,1)S(1)}, bf16[32,1152]{1,0:T(8,128)(2,1)S(1)}, u32[]{:S(2)}, u32[]{:S(2)}) collective-permute-start(bf16[32,1152]{1,0:T(8,128)(2,1)S(1)} %get-tuple-element.8), channel_id=1, source_target_pairs={{0,6},{2,0},{4,2},{6,4},{1,7},{3,1},{5,3},{7,5},{8,14},{10,8},{12,... | collective-permute-start | bytes 221192 | tf_op jit(solution)/shard_map/ppermute | solution.py:146
  46.5 15.7 %collective-permute-start.1 = (bf16[32,1152]{1,0:T(8,128)(2,1)S(1)}, bf16[32,1152]{1,0:T(8,128)(2,1)S(1)}, u32[]{:S(2)}, u32[]{:S(2)}) collective-permute-start(bf16[32,1152]{1,0:T(8,128)(2,1)S(1)} %get-tuple-element.8), channel_id=1, source_target_pairs={{0,4},{2,6},{4,0},{6,2},{1,5},{3,7},{5,1},{7,3},{8,12},{10,14},{12... | collective-permute-start | bytes 221192 | tf_op jit(solution)/shard_map/ppermute | solution.py:146
  50.9 11.3 %collective-permute-start = (bf16[32,1152]{1,0:T(8,128)(2,1)S(1)}, bf16[32,1152]{1,0:T(8,128)(2,1)S(1)}, u32[]{:S(2)}, u32[]{:S(2)}) collective-permute-start(bf16[32,1152]{1,0:T(8,128)(2,1)S(1)} %get-tuple-element.8), channel_id=1, source_target_pairs={{0,2},{2,4},{4,6},{6,0},{1,3},{3,5},{5,7},{7,1},{8,10},{10,12},{12... | collective-permute-start | bytes 221192 | tf_op jit(solution)/shard_map/ppermute | solution.py:146
  60.0 23.7 %collective-permute-start.6 = (bf16[512,1152]{1,0:T(8,128)(2,1)S(1)}, bf16[512,1152]{1,0:T(8,128)(2,1)S(1)}, u32[]{:S(2)}, u32[]{:S(2)}) collective-permute-start(bf16[512,1152]{1,0:T(8,128)(2,1)S(1)} %bitcast.16), channel_id=1, source_target_pairs={{0,1},{1,0},{2,3},{3,2},{4,5},{5,4},{6,7},{7,6},{8,9},{9,8},{10,11... | collective-permute-start | bytes 3538952 | tf_op jit(solution)/shard_map/ppermute | solution.py:142
  62.2 21.5 %copy-start.4 = (bf16[128,1152]{1,0:T(8,128)(2,1)}, bf16[128,1152]{1,0:T(8,128)(2,1)S(1)}, u32[]{:S(2)}) copy-start(bf16[128,1152]{1,0:T(8,128)(2,1)S(1)} %constant_dynamic-update-slice_fusion.refs_0_) | copy-start | bytes 884740
  62.2 12.5 %collective-permute-start.5 = (bf16[128,1152]{1,0:T(8,128)(2,1)S(1)}, bf16[128,1152]{1,0:T(8,128)(2,1)S(1)}, u32[]{:S(2)}, u32[]{:S(2)}) collective-permute-start(bf16[128,1152]{1,0:T(8,128)(2,1)S(1)} %constant_dynamic-update-slice_fusion.refs_0_), channel_id=1, source_target_pairs={{0,16},{16,32},{32,48},{48,0},{1,17},{17,33},{33,49},{49,1},{2,18}... | collective-permute-start | bytes 884744 | tf_op jit(solution)/shard_map/ppermute | solution.py:146
  65.6 16.4 %collective-permute-start.4 = (bf16[128,1152]{1,0:T(8,128)(2,1)S(1)}, bf16[128,1152]{1,0:T(8,128)(2,1)S(1)}, u32[]{:S(2)}, u32[]{:S(2)}) collective-permute-start(bf16[128,1152]{1,0:T(8,128)(2,1)S(1)} %constant_dynamic-update-slice_fusion.refs_0_), channel_id=1, source_target_pairs={{0,32},{16,48},{32,0},{48,16},{1,33},{17,49},{33,1},{49,17},{2,34}... | collective-permute-start | bytes 884744 | tf_op jit(solution)/shard_map/ppermute | solution.py:146
  70.3 13.4 %collective-permute-start.3 = (bf16[128,1152]{1,0:T(8,128)(2,1)S(1)}, bf16[128,1152]{1,0:T(8,128)(2,1)}, u32[]{:S(2)}, u32[]{:S(2)}) collective-permute-start(bf16[128,1152]{1,0:T(8,128)(2,1)S(1)} %constant_dynamic-update-slice_fusion.refs_0_), channel_id=1, source_target_pairs={{0,48},{16,0},{32,16},{48,32},{1,49},{17,1},{33,17},{49,33},{2,50}... | collective-permute-start | bytes 884744 | tf_op jit(solution)/shard_map/ppermute | solution.py:146
  74.8 9.0 %copy-start.5 = (bf16[128,1152]{1,0:T(8,128)(2,1)}, bf16[128,1152]{1,0:T(8,128)(2,1)S(1)}, u32[]{:S(2)}) copy-start(bf16[128,1152]{1,0:T(8,128)(2,1)S(1)} %collective-permute-done.5.refs_3_) | copy-start | bytes 884740
  92.4 28.2 %collective-permute-start.13 = (f32[512,1152]{1,0:T(8,128)}, f32[512,1152]{1,0:T(8,128)}, u32[]{:S(2)}, u32[]{:S(2)}) collective-permute-start(f32[512,1152]{1,0:T(8,128)} %fusion.6), channel_id=1, source_target_pairs={{0,1},{1,0},{2,3},{3,2},{4,5},{5,4},{6,7},{7,6},{8,9},{9,8},{10,11... | collective-permute-start | bytes 7077896 | tf_op jit(solution)/shard_map/ppermute | solution.py:142
  97.7 21.9 %all-to-all-start.2 = ((f32[32,8,128]{2,1,0:T(8,128)}), f32[32,8,128]{2,1,0:T(8,128)}, u32[]{:S(2)}, u32[]{:S(2)}) async-start(f32[32,8,128]{2,1,0:T(8,128)} %get-tuple-element.11), calls=%async_computation.2 | async-start | bytes 262144 | tf_op jit(solution)/shard_map/all_to_all | solution.py:249
  108.6 12.1 %copy-start.1 = (bf16[1024,512]{1,0:T(8,128)(2,1)S(1)}, bf16[1024,512]{1,0:T(8,128)(2,1)}, u32[]{:S(2)}) copy-start(bf16[1024,512]{1,0:T(8,128)(2,1)} %get-tuple-element.10) | copy-start | bytes 3145732
  108.7 19.4 %collective-permute-start.7 = (f16[128,1152]{1,0:T(8,128)(2,1)S(1)}, f16[128,1152]{1,0:T(8,128)(2,1)S(1)}, u32[]{:S(2)}, u32[]{:S(2)}) collective-permute-start(f16[128,1152]{1,0:T(8,128)(2,1)S(1)} %get-tuple-element.13), channel_id=1, source_target_pairs={{0,16},{16,32},{32,48},{48,0},{1,17},{17,33},{33,49},{49,1},{2,18}... | collective-permute-start | bytes 884744 | tf_op jit(solution)/shard_map/ppermute | solution.py:146
  112.2 16.3 %collective-permute-start.9 = (f16[128,1152]{1,0:T(8,128)(2,1)S(1)}, f16[128,1152]{1,0:T(8,128)(2,1)}, u32[]{:S(2)}, u32[]{:S(2)}) collective-permute-start(f16[128,1152]{1,0:T(8,128)(2,1)S(1)} %get-tuple-element.14), channel_id=1, source_target_pairs={{0,48},{16,0},{32,16},{48,32},{1,49},{17,1},{33,17},{49,33},{2,50}... | collective-permute-start | bytes 884744 | tf_op jit(solution)/shard_map/ppermute | solution.py:146
  115.9 12.6 %collective-permute-start.8 = (f16[128,1152]{1,0:T(8,128)(2,1)S(1)}, f16[128,1152]{1,0:T(8,128)(2,1)}, u32[]{:S(2)}, u32[]{:S(2)}) collective-permute-start(f16[128,1152]{1,0:T(8,128)(2,1)S(1)} %get-tuple-element.15), channel_id=1, source_target_pairs={{0,32},{16,48},{32,0},{48,16},{1,33},{17,49},{33,1},{49,17},{2,34}... | collective-permute-start | bytes 884744 | tf_op jit(solution)/shard_map/ppermute | solution.py:146
  124.5 21.1 %all-to-all-start.3 = ((f16[4,128,1280]{2,1,0:T(8,128)(2,1)}), f16[4,128,1280]{2,1,0:T(8,128)(2,1)S(1)}, u32[]{:S(2)}, u32[]{:S(2)}) async-start(f16[4,128,1280]{2,1,0:T(8,128)(2,1)} %bitcast.3), calls=%async_computation.3 | async-start | bytes 2621440 | tf_op jit(solution)/shard_map/all_to_all | solution.py:192
  130.0 20.2 %collective-permute-start.10 = (f16[32,1152]{1,0:T(8,128)(2,1)S(1)}, f16[32,1152]{1,0:T(8,128)(2,1)S(1)}, u32[]{:S(2)}, u32[]{:S(2)}) collective-permute-start(f16[32,1152]{1,0:T(8,128)(2,1)S(1)} %get-tuple-element.16), channel_id=1, source_target_pairs={{0,6},{2,0},{4,2},{6,4},{1,7},{3,1},{5,3},{7,5},{8,14},{10,8},{12,... | collective-permute-start | bytes 221192 | tf_op jit(solution)/shard_map/ppermute | solution.py:146
  132.3 17.9 %collective-permute-start.12 = (f16[32,1152]{1,0:T(8,128)(2,1)S(1)}, f16[32,1152]{1,0:T(8,128)(2,1)S(1)}, u32[]{:S(2)}, u32[]{:S(2)}) collective-permute-start(f16[32,1152]{1,0:T(8,128)(2,1)S(1)} %get-tuple-element.17), channel_id=1, source_target_pairs={{0,2},{2,4},{4,6},{6,0},{1,3},{3,5},{5,7},{7,1},{8,10},{10,12},{12... | collective-permute-start | bytes 221192 | tf_op jit(solution)/shard_map/ppermute | solution.py:146
  135.8 14.4 %copy-start.2 = (bf16[32,1152]{1,0:T(8,128)(2,1)S(1)}, bf16[32,1152]{1,0:T(8,128)(2,1)}, u32[]{:S(2)}) copy-start(bf16[32,1152]{1,0:T(8,128)(2,1)} %images_hbm_ref.1) | copy-start | bytes 221188
  135.8 14.3 %collective-permute-start.11 = (f16[32,1152]{1,0:T(8,128)(2,1)S(1)}, f16[32,1152]{1,0:T(8,128)(2,1)S(1)}, u32[]{:S(2)}, u32[]{:S(2)}) collective-permute-start(f16[32,1152]{1,0:T(8,128)(2,1)S(1)} %get-tuple-element.18), channel_id=1, source_target_pairs={{0,4},{2,6},{4,0},{6,2},{1,5},{3,7},{5,1},{7,3},{8,12},{10,14},{12... | collective-permute-start | bytes 221192 | tf_op jit(solution)/shard_map/ppermute | solution.py:146
  146.6 25.3 %copy-start.3 = (bf16[32,1152]{1,0:T(8,128)(2,1)S(1)}, bf16[32,1152]{1,0:T(8,128)(2,1)}, u32[]{:S(2)}) copy-start(bf16[32,1152]{1,0:T(8,128)(2,1)} %texts_hbm_ref.1) | copy-start | bytes 221188
  146.6 24.6 %all-to-all-start.4 = ((f16[4,32,1280]{2,1,0:T(8,128)(2,1)}), f16[4,32,1280]{2,1,0:T(8,128)(2,1)S(1)}, u32[]{:S(2)}, u32[]{:S(2)}) async-start(f16[4,32,1280]{2,1,0:T(8,128)(2,1)} %bitcast.4), calls=%async_computation.4 | async-start | bytes 655360 | tf_op jit(solution)/shard_map/all_to_all | solution.py:192
  (3 other events, 9.0 us)
